TPU v7x, 32 devices: a whole 2x2x4 slice. The times are simulated.
32 devices in a mesh: dp: 16 (over z, y, x), tensor: 2 (over core).
Axes of the slice: x: 2, y: 2, z: 4, core: 2. Of those that a mesh axis runs over, the one named last changes fastest.
Arguments:
- incoming_embeddings: bfloat16 [16, 1024, 1024], P('dp', 'tensor'), may hold values from -6 to 6
- text_boundary_indicators: int32 [16, 1024], P('dp', 'tensor'), may hold values from 0 to 1, as said below
- upstream_sensitivity: bfloat16 [16, 1024, 1024], P('dp', 'tensor'), may hold values from -6 to 6
- primary_standardize_scaling: bfloat16 [1024], P(('dp', 'tensor')), may hold values from 0.5 to 1.5
- primary_standardize_offset: bfloat16 [1024], P(('dp', 'tensor')), may hold values from -1 to 1
- secondary_standardize_scaling: bfloat16 [1024], P(('dp', 'tensor')), may hold values from 0.5 to 1.5
- secondary_standardize_offset: bfloat16 [1024], P(('dp', 'tensor')), may hold values from -1 to 1
- feature_fading_logarithms: bfloat16 [1024], P(('dp', 'tensor')), may hold values from -8.6 to -3.2
- present_symbol_reward: bfloat16 [1024], P(('dp', 'tensor')), may hold values from -1 to 1
- timemix_lookup_blend: bfloat16 [1024], P(('dp', 'tensor')), may hold values from 0 to 1
- timemix_payload_blend: bfloat16 [1024], P(('dp', 'tensor')), may hold values from 0 to 1
- timemix_gate_blend: bfloat16 [1024], P(('dp', 'tensor')), may hold values from 0 to 1
- timemix_lookup_proj: bfloat16 [1024, 1024], P(('dp', 'tensor')), may hold values from -0.1875 to 0.1875
- timemix_payload_proj: bfloat16 [1024, 1024], P(('dp', 'tensor')), may hold values from -0.1875 to 0.1875
- timemix_gate_proj: bfloat16 [1024, 1024], P(('dp', 'tensor')), may hold values from -0.1875 to 0.1875
- timemix_emit_proj: bfloat16 [1024, 1024], P(('dp', 'tensor')), may hold values from -1.5 to 1.5
- feedmix_lookup_blend: bfloat16 [1024], P(('dp', 'tensor')), may hold values from 0 to 1
- feedmix_gate_blend: bfloat16 [1024], P(('dp', 'tensor')), may hold values from 0 to 1
- feedmix_gate_proj: bfloat16 [1024, 1024], P(('dp', 'tensor')), may hold values from -0.1875 to 0.1875
- feedmix_lookup_proj: bfloat16 [1024, 4096], P('dp', 'tensor'), may hold values from -0.1875 to 0.1875
- feedmix_payload_proj: bfloat16 [4096, 1024], P('tensor', 'dp'), may hold values from -0.09375 to 0.09375
Outputs:
- layer_out: bfloat16 [16, 1024, 1024], P('dp', 'tensor')
- grad_tokens: float32 [16, 1024, 1024], P('dp', 'tensor')
- grad_ln1_gain: float32 [1024], P(('dp', 'tensor'))
- grad_ln1_bias: float32 [1024], P(('dp', 'tensor'))
- grad_ln2_gain: float32 [1024], P(('dp', 'tensor'))
- grad_ln2_bias: float32 [1024], P(('dp', 'tensor'))
- grad_time_decay: float32 [1024], P(('dp', 'tensor'))
- grad_time_bonus: float32 [1024], P(('dp', 'tensor'))
- grad_att_mix_k: float32 [1024], P(('dp', 'tensor'))
- grad_att_mix_v: float32 [1024], P(('dp', 'tensor'))
- grad_att_mix_r: float32 [1024], P(('dp', 'tensor'))
- grad_att_key: float32 [1024, 1024], P(('dp', 'tensor'))
- grad_att_value: float32 [1024, 1024], P(('dp', 'tensor'))
- grad_att_recept: float32 [1024, 1024], P(('dp', 'tensor'))
- grad_att_out: float32 [1024, 1024], P(('dp', 'tensor'))
- grad_ffn_mix_k: float32 [1024], P(('dp', 'tensor'))
- grad_ffn_mix_r: float32 [1024], P(('dp', 'tensor'))
- grad_ffn_recept: float32 [1024, 1024], P(('dp', 'tensor'))
- grad_ffn_key: float32 [1024, 4096], P('dp', 'tensor')
- grad_ffn_value: float32 [4096, 1024], P('tensor', 'dp')
Inputs may be any that keep to these rules, and one draw needn't show every extreme that they name: `text_boundary_indicators`: position 0 of every row is a document start, and each row has at most 3 further starts.
All inputs are finite; a program needn't handle non-finite values.
Results may differ from a plain program's by a relative error of at most 0.02.
Values may be sent and summed in bfloat16 or wider, within the bound.
A program may use at most 192 MiB of HBM per device.

v0:
```python
import jax
import jax.numpy as jnp
from jax import lax
from jax.sharding import PartitionSpec as P


def shifted(value, axis, steps):
    count = lax.axis_size(axis)
    first, last = (max(0, -steps), min(count, count - steps))
    return lax.ppermute(value, axis, [(source, source + steps) for source in range(first, last)])


def carried_in(array, axis, join, neutral):
    place = lax.axis_index(axis)
    gathered = jax.tree.map(
        lambda a, kind: lax.all_gather(a.astype(kind), axis),
        array,
        (jnp.bfloat16, jnp.bfloat16, jnp.bfloat16),
    )
    state = jax.tree.map(lambda a, e: jnp.zeros_like(a) + jnp.asarray(e, a.dtype), array, neutral)

    def one(turn, state):
        return join(
            state,
            jax.tree.map(
                lambda a, own: lax.dynamic_index_in_dim(a, turn, 0, False).astype(own.dtype),
                gathered,
                array,
            ),
        )

    return lax.fori_loop(0, place, one, state)


def entering(array, axis, combine, identity):
    count, place = (lax.axis_size(axis), lax.axis_index(axis))
    everything = jax.tree.map(
        lambda part, kind: lax.all_gather(part.astype(kind), axis),
        array,
        jax.tree.map(lambda a: jnp.bfloat16 if a.dtype == jnp.float32 else a.dtype, array),
    )
    start = jax.tree.map(
        lambda part, zero: jnp.broadcast_to(jnp.asarray(zero, part.dtype), part.shape),
        array,
        identity,
    )

    def turn(k, before):
        at = count - 1 - k
        reached = at > place
        new = combine(
            before, jax.tree.map(lambda part, own: part[at].astype(own.dtype), everything, array)
        )
        return jax.tree.map(lambda a, b: jnp.where(reached, a, b), new, before)

    return lax.fori_loop(0, count, turn, start)


def layer_norm(values, scale_vec, shift_vec):
    center = values - jnp.mean(values, axis=-1, keepdims=True)
    inverse = lax.rsqrt(jnp.mean(center * center, axis=-1, keepdims=True) + 1e-05)
    normed = center * inverse
    return (normed * scale_vec + shift_vec, normed, inverse)


def norm_back(upstream, normed, inverse, scale_vec):
    scaled = upstream * scale_vec
    inner = (
        scaled
        - jnp.mean(scaled, axis=-1, keepdims=True)
        - normed * jnp.mean(scaled * normed, axis=-1, keepdims=True)
    )
    return (
        inverse * inner,
        jnp.sum(upstream * normed, axis=(0, 1)),
        jnp.sum(upstream, axis=(0, 1)),
    )


def shift_prev(values, persist_indicator):
    arrived = shifted(values[:, -1:, :], "tensor", 1)
    return jnp.concatenate([arrived, values[:, :-1]], axis=1) * persist_indicator[:, :, None]


def shift_back(upstream, persist_indicator):
    masked = upstream * persist_indicator[:, :, None]
    arrived = shifted(masked[:, :1, :], "tensor", -1)
    return jnp.concatenate([masked[:, 1:], arrived], axis=1)


def project(values, matrix):
    return jnp.einsum("rtd,de->rte", values, matrix, preferred_element_type=jnp.float32)


def project_back(upstream, matrix):
    return jnp.einsum("rte,de->rtd", upstream, matrix, preferred_element_type=jnp.float32)


def outer_sum(values, upstream):
    return jnp.einsum("rtd,rte->de", values, upstream, preferred_element_type=jnp.float32)


def mix_back(upstreams, shares, differ, persist_indicator):
    toward = jnp.zeros_like(differ)
    behind = jnp.zeros_like(differ)
    share_grads = []
    for upstream, share in zip(upstreams, shares):
        toward = toward + upstream * share
        behind = behind + upstream * (1.0 - share)
        share_grads.append(jnp.sum(upstream * differ, axis=(0, 1)))
    return (toward + shift_back(behind, persist_indicator), share_grads)


def chain_combine(earlier, later):
    return (
        earlier[0] * later[0],
        later[0] * earlier[1] + later[1],
        later[0] * earlier[2] + later[2],
    )


def scan_fragments(
    lookup_wide, payload_wide, fading_power, reward_coords, text_boundary_indicators
):
    decay_rate = jnp.exp(fading_power)
    row_count, span_len, width_len = lookup_wide.shape
    block_len = min(32, span_len)
    block_count = span_len // block_len
    places = jnp.arange(block_len, dtype=jnp.float32)
    rising = jnp.exp(places[:, None] * decay_rate)
    falling = jnp.exp(-(places[:, None] - 1.0) * decay_rate)
    trailing = jnp.exp(-(block_len - 1.0 - places)[:, None] * decay_rate)
    leading = jnp.exp(-places[:, None] * decay_rate)
    settle = jnp.exp(-block_len * decay_rate)
    before = places[:, None] > places[None, :]

    def split_blocks(values):
        return jnp.swapaxes(
            values.reshape((row_count, block_count, block_len) + values.shape[2:]), 0, 1
        )

    def advance(state_pair, scanned):
        accrued_dividend_sum, accrued_divisor_sum = state_pair
        lookup_narrow, payload_narrow, reset_b = scanned
        tree_levels = jnp.cumsum(reset_b, axis=1)
        linked = ((tree_levels[:, :, None] == tree_levels[:, None, :]) & before).astype(jnp.float32)
        key_term = jnp.exp(lookup_narrow)
        keyed_value = key_term * payload_narrow
        inside_numerator = falling * jnp.einsum(
            "rti,rid->rtd", linked, rising * keyed_value, precision=lax.Precision.HIGHEST
        )
        interior_divisor_sum = falling * jnp.einsum(
            "rti,rid->rtd", linked, rising * key_term, precision=lax.Precision.HIGHEST
        )
        leftover_multiplier = (tree_levels == 0).astype(jnp.float32)[:, :, None] * leading
        reward_multiplier = jnp.exp(reward_coords + lookup_narrow)
        above_total = (
            inside_numerator
            + reward_multiplier * payload_narrow
            + leftover_multiplier * accrued_dividend_sum[:, None, :]
        )
        below_total = (
            interior_divisor_sum
            + reward_multiplier
            + leftover_multiplier * accrued_divisor_sum[:, None, :]
        )
        ending = (tree_levels == tree_levels[:, -1:]).astype(jnp.float32)[:, :, None] * trailing
        intact = (tree_levels[:, -1] == 0).astype(jnp.float32)[:, None] * settle
        new_num = intact * accrued_dividend_sum + jnp.sum(ending * keyed_value, axis=1)
        new_den = intact * accrued_divisor_sum + jnp.sum(ending * key_term, axis=1)
        return ((new_num, new_den), (above_total, below_total))

    initial = jnp.zeros((row_count, width_len), jnp.float32)
    (total_num, total_den), (uppers, lowers) = lax.scan(
        advance,
        (initial, initial),
        (
            split_blocks(lookup_wide),
            split_blocks(payload_wide),
            split_blocks(text_boundary_indicators),
        ),
    )

    def join_blocks(values):
        return jnp.swapaxes(values, 0, 1).reshape(row_count, span_len, width_len)

    tree_levels = jnp.cumsum(text_boundary_indicators, axis=1)
    reaching = (tree_levels == 0).astype(jnp.float32)[:, :, None] * jnp.exp(
        -jnp.arange(span_len, dtype=jnp.float32)[:, None] * decay_rate
    )
    passing = (tree_levels[:, -1] == 0).astype(jnp.float32)[:, None] * jnp.exp(
        -span_len * decay_rate
    )
    return (join_blocks(uppers), join_blocks(lowers), reaching, total_num, total_den, passing)


def recurrence_finish(pieces_list, incoming_num, incoming_den):
    above_total = pieces_list[0] + pieces_list[2] * incoming_num[:, None, :]
    below_total = pieces_list[1] + pieces_list[2] * incoming_den[:, None, :]
    return (above_total / below_total, below_total)


def ffn_apply(inputs, key_weight, value_weight):
    hidden_pre = project(inputs, key_weight)
    hidden = jnp.square(jax.nn.relu(hidden_pre)).astype(jnp.bfloat16)
    return (hidden_pre, hidden, project(hidden, value_weight))


def ffn_grads(inputs, hidden_pre, hidden, upstream, key_weight, value_weight):
    g_hidden = jnp.einsum("rtd,fd->rtf", upstream, value_weight, preferred_element_type=jnp.float32)
    grad_value = jnp.einsum("rtf,rtd->fd", hidden, upstream, preferred_element_type=jnp.float32)
    g_pre = (2.0 * jax.nn.relu(hidden_pre) * g_hidden).astype(jnp.bfloat16)
    grad_key = jnp.einsum("rtd,rtf->df", inputs, g_pre, preferred_element_type=jnp.float32)
    g_inputs = jnp.einsum("rtf,df->rtd", g_pre, key_weight, preferred_element_type=jnp.float32)
    return (g_inputs, grad_key, grad_value)


def shards(
    incoming_embeddings,
    text_boundary_indicators,
    upstream_sensitivity,
    primary_standardize_scaling,
    primary_standardize_offset,
    secondary_standardize_scaling,
    secondary_standardize_offset,
    feature_fading_logarithms,
    present_symbol_reward,
    timemix_lookup_blend,
    timemix_payload_blend,
    timemix_gate_blend,
    timemix_lookup_proj,
    timemix_payload_proj,
    timemix_gate_proj,
    timemix_emit_proj,
    feedmix_lookup_blend,
    feedmix_gate_blend,
    feedmix_gate_proj,
    feedmix_lookup_proj,
    feedmix_payload_proj,
):
    gathered_portions = (
        lax.all_gather(primary_standardize_scaling, ("dp", "tensor"), axis=0, tiled=True),
        lax.all_gather(primary_standardize_offset, ("dp", "tensor"), axis=0, tiled=True),
        lax.all_gather(secondary_standardize_scaling, ("dp", "tensor"), axis=0, tiled=True),
        lax.all_gather(secondary_standardize_offset, ("dp", "tensor"), axis=0, tiled=True),
        lax.all_gather(feature_fading_logarithms, ("dp", "tensor"), axis=0, tiled=True),
        lax.all_gather(present_symbol_reward, ("dp", "tensor"), axis=0, tiled=True),
        lax.all_gather(timemix_lookup_blend, ("dp", "tensor"), axis=0, tiled=True),
        lax.all_gather(timemix_payload_blend, ("dp", "tensor"), axis=0, tiled=True),
        lax.all_gather(timemix_gate_blend, ("dp", "tensor"), axis=0, tiled=True),
        lax.all_gather(timemix_lookup_proj, ("dp", "tensor"), axis=0, tiled=True),
        lax.all_gather(timemix_payload_proj, ("dp", "tensor"), axis=0, tiled=True),
        lax.all_gather(timemix_gate_proj, ("dp", "tensor"), axis=0, tiled=True),
        lax.all_gather(timemix_emit_proj, ("dp", "tensor"), axis=0, tiled=True),
        lax.all_gather(feedmix_lookup_blend, ("dp", "tensor"), axis=0, tiled=True),
        lax.all_gather(feedmix_gate_blend, ("dp", "tensor"), axis=0, tiled=True),
        lax.all_gather(feedmix_gate_proj, ("dp", "tensor"), axis=0, tiled=True),
    )
    initial_scaling_coords = gathered_portions[0].astype(jnp.float32)
    initial_offset_coords = gathered_portions[1].astype(jnp.float32)
    later_scaling_coords = gathered_portions[2].astype(jnp.float32)
    later_offset_coords = gathered_portions[3].astype(jnp.float32)
    fading_power = gathered_portions[4].astype(jnp.float32)
    reward_coords = gathered_portions[5].astype(jnp.float32)
    share_k1 = gathered_portions[6].astype(jnp.float32)
    share_v1 = gathered_portions[7].astype(jnp.float32)
    share_r1 = gathered_portions[8].astype(jnp.float32)
    lookup_coefficients_initial = gathered_portions[9]
    payload_coefficients_initial = gathered_portions[10]
    gate_coefficients_initial = gathered_portions[11]
    emit_coefficients_initial = gathered_portions[12]
    share_k2 = gathered_portions[13].astype(jnp.float32)
    share_r2 = gathered_portions[14].astype(jnp.float32)
    gate_coefficients_later = gathered_portions[15]
    lookup_coefficients_later, payload_coefficients_later = (
        lax.all_gather(feedmix_lookup_proj, "dp", axis=0, tiled=True),
        lax.all_gather(feedmix_payload_proj, "dp", axis=1, tiled=True),
    )
    persist_indicator = (1 - text_boundary_indicators).astype(jnp.float32)
    inputs = incoming_embeddings.astype(jnp.float32)
    normed_one, unit_one, inverse_one = layer_norm(
        inputs, initial_scaling_coords, initial_offset_coords
    )
    prev_one = shift_prev(normed_one, persist_indicator)
    differ_one = normed_one - prev_one
    in_key = (prev_one + differ_one * share_k1).astype(jnp.bfloat16)
    in_value = (prev_one + differ_one * share_v1).astype(jnp.bfloat16)
    in_recept = (prev_one + differ_one * share_r1).astype(jnp.bfloat16)
    initial_lookup_lines = project(in_key, lookup_coefficients_initial)
    initial_payload_lines = project(in_value, payload_coefficients_initial)
    recept_one = project(in_recept, gate_coefficients_initial)
    pieces_list = scan_fragments(
        initial_lookup_lines,
        initial_payload_lines,
        fading_power,
        reward_coords,
        text_boundary_indicators,
    )
    passing = pieces_list[5]
    identity = (jnp.ones_like(passing), jnp.zeros_like(passing), jnp.zeros_like(passing))
    unused_item, incoming_num, incoming_den = carried_in(
        (passing, pieces_list[3], pieces_list[4]), "tensor", chain_combine, identity
    )
    blended_mean_state, below_total = recurrence_finish(pieces_list, incoming_num, incoming_den)
    sig_one = jax.nn.sigmoid(recept_one)
    mixed_att = (sig_one * blended_mean_state).astype(jnp.bfloat16)
    resid_one = inputs + project(mixed_att, emit_coefficients_initial)
    normed_two, unit_two, inverse_two = layer_norm(
        resid_one, later_scaling_coords, later_offset_coords
    )
    prev_two = shift_prev(normed_two, persist_indicator)
    differ_two = normed_two - prev_two
    in_key_two = (prev_two + differ_two * share_k2).astype(jnp.bfloat16)
    in_recept_two = (prev_two + differ_two * share_r2).astype(jnp.bfloat16)
    recept_two = project(in_recept_two, gate_coefficients_later)
    sig_two = jax.nn.sigmoid(recept_two)
    row_inputs = lax.all_gather(in_key_two, "tensor", axis=1, tiled=True)
    hidden_pre, hidden, partial_value = ffn_apply(
        row_inputs, lookup_coefficients_later, payload_coefficients_later
    )
    value_two = lax.psum_scatter(
        partial_value.astype(jnp.bfloat16), "tensor", scatter_dimension=1, tiled=True
    ).astype(jnp.float32)
    layer_out = (resid_one + sig_two * value_two).astype(jnp.bfloat16)
    upstream = upstream_sensitivity.astype(jnp.float32)
    g_value_two = (upstream * sig_two).astype(jnp.bfloat16)
    g_recept_two = (upstream * value_two * sig_two * (1.0 - sig_two)).astype(jnp.bfloat16)
    grad_recept_two = outer_sum(in_recept_two, g_recept_two)
    g_mix_r2 = project_back(g_recept_two, gate_coefficients_later)
    row_grads = lax.all_gather(g_value_two, "tensor", axis=1, tiled=True)
    partial_grad, grad_key_two, grad_value_two = ffn_grads(
        row_inputs,
        hidden_pre,
        hidden,
        row_grads,
        lookup_coefficients_later,
        payload_coefficients_later,
    )
    g_mix_k2 = lax.psum_scatter(
        partial_grad.astype(jnp.bfloat16), "tensor", scatter_dimension=1, tiled=True
    ).astype(jnp.float32)
    sum_key_two, sum_value_two = (
        lax.psum_scatter(
            grad_key_two.astype(jnp.bfloat16), "dp", scatter_dimension=0, tiled=True
        ).astype(jnp.float32),
        lax.psum_scatter(
            grad_value_two.astype(jnp.bfloat16), "dp", scatter_dimension=1, tiled=True
        ).astype(jnp.float32),
    )
    g_normed_two, shares_two = mix_back(
        (g_mix_k2, g_mix_r2), (share_k2, share_r2), differ_two, persist_indicator
    )
    g_resid_part, grad_gain_two, grad_bias_two = norm_back(
        g_normed_two, unit_two, inverse_two, later_scaling_coords
    )
    g_resid = upstream + g_resid_part
    g_branch = g_resid.astype(jnp.bfloat16)
    grad_out_one = outer_sum(mixed_att, g_branch)
    g_mixed = project_back(g_branch, emit_coefficients_initial)
    g_weighted = g_mixed * sig_one
    g_recept_one = (g_mixed * blended_mean_state * sig_one * (1.0 - sig_one)).astype(jnp.bfloat16)
    reaching = pieces_list[2]
    g_in_num = jnp.sum(g_weighted * reaching / below_total, axis=1)
    g_in_den = -jnp.sum(g_weighted * reaching * blended_mean_state / below_total, axis=1)
    unused_item, back_num, back_den = entering(
        (passing, g_in_num, g_in_den), "tensor", chain_combine, identity
    )
    g_passing = back_num * incoming_num + back_den * incoming_den

    def device_fragment(lookup_wide, payload_wide, fading_coords, reward_power):
        shard_pieces = scan_fragments(
            lookup_wide, payload_wide, fading_coords, reward_power, text_boundary_indicators
        )
        local_out, unused_item = recurrence_finish(shard_pieces, incoming_num, incoming_den)
        return (local_out, shard_pieces[3], shard_pieces[4], shard_pieces[5])

    unused_item, reverse_pass_rule = jax.vjp(
        device_fragment, initial_lookup_lines, initial_payload_lines, fading_power, reward_coords
    )
    derivative_lookup_wide, derivative_payload_wide, fading_derivative, reward_derivative = (
        reverse_pass_rule((g_weighted, back_num, back_den, g_passing))
    )
    g_key_one = derivative_lookup_wide.astype(jnp.bfloat16)
    g_value_one = derivative_payload_wide.astype(jnp.bfloat16)
    grad_key_one = outer_sum(in_key, g_key_one)
    grad_value_one = outer_sum(in_value, g_value_one)
    grad_recept_one = outer_sum(in_recept, g_recept_one)
    g_mix_k1 = project_back(g_key_one, lookup_coefficients_initial)
    g_mix_v1 = project_back(g_value_one, payload_coefficients_initial)
    g_mix_r1 = project_back(g_recept_one, gate_coefficients_initial)
    g_normed_one, shares_one = mix_back(
        (g_mix_k1, g_mix_v1, g_mix_r1),
        (share_k1, share_v1, share_r1),
        differ_one,
        persist_indicator,
    )
    g_input_part, grad_gain_one, grad_bias_one = norm_back(
        g_normed_one, unit_one, inverse_one, initial_scaling_coords
    )
    grad_tokens = g_resid + g_input_part
    summed = (
        lax.psum_scatter(grad_gain_one, ("dp", "tensor"), scatter_dimension=0, tiled=True),
        lax.psum_scatter(grad_bias_one, ("dp", "tensor"), scatter_dimension=0, tiled=True),
        lax.psum_scatter(grad_gain_two, ("dp", "tensor"), scatter_dimension=0, tiled=True),
        lax.psum_scatter(grad_bias_two, ("dp", "tensor"), scatter_dimension=0, tiled=True),
        lax.psum_scatter(fading_derivative, ("dp", "tensor"), scatter_dimension=0, tiled=True),
        lax.psum_scatter(reward_derivative, ("dp", "tensor"), scatter_dimension=0, tiled=True),
        lax.psum_scatter(shares_one[0], ("dp", "tensor"), scatter_dimension=0, tiled=True),
        lax.psum_scatter(shares_one[1], ("dp", "tensor"), scatter_dimension=0, tiled=True),
        lax.psum_scatter(shares_one[2], ("dp", "tensor"), scatter_dimension=0, tiled=True),
        lax.psum_scatter(grad_key_one, ("dp", "tensor"), scatter_dimension=0, tiled=True),
        lax.psum_scatter(grad_value_one, ("dp", "tensor"), scatter_dimension=0, tiled=True),
        lax.psum_scatter(grad_recept_one, ("dp", "tensor"), scatter_dimension=0, tiled=True),
        lax.psum_scatter(grad_out_one, ("dp", "tensor"), scatter_dimension=0, tiled=True),
        lax.psum_scatter(shares_two[0], ("dp", "tensor"), scatter_dimension=0, tiled=True),
        lax.psum_scatter(shares_two[1], ("dp", "tensor"), scatter_dimension=0, tiled=True),
        lax.psum_scatter(grad_recept_two, ("dp", "tensor"), scatter_dimension=0, tiled=True),
    )
    return (
        layer_out,
        grad_tokens,
        summed[0],
        summed[1],
        summed[2],
        summed[3],
        summed[4],
        summed[5],
        summed[6],
        summed[7],
        summed[8],
        summed[9],
        summed[10],
        summed[11],
        summed[12],
        summed[13],
        summed[14],
        summed[15],
        sum_key_two,
        sum_value_two,
    )


def solution(mesh):
    in_specs = (
        P("dp", "tensor", None),
        P("dp", "tensor"),
        P("dp", "tensor", None),
        P(("dp", "tensor")),
        P(("dp", "tensor")),
        P(("dp", "tensor")),
        P(("dp", "tensor")),
        P(("dp", "tensor")),
        P(("dp", "tensor")),
        P(("dp", "tensor")),
        P(("dp", "tensor")),
        P(("dp", "tensor")),
        P(("dp", "tensor"), None),
        P(("dp", "tensor"), None),
        P(("dp", "tensor"), None),
        P(("dp", "tensor"), None),
        P(("dp", "tensor")),
        P(("dp", "tensor")),
        P(("dp", "tensor"), None),
        P("dp", "tensor"),
        P("tensor", "dp"),
    )
    out_specs = (
        P("dp", "tensor", None),
        P("dp", "tensor", None),
        P(("dp", "tensor")),
        P(("dp", "tensor")),
        P(("dp", "tensor")),
        P(("dp", "tensor")),
        P(("dp", "tensor")),
        P(("dp", "tensor")),
        P(("dp", "tensor")),
        P(("dp", "tensor")),
        P(("dp", "tensor")),
        P(("dp", "tensor"), None),
        P(("dp", "tensor"), None),
        P(("dp", "tensor"), None),
        P(("dp", "tensor"), None),
        P(("dp", "tensor")),
        P(("dp", "tensor")),
        P(("dp", "tensor"), None),
        P("dp", "tensor"),
        P("tensor", "dp"),
    )
    return jax.shard_map(shards, mesh=mesh, in_specs=in_specs, out_specs=out_specs, check_vma=False)
```

profile of v0, /device:TPU:0, one launch (start us, length us, event | category | flops | bytes accessed | tf_op | source)
XLA Modules:
  0.0 1474.6 jit_solution(9288518616579800908)
XLA Ops:
  18.7 42.9 %all-reduce.23 = (bf16[1024]{0:T(1024)(128)(2,1)S(1)}, bf16[1024]{0:T(1024)(128)(2,1)S(1)}, bf16[1024]{0:T(1024)(128)(2,1)S(1)}, bf16[1024]{0:T(1024)(128)(2,1)S...) all-reduce(bf16[1024]{0:T(1024)(128)(2,1)S(1)} %dynamic-update-slic, ...), channel_id=1, replica_groups=mesh['dp'=16,'tensor'=2] {'dp','tensor'}, use_global_device_ids=true, to_apply=%add.2 | all-reduce | flops 11264 | bytes 45056
  74.3 4.6 add_convert_fusion.2
  78.9 4.6 fusion.183
  83.6 44.9 %all-gather.19.cloned.1.call-done = bf16[1024,1024]{1,0:T(8,128)(2,1)} async-done(((bf16[32,1024]{1,0:T(8,128)(2,1)}), bf16[1024,1024]{1,0:T(8,128)(2,1)}) %all-gather.19.cloned.1.call-update) | async-done | bytes 2097168 | tf_op jit(solution)/shard_map/all_gather | solution.py:251
  128.5 4.2 fusion.180
  134.5 104.6 %while.142 = (s32[]{:T(128)}, f32[1,1024]{1,0:T(1,128)S(1)}, f32[1,1024]{1,0:T(1,128)S(1)}, f32[16,1,32,1024]{3,2,1,0:T(8,128)}, f32[16,1,32,1024]{3,2,1,0:T(8,1...) while((s32[]{:T(128)}, f32[1,1024]{1,0:T(1,128)S(1)}, ...), condition=%wide.region_6.7_spmd.clone.clone.clone, body=%wide.region_2.6_spmd.clone.clone.clone.sunk | while | flops 26128484 | bytes 1409369 | solution.py:174
  243.1 7.0 multiply_convert_fusion.3
  250.0 3.3 fusion.214
  257.1 4.1 fusion.189
  263.6 7.3 all-gather.27.cloned.1.call-done
  270.9 79.9 %all-gather.29.cloned.1.call-done = bf16[1024,2048]{1,0:T(8,128)(2,1)} async-done(((bf16[64,2048]{1,0:T(8,128)(2,1)}), bf16[1024,2048]{1,0:T(8,128)(2,1)}) %all-gather.29.cloned.1.call-update) | async-done | bytes 4194320 | tf_op jit(solution)/shard_map/all_gather | solution.py:276
  350.9 10.6 fusion.168
  361.4 66.9 %all-gather.31.cloned.1.call-done = bf16[2048,1024]{0,1:T(8,128)(2,1)} async-done(((bf16[2048,64]{0,1:T(8,128)(2,1)}), bf16[2048,1024]{0,1:T(8,128)(2,1)}) %all-gather.31.cloned.1.call-update) | async-done | bytes 4194320 | tf_op jit(solution)/shard_map/all_gather | solution.py:277
  428.3 10.4 convert_bitcast_fusion.1
  438.8 47.4 %all-gather.25.cloned.1.call-done = bf16[1024,1024]{1,0:T(8,128)(2,1)} async-done(((bf16[32,1024]{1,0:T(8,128)(2,1)}), bf16[1024,1024]{1,0:T(8,128)(2,1)}) %all-gather.25.cloned.1.call-update) | async-done | bytes 2097168 | tf_op jit(solution)/shard_map/all_gather | solution.py:257
  486.2 11.3 reduce-scatter.10.cloned.1.call-done
  497.5 6.2 fusion.190
  504.3 11.4 all-gather.33.cloned.1.call-done
  515.7 9.9 multiply_convert_fusion
  527.5 5.7 convert_bitcast_fusion
  533.3 10.6 convolution_convert_fusion
  544.1 9.4 convolution_convert_fusion.1
  555.8 3.3 fusion.219
  559.3 7.1 fusion.159
  582.2 196.8 %while.144 = (s32[]{:T(128)}, f32[1,1024]{1,0:T(1,128)S(1)}, f32[1,1024]{1,0:T(1,128)S(1)}, f32[16,1,32,1024]{3,2,1,0:T(8,128)}, f32[16,1,32,1024]{3,2,1,0:T(8,1...) while((s32[]{:T(128)}, f32[1,1024]{1,0:T(1,128)S(1)}, ...), condition=%wide.region_25.26_spmd.clone.clone.clone.clone, body=%wide.region_21.25_spmd.clone.clone.clone.clone.sunk | while | flops 26199268 | bytes 2509438 | solution.py:174
  592.3 2.3 multiply_dynamic-update-slice_fusion.2
  616.9 2.3 multiply_dynamic-update-slice_fusion.2
  629.3 2.3 multiply_dynamic-update-slice_fusion.2
  641.5 2.3 multiply_dynamic-update-slice_fusion.2
  678.4 2.3 multiply_dynamic-update-slice_fusion.2
  727.7 2.3 multiply_dynamic-update-slice_fusion.2
  740.0 2.3 multiply_dynamic-update-slice_fusion.2
  752.3 2.3 multiply_dynamic-update-slice_fusion.2
  764.5 2.3 multiply_dynamic-update-slice_fusion.2
  787.2 2.4 fusion.211
  790.4 4.7 fusion.179
  795.2 2.6 all-gather.4
  799.7 4.5 fusion.195
  804.2 236.2 %while.143 = (s32[]{:T(128)}, f32[32,1024]{1,0:T(8,128)}, f32[32,1024]{1,0:T(8,128)S(1)}, f32[32,1024]{1,0:T(8,128)S(1)}, f32[1024]{0:T(1024)}, /*index=5*/f32[3...) while((s32[]{:T(128)}, f32[32,1024]{1,0:T(8,128)}, ...), condition=%wide.region_30.31_spmd.clone.clone.clone, body=%wide.region_26.30_spmd.clone.clone.clone.sunk | while | flops 26747908 | bytes 4625540 | solution.py:174
  1040.5 4.8 fusion.191
  1045.3 4.8 fusion.218
  1050.5 4.8 fusion.193
  1056.1 3.3 fusion.217
  1070.5 42.0 %all-reduce.22 = (f32[1024]{0:T(1024)S(1)}, f32[1024]{0:T(1024)S(1)}, f32[1024]{0:T(1024)S(1)}, f32[1024]{0:T(1024)S(1)}, f32[1024]{0:T(1024)S(1)}, /*index=5*/f...) all-reduce(f32[1024]{0:T(1024)S(1)} %get-tuple-element.2317, ...), channel_id=9, replica_groups=mesh['dp'=16,'tensor'=2] {'dp','tensor'}, use_global_device_ids=true, to_apply=%region_34.35.clone | all-reduce | flops 11264 | bytes 90112
  1118.9 3.6 fusion.145
  1126.1 61.9 %reduce-scatter.16.cloned.1.call-done = f32[32,1024]{1,0:T(8,128)} async-done(((f32[1024,1024]{1,0:T(8,128)}), f32[32,1024]{1,0:T(8,128)}) %reduce-scatter.16.cloned.1.call-update) | async-done | bytes 131088 | tf_op jit(solution)/shard_map/reduce_scatter | solution.py:412
  1188.0 139.7 %reduce-scatter.18.cloned.1.call-done = f32[32,1024]{1,0:T(8,128)} async-done(((f32[1024,1024]{1,0:T(8,128)}), f32[32,1024]{1,0:T(8,128)}) %reduce-scatter.18.cloned.1.call-update) | async-done | bytes 131088 | tf_op jit(solution)/shard_map/reduce_scatter | solution.py:413
  1327.7 139.6 %reduce-scatter.14.cloned.1.call-done = f32[32,1024]{1,0:T(8,128)} async-done(((f32[1024,1024]{1,0:T(8,128)}), f32[32,1024]{1,0:T(8,128)}) %reduce-scatter.14.cloned.1.call-update) | async-done | bytes 131088 | tf_op jit(solution)/shard_map/reduce_scatter | solution.py:411
  (927 shorter events, 582.5 us)
Async XLA Ops:
  7.2 57.6 %copy-start = (bf16[1,512,1024]{2,1,0:T(8,128)(2,1)S(1)}, bf16[1,512,1024]{2,1,0:T(8,128)(2,1)}, u32[]{:S(2)}) copy-start(bf16[1,512,1024]{2,1,0:T(8,128)(2,1)} %param.31) | copy-start | bytes 3145732
  7.2 71.7 %all-gather.21.cloned.1.call-start = ((), (), s32[]{:S(2)}) async-start(), calls=%async_computation.11 | async-start | bytes 2162688 | tf_op jit(solution)/shard_map/all_gather | solution.py:252
  7.9 120.6 %all-gather.19.cloned.1.call-start = ((), (), s32[]{:S(2)}) async-start(), calls=%async_computation.10 | async-start | bytes 2162688 | tf_op jit(solution)/shard_map/all_gather | solution.py:251
  8.7 234.4 %all-gather.17.cloned.1.call-start = ((), (), s32[]{:S(2)}) async-start(), calls=%async_computation.9 | async-start | bytes 2162688 | tf_op jit(solution)/shard_map/all_gather | solution.py:253
  9.4 240.6 %all-gather.23.cloned.1.call-start = ((), (), s32[]{:S(2)}) async-start(), calls=%async_computation.12 | async-start | bytes 2162688 | tf_op jit(solution)/shard_map/all_gather | solution.py:254
  61.6 10.1 copy-start.61
  61.6 10.7 copy-start.66
  61.6 10.7 copy-start.63
  61.6 10.7 copy-start.68
  61.6 12.6 copy-start.42
  61.6 12.6 copy-start.28
  63.1 11.2 copy-start.40
  64.8 14.1 copy-start.46
  65.2 13.7 copy-start.4
  65.2 9.0 collective-permute-start
  67.1 203.8 %all-gather.27.cloned.1.call-start = ((), (), s32[]{:S(2)}) async-start(), calls=%async_computation.14 | async-start | bytes 3145728 | tf_op jit(solution)/shard_map/all_gather | solution.py:317
  71.7 487.6 %copy-start.38 = (f32[1,512]{1,0:T(1,128)}, f32[1,512]{1,0:T(1,128)S(1)}, u32[]{:S(2)}) copy-start(f32[1,512]{1,0:T(1,128)S(1)} %get-tuple-element.2603) | copy-start | bytes 6148
  72.3 6.6 copy-start.48
  72.3 6.6 copy-start.50
  72.3 6.6 copy-start.52
  74.2 4.7 copy-start.54
  78.9 49.6 %copy-start.16 = (bf16[1,512,1024]{2,1,0:T(8,128)(2,1)S(1)}, bf16[1,512,1024]{2,1,0:T(8,128)(2,1)}, u32[]{:S(2)}) copy-start(bf16[1,512,1024]{2,1,0:T(8,128)(2,1)} %get-tuple-element.2592) | copy-start | bytes 3145732
  239.2 10.9 copy-start.13
  243.0 546.5 %copy-start.24 = (f32[1,1024]{1,0:T(1,128)}, f32[1,1024]{1,0:T(1,128)S(1)}, u32[]{:S(2)}) copy-start(f32[1,1024]{1,0:T(1,128)S(1)} %get-tuple-element.1289) | copy-start | bytes 12292
  243.0 546.5 %copy-start.26 = (f32[1,1024]{1,0:T(1,128)}, f32[1,1024]{1,0:T(1,128)S(1)}, u32[]{:S(2)}) copy-start(f32[1,1024]{1,0:T(1,128)S(1)} %get-tuple-element.1287) | copy-start | bytes 12292
  254.1 7.1 copy-start.1
  254.1 3.0 collective-permute-start.1
  261.2 89.6 %all-gather.29.cloned.1.call-start = ((), (), s32[]{:S(2)}) async-start(), calls=%async_computation.15 | async-start | bytes 4456448 | tf_op jit(solution)/shard_map/all_gather | solution.py:276
  261.8 166.5 %all-gather.31.cloned.1.call-start = ((), (), s32[]{:S(2)}) async-start(), calls=%async_computation.16 | async-start | bytes 4456448 | tf_op jit(solution)/shard_map/all_gather | solution.py:277
  262.6 223.6 %all-gather.25.cloned.1.call-start = ((), (), s32[]{:S(2)}) async-start(), calls=%async_computation.13 | async-start | bytes 2162688 | tf_op jit(solution)/shard_map/all_gather | solution.py:257
  263.3 234.2 %reduce-scatter.10.cloned.1.call-start = ((), (), s32[]{:S(2)}) async-start(), calls=%async_computation.17 | async-start | bytes 3145728 | tf_op jit(solution)/shard_map/reduce_scatter | solution.py:321
  438.8 76.9 %all-gather.33.cloned.1.call-start = ((), (), s32[]{:S(2)}) async-start(), calls=%async_computation.18 | async-start | bytes 3145728 | tf_op jit(solution)/shard_map/all_gather | solution.py:330
  503.8 55.5 %reduce-scatter.12.cloned.1.call-start = ((), (), s32[]{:S(2)}) async-start(), calls=%async_computation.19 | async-start | bytes 3145728 | tf_op jit(solution)/shard_map/reduce_scatter | solution.py:339
  515.7 11.8 copy-start.70
  533.3 589.3 %reduce-scatter.26.cloned.1.call-start = ((), (), s32[]{:S(2)}) async-start(), calls=%async_computation.26 | async-start | bytes 4456448 | tf_op jit(solution)/shard_map/reduce_scatter | solution.py:346
  543.9 580.4 %reduce-scatter.24.cloned.1.call-start = ((), (), s32[]{:S(2)}) async-start(), calls=%async_computation.25 | async-start | bytes 4456448 | tf_op jit(solution)/shard_map/reduce_scatter | solution.py:343
  553.5 572.6 %reduce-scatter.22.cloned.1.call-start = ((), (), s32[]{:S(2)}) async-start(), calls=%async_computation.24 | async-start | bytes 4325376 | tf_op jit(solution)/shard_map/reduce_scatter | solution.py:417
  559.2 566.9 %reduce-scatter.20.cloned.1.call-start = ((), (), s32[]{:S(2)}) async-start(), calls=%async_computation.23 | async-start | bytes 4325376 | tf_op jit(solution)/shard_map/reduce_scatter | solution.py:414
  566.4 4.7 copy-start.9
  566.4 214.6 %collective-permute-start.2 = (f32[1,1,1024]{2,1,0:T(1,128)S(1)}, f32[1,1,1024]{2,1,0:T(1,128)S(1)}, u32[]{:S(2)}, u32[]{:S(2)}) collective-permute-start(f32[1,1,1024]{2,1,0:T(1,128)S(1)} %slice.68), channel_id=1, source_target_pairs={{1,0},{3,2},{5,4},{7,6},{9,8},{11,10},{13,12},{15,14},{17,16},{19,... | collective-permute-start | bytes 12296 | tf_op jit(solution)/shard_map/ppermute | solution.py:10
  784.3 5.2 copy-start.2
  790.4 9.3 copy-start.3
  799.6 4.5 copy-start.30
  799.7 4.5 copy-start.32
  804.2 383.8 %reduce-scatter.16.cloned.1.call-start = ((), (), s32[]{:S(2)}) async-start(), calls=%async_computation.21 | async-start | bytes 4325376 | tf_op jit(solution)/shard_map/reduce_scatter | solution.py:412
  1045.3 282.4 %reduce-scatter.18.cloned.1.call-start = ((), (), s32[]{:S(2)}) async-start(), calls=%async_computation.22 | async-start | bytes 4325376 | tf_op jit(solution)/shard_map/reduce_scatter | solution.py:413
  1050.2 417.1 %reduce-scatter.14.cloned.1.call-start = ((), (), s32[]{:S(2)}) async-start(), calls=%async_computation.20 | async-start | bytes 4325376 | tf_op jit(solution)/shard_map/reduce_scatter | solution.py:411
  1063.2 3.3 collective-permute-start.3
  (48 other events, 94.2 us)
Sparse Core Ops, SparseCore 0:
  10.9 59.4 all-gather.20
  73.2 55.2 all-gather.18
  131.3 55.3 all-gather.16
  189.5 55.2 all-gather.22
  261.4 9.5 all-gather.26
  273.6 77.2 all-gather.28
  353.6 74.6 all-gather.30
  431.2 54.9 all-gather.24
  489.0 8.4 reduce-scatter.9
  503.9 11.7 all-gather.32
  533.4 10.7 reduce-scatter.11
  546.3 96.2 reduce-scatter.25
  645.0 94.6 reduce-scatter.23
  742.4 140.5 reduce-scatter.21
  885.6 136.9 reduce-scatter.19
  1045.4 142.5 reduce-scatter.15
  1190.7 136.9 reduce-scatter.17
  1330.4 136.8 reduce-scatter.13
where the time goes:
time: 1490 us; the launch traced here: 1470 us
  waiting for transfers between devices  615 us (41%)
  other arithmetic  291 us (20%)
  matrix products  282 us (19%)
  local copies, waits for them, and re-layouts  143 us (10%)
  blocking collectives  94.6 us (6%)
  loops' own time  22.8 us (2%)
  between operations  17.4 us (1%)
    reduce_scatter x1, waiting for transfers between devices, shards(): lax.psum_scatter(grad_recept_one, ('dp', 'tensor'), scatter_dimension=0,...  140 us
    reduce_scatter x1, waiting for transfers between devices, shards(): lax.psum_scatter(grad_key_one, ('dp', 'tensor'), scatter_dimension=0, til...  140 us
    dot_general x48, matrix products, advance(): jnp.einsum('rti,rid->rtd', linked, rising * keyed_value, precision=lax.Pr...  104 us
    dynamic_update_slice x96, other arithmetic, scan_fragments(): lax.scan(advance, (initial, initial), (split_blocks(lookup_wide), split_b...  94.2 us
    unnamed x2, blocking collectives  84.9 us
    all_gather x1, waiting for transfers between devices, shards(): lax.all_gather(feedmix_lookup_proj, 'dp', axis=0, tiled=True)  79.9 us
    all_gather x1, waiting for transfers between devices, shards(): lax.all_gather(feedmix_payload_proj, 'dp', axis=1, tiled=True)  66.9 us
    reduce_scatter x1, waiting for transfers between devices, shards(): lax.psum_scatter(grad_value_one, ('dp', 'tensor'), scatter_dimension=0, t...  61.9 us
  transfers between devices with their start and end apart: 22, of which 11 were waited for; matrix products, arithmetic and copies ran while one was open for 46% of the time, Pallas kernels for 0%

commit v1 on v0

--- a/solution.py
+++ b/solution.py
@@ -1,7 +1,521 @@
+import functools
+
 import jax
 import jax.numpy as jnp
 from jax import lax
+from jax.experimental import pallas as pl
+from jax.experimental.pallas import tpu as pltpu
 from jax.sharding import PartitionSpec as P
+
+F32, BF16 = jnp.float32, jnp.bfloat16
+MESH_ID = pl.DeviceIdType.MESH
+MIB = 1 << 20
+PIECES = 13
+
+
+def place():
+    i, c = lax.axis_index("dp"), lax.axis_index("tensor")
+    return i // 4, i % 4, c
+
+
+def neighbours(z, yx):
+    x = yx + 1 - 2 * (yx % 2)
+    y = (yx + 2) % 4
+    d = (x + 2) % 4
+    zs = (z + 1 - 2 * (z % 2), (z + 2) % 4, 3 - z)
+    return x, y, d, zs
+
+
+def enter(z, yx, c):
+    x, y, d, zs = neighbours(z, yx)
+    barrier = pltpu.get_barrier_semaphore()
+    targets = [(z * 4 + yx, 1 - c), (z * 4 + x, c), (z * 4 + y, c)]
+    targets += [(peer * 4 + yx, c) for peer in zs]
+    for target in targets:
+        pl.semaphore_signal(barrier, inc=1, device_id=target, device_id_type=MESH_ID)
+    pl.semaphore_wait(barrier, len(targets))
+
+
+def remote(src, dst, send, recv, target):
+    return pltpu.make_async_remote_copy(
+        src_ref=src, dst_ref=dst, send_sem=send, recv_sem=recv,
+        device_id=target, device_id_type=MESH_ID,
+    )
+
+
+class Gather:
+    def __init__(self, view, sends, recvs, first=0):
+        self.view, self.sends, self.recvs, self.first = view, sends, recvs, first
+        self.z, self.yx, self.c = place()
+        self.x, self.y, self.d, self.zs = neighbours(self.z, self.yx)
+
+    def to(self, z, yx):
+        return (z * 4 + yx, self.c)
+
+    def copy(self, p, k, ref, target):
+        return remote(ref, ref, self.sends.at[p, k], self.recvs.at[p, k], target)
+
+    def along(self, p):
+        own = self.view(p).at[self.z, self.yx]
+        return [self.copy(p, k, own, self.to(peer, self.yx)) for k, peer in enumerate(self.zs)]
+
+    def plane(self, p):
+        own = self.view(p).at[:, self.yx]
+        return [self.copy(p, 3, own, self.to(self.z, self.x)), self.copy(p, 4, own, self.to(self.z, self.y))]
+
+    def onward(self, p):
+        return [
+            self.copy(p, 5, self.view(p).at[0:2, self.x], self.to(self.z, self.y)),
+            self.copy(p, 6, self.view(p).at[2:4, self.y], self.to(self.z, self.x)),
+        ]
+
+    def start(self, copies):
+        for copy in copies:
+            copy.start()
+
+    def arrive(self, copies):
+        for copy in copies:
+            copy.wait_recv()
+
+    def step(self, p):
+        self.arrive(self.along(p))
+        self.start(self.plane(p))
+
+    def forward(self, p):
+        self.arrive(self.plane(p))
+        self.start(self.onward(p))
+
+    def finish(self, p):
+        for copy in self.along(p) + self.plane(p) + self.onward(p):
+            copy.wait_send()
+
+
+def gather_kernel(own4, other4, rest, vec, g, gv, local_sem, ex_send, ex_recv, sends, recvs, vsends, vrecvs):
+    z, yx, c = place()
+    enter(z, yx, c)
+    half = own4.shape[1]
+    mine = pl.ds(pl.multiple_of(c * half, half), half)
+    partner = (z * 4 + yx, 1 - c)
+    swaps = [
+        remote(other4, g.at[0:4, z, yx, mine], ex_send.at[0], ex_recv.at[0], partner),
+        remote(vec, gv.at[z, yx, c], ex_send.at[1], ex_recv.at[1], partner),
+    ]
+    locals_ = [
+        pltpu.make_async_copy(own4, g.at[0:4, z, yx, mine], local_sem.at[0]),
+        pltpu.make_async_copy(rest, g.at[4:PIECES, z, yx], local_sem.at[1]),
+        pltpu.make_async_copy(vec, gv.at[z, yx, c], local_sem.at[2]),
+    ]
+    for copy in swaps + locals_:
+        copy.start()
+    for copy in swaps + locals_:
+        copy.wait()
+    weights = Gather(lambda p: g.at[p], sends, recvs)
+    vectors = Gather(lambda p: gv, vsends, vrecvs)
+    vectors.start(vectors.along(0))
+
+    def launch(p, carry):
+        weights.start(weights.along(p))
+        return carry
+
+    lax.fori_loop(0, PIECES, launch, 0)
+    vectors.step(0)
+
+    def turn(p, carry):
+        weights.step(p)
+
+        @pl.when(p > 0)
+        def _():
+            weights.forward(p - 1)
+
+        return carry
+
+    weights.step(0)
+    vectors.forward(0)
+    lax.fori_loop(1, PIECES, turn, 0)
+    weights.forward(PIECES - 1)
+
+    def close(p, carry):
+        weights.arrive(weights.onward(p))
+        weights.finish(p)
+        return carry
+
+    lax.fori_loop(0, PIECES, close, 0)
+    vectors.arrive(vectors.onward(0))
+    vectors.finish(0)
+
+
+def gather_weights(own4, other4, rest, vec):
+    any_ = pl.BlockSpec(memory_space=pl.ANY)
+    return pl.pallas_call(
+        gather_kernel,
+        out_shape=(
+            jax.ShapeDtypeStruct((PIECES, 4, 4) + rest.shape[1:], BF16),
+            jax.ShapeDtypeStruct((4, 4, 2) + vec.shape, BF16),
+        ),
+        in_specs=[any_] * 4,
+        out_specs=(any_, any_),
+        scratch_shapes=[
+            pltpu.SemaphoreType.DMA((3,)),
+            pltpu.SemaphoreType.DMA((2,)),
+            pltpu.SemaphoreType.DMA((2,)),
+            pltpu.SemaphoreType.DMA((PIECES, 7)),
+            pltpu.SemaphoreType.DMA((PIECES, 7)),
+            pltpu.SemaphoreType.DMA((1, 7)),
+            pltpu.SemaphoreType.DMA((1, 7)),
+        ],
+        compiler_params=pltpu.CompilerParams(collective_id=0, has_side_effects=True),
+        name="gather_weights",
+    )(own4, other4, rest, vec)
+
+
+class Reduce:
+    def __init__(self, part, ring1, ring2, line, out, sends, recvs):
+        self.part, self.ring1, self.ring2, self.line, self.out = part, ring1, ring2, line, out
+        self.sends, self.recvs = sends, recvs
+        self.z, self.yx, self.c = place()
+        self.x, self.y, self.d, self.zs = neighbours(self.z, self.yx)
+
+    def copy(self, p, k, src, dst, z, yx):
+        return remote(src, dst, self.sends.at[p, k], self.recvs.at[p, k], (z * 4 + yx, self.c))
+
+    def diagonal(self, p):
+        part, z = self.part.at[p], self.z
+        return [
+            self.copy(p, 0, part.at[0:2, self.d], self.ring1.at[p, 0], z, self.x),
+            self.copy(p, 1, part.at[2:4, self.d], self.ring1.at[p, 1], z, self.y),
+        ]
+
+    def side(self, p):
+        part, z = self.part.at[p], self.z
+        return [
+            self.copy(p, 2, part.at[:, self.x], self.ring2.at[p, 0], z, self.x),
+            self.copy(p, 3, part.at[:, self.y], self.ring2.at[p, 1], z, self.y),
+        ]
+
+    def down(self, p):
+        part = self.part.at[p]
+        return [
+            self.copy(p, 4 + k, part.at[peer, self.yx], self.line.at[p, k], peer, self.yx)
+            for k, peer in enumerate(self.zs)
+        ]
+
+    def start(self, copies):
+        for copy in copies:
+            copy.start()
+
+    def arrive(self, copies):
+        for copy in copies:
+            copy.wait_recv()
+
+    def add(self, p, a, yx, pieces):
+        total = self.part[p, a, yx].astype(F32)
+        for piece in pieces:
+            total = total + piece.astype(F32)
+        return total
+
+    def stage1(self, p):
+        self.start(self.diagonal(p))
+
+    def stage2(self, p):
+        self.arrive(self.diagonal(p))
+        for a in range(2):
+            self.part[p, a, self.y] = self.add(p, a, self.y, [self.ring1[p, 0, a]]).astype(BF16)
+            self.part[p, a + 2, self.x] = self.add(p, a + 2, self.x, [self.ring1[p, 1, a]]).astype(BF16)
+        self.start(self.side(p))
+
+    def stage3(self, p):
+        self.arrive(self.side(p))
+        for a in range(4):
+            self.part[p, a, self.yx] = self.add(
+                p, a, self.yx, [self.ring2[p, 0, a], self.ring2[p, 1, a]]
+            ).astype(BF16)
+        self.start(self.down(p))
+
+    def stage4(self, p):
+        self.arrive(self.down(p))
+        self.out[p] = self.add(p, self.z, self.yx, [self.line[p, k] for k in range(3)])
+
+    def finish(self, p):
+        for copy in self.diagonal(p) + self.side(p) + self.down(p):
+            copy.wait_send()
+
+
+def reduce_kernel(
+    partial, vec, out, recv4, vout, part, ring1, ring2, line, vbuf, local_sem, sends, recvs, vsends, vrecvs, ex_send, ex_recv
+):
+    z, yx, c = place()
+    x, y, d, zs = neighbours(z, yx)
+    enter(z, yx, c)
+    sums = Reduce(part, ring1, ring2, line, out, sends, recvs)
+
+    def local(p):
+        return pltpu.make_async_copy(partial.at[p], part.at[p], local_sem.at[p])
+
+    def vec_copy(k, target):
+        return remote(vout, vbuf.at[k], vsends.at[k], vrecvs.at[k], target)
+
+    vcopies = [
+        [vec_copy(0, (z * 4 + yx, 1 - c))],
+        [vec_copy(1, (z * 4 + x, c))],
+        [vec_copy(2, (z * 4 + y, c))],
+        [vec_copy(3 + k, (peer * 4 + yx, c)) for k, peer in enumerate(zs)],
+    ]
+
+    vout[...] = vec[...]
+
+    def fetch(p, carry):
+        local(p).start()
+        return carry
+
+    lax.fori_loop(0, PIECES, fetch, 0)
+    for copy in vcopies[0]:
+        copy.start()
+
+    def turn(p, carry):
+        @pl.when(p < PIECES)
+        def _():
+            local(p).wait()
+            sums.stage1(p)
+
+        @pl.when((p >= 1) & (p < PIECES + 1))
+        def _():
+            sums.stage2(p - 1)
+
+        @pl.when((p >= 2) & (p < PIECES + 2))
+        def _():
+            sums.stage3(p - 2)
+
+        @pl.when(p >= 3)
+        def _():
+            sums.stage4(p - 3)
+
+        return carry
+
+    lax.fori_loop(0, 4, turn, 0)
+    at = 4
+    for k, copies in enumerate(vcopies):
+        for copy in copies:
+            copy.wait()
+        vout[...] = functools.reduce(
+            lambda a, b: a + b, [vbuf[j] for j in ([k] if k < 3 else [3, 4, 5])], vout[...]
+        )
+        if k + 1 < len(vcopies):
+            for copy in vcopies[k + 1]:
+                copy.start()
+        upto = at + 3 if k + 1 < len(vcopies) else PIECES + 3
+        lax.fori_loop(at, upto, turn, 0)
+        at = upto
+    half = recv4.shape[1]
+    others = pl.ds(pl.multiple_of((1 - c) * half, half), half)
+    swap = remote(out.at[0:4, others], recv4, ex_send, ex_recv, (z * 4 + yx, 1 - c))
+    swap.start()
+
+    def close(p, carry):
+        sums.finish(p)
+        return carry
+
+    lax.fori_loop(0, PIECES, close, 0)
+    swap.wait()
+
+
+def reduce_weights(partial, vec):
+    rows, width = partial.shape[3:]
+    any_ = pl.BlockSpec(memory_space=pl.ANY)
+    vmem = pl.BlockSpec(memory_space=pltpu.VMEM)
+    return pl.pallas_call(
+        reduce_kernel,
+        out_shape=(
+            jax.ShapeDtypeStruct((PIECES, rows, width), F32),
+            jax.ShapeDtypeStruct((4, rows // 2, width), F32),
+            jax.ShapeDtypeStruct(vec.shape, F32),
+        ),
+        in_specs=[any_, vmem],
+        out_specs=(vmem, vmem, vmem),
+        scratch_shapes=[
+            pltpu.VMEM((PIECES, 4, 4, rows, width), BF16),
+            pltpu.VMEM((PIECES, 2, 2, rows, width), BF16),
+            pltpu.VMEM((PIECES, 2, 4, rows, width), BF16),
+            pltpu.VMEM((PIECES, 3, rows, width), BF16),
+            pltpu.VMEM((6,) + vec.shape, F32),
+            pltpu.SemaphoreType.DMA((PIECES,)),
+            pltpu.SemaphoreType.DMA((PIECES, 7)),
+            pltpu.SemaphoreType.DMA((PIECES, 7)),
+            pltpu.SemaphoreType.DMA((6,)),
+            pltpu.SemaphoreType.DMA((6,)),
+            pltpu.SemaphoreType.DMA,
+            pltpu.SemaphoreType.DMA,
+        ],
+        compiler_params=pltpu.CompilerParams(
+            collective_id=1, has_side_effects=True, vmem_limit_bytes=48 * MIB
+        ),
+        name="reduce_weights",
+    )(partial, vec)
+
+
+def spread(column):
+    return jnp.broadcast_to(column[:, None], (column.shape[0], 128)).astype(F32)
+
+
+def resets(keep):
+    length = keep.shape[0]
+    place_in = jnp.arange(length) % 8
+
+    def masks(step, inside):
+        one = step
+        two = one * inside(one, 1)
+        four = two * inside(two, 2)
+        return one, two, four
+
+    def down(v, n):
+        return jnp.concatenate([jnp.zeros_like(v[:n]), v[:-n]])
+
+    def up(v, n):
+        return jnp.concatenate([v[n:], jnp.zeros_like(v[:n])])
+
+    f1, f2, f4 = masks(keep, down)
+    after = up(keep, 1)
+    b1, b2, b4 = masks(after, up)
+    grouped = keep.reshape(-1, 8)
+    fp = jnp.cumprod(grouped, axis=1).reshape(-1)
+    bp = jnp.cumprod(after.reshape(-1, 8)[:, ::-1], axis=1)[:, ::-1].reshape(-1)
+    forward = [
+        keep,
+        jnp.where(place_in >= 1, f1, 0.0),
+        jnp.where(place_in >= 2, f2, 0.0),
+        jnp.where(place_in >= 4, f4, 0.0),
+        fp,
+    ]
+    backward = [
+        after,
+        jnp.where(place_in <= 6, b1, 0.0),
+        jnp.where(place_in <= 5, b2, 0.0),
+        jnp.where(place_in <= 3, b4, 0.0),
+        bp,
+    ]
+    return jnp.stack([spread(m) for m in forward]), jnp.stack([spread(m) for m in backward])
+
+
+def decay_rows(fading, reward):
+    rate = jnp.exp(fading)
+    d = jnp.exp(-rate)
+    steps = jnp.arange(8, dtype=F32)[:, None]
+    rising = jnp.exp(-(steps + 1.0) * rate)
+    falling = jnp.exp(-(8.0 - steps) * rate)
+    zero = jnp.zeros_like(d)
+    head = jnp.stack([d, jnp.exp(-2.0 * rate), jnp.exp(-4.0 * rate), jnp.exp(reward), rate * d, zero, zero, zero])
+    return jnp.concatenate([head, rising, falling])
+
+
+def lanes(j):
+    return slice(j * 128, (j + 1) * 128)
+
+
+def bottom(v):
+    return jnp.broadcast_to(v[7:8], v.shape)
+
+
+def top(v):
+    return jnp.broadcast_to(v[0:1], v.shape)
+
+
+def wkv_forward(k_ref, v_ref, r_ref, masks_ref, rows_ref, mixed_ref, sn_ref, sd_ref):
+    length, width = k_ref.shape
+    tiles = width // 128
+    first = lax.broadcasted_iota(jnp.int32, (8, 128), 0) == 0
+    zero = jnp.zeros((8, 128), F32)
+
+    def pair(g, carry):
+        carry = list(carry)
+        base = pl.multiple_of(g * 16, 16)
+        for j in range(tiles):
+            d1, d2, d4, eu = (rows_ref[n : n + 1, lanes(j)] for n in range(4))
+            dp = rows_ref[8:16, lanes(j)]
+            made = []
+            for h in range(2):
+                at = pl.ds(base + 8 * h, 8)
+                keep, m1, m2, m4, mp = (masks_ref[n, at, :] for n in range(5))
+                ek = jnp.exp(k_ref[at, lanes(j)])
+                v = v_ref[at, lanes(j)]
+                num, den = ek * v, ek
+                x, b = num, eu * ek
+                for n, coef in ((1, m1 * d1), (2, m2 * d2), (4, m4 * d4)):
+                    num = num + coef * pltpu.roll(num, n, 0)
+                    den = den + coef * pltpu.roll(den, n, 0)
+                coef = mp * dp
+                cn, cd = carry[2 * j], carry[2 * j + 1]
+                num = num + coef * cn
+                den = den + coef * cd
+                sn = keep * jnp.where(first, cn, pltpu.roll(num, 1, 0))
+                sd = keep * jnp.where(first, cd, pltpu.roll(den, 1, 0))
+                carry[2 * j], carry[2 * j + 1] = bottom(num), bottom(den)
+                sn_ref[at, lanes(j)] = sn
+                sd_ref[at, lanes(j)] = sd
+                weighted = (sn + eu * x) / (sd + b)
+                made.append(jax.nn.sigmoid(r_ref[at, lanes(j)]) * weighted)
+            mixed_ref[pl.ds(base, 16), lanes(j)] = jnp.concatenate(made, axis=0).astype(BF16)
+        return tuple(carry)
+
+    lax.fori_loop(0, length // 16, pair, (zero,) * (2 * tiles))
+
+
+def wkv_backward(
+    g_ref, k_ref, v_ref, r_ref, sn_ref, sd_ref, masks_ref, rows_ref, gk_ref, gv_ref, gr_ref, sums_ref
+):
+    length, width = k_ref.shape
+    tiles = width // 128
+    last = lax.broadcasted_iota(jnp.int32, (8, 128), 0) == 7
+    zero = jnp.zeros((8, 128), F32)
+    pairs = length // 16
+
+    def pair(step, carry):
+        carry = list(carry)
+        base = pl.multiple_of((pairs - 1 - step) * 16, 16)
+        for j in range(tiles):
+            d1, d2, d4, eu = (rows_ref[n : n + 1, lanes(j)] for n in range(4))
+            dp = rows_ref[16:24, lanes(j)]
+            made = [None, None]
+            for h in (1, 0):
+                at = pl.ds(base + 8 * h, 8)
+                after, m1, m2, m4, mp = (masks_ref[n, at, :] for n in range(5))
+                ek = jnp.exp(k_ref[at, lanes(j)])
+                v = v_ref[at, lanes(j)]
+                sn, sd = sn_ref[at, lanes(j)], sd_ref[at, lanes(j)]
+                s = jax.nn.sigmoid(r_ref[at, lanes(j)])
+                b = eu * ek
+                inverse = 1.0 / (sd + b)
+                weighted = (sn + b * v) * inverse
+                g = g_ref[at, lanes(j)]
+                gs = g * s
+                p = gs * inverse
+                q = -p * weighted
+                gr = gs * weighted * (1.0 - s)
+                hp, hq = p, q
+                for n, coef in ((1, m1 * d1), (2, m2 * d2), (4, m4 * d4)):
+                    hp = hp + coef * pltpu.roll(hp, 8 - n, 0)
+                    hq = hq + coef * pltpu.roll(hq, 8 - n, 0)
+                coef = mp * dp
+                cp, cq = carry[4 * j], carry[4 * j + 1]
+                hp = hp + coef * cp
+                hq = hq + coef * cq
+                ap = after * jnp.where(last, cp, pltpu.roll(hp, 7, 0))
+                aq = after * jnp.where(last, cq, pltpu.roll(hq, 7, 0))
+                carry[4 * j], carry[4 * j + 1] = top(hp), top(hq)
+                bonus = b * (v * p + q)
+                gv = ek * ap + b * p
+                gk = ek * (v * ap + aq) + bonus
+                carry[4 * j + 2] = carry[4 * j + 2] + bonus
+                carry[4 * j + 3] = carry[4 * j + 3] + (ap * sn + aq * sd)
+                made[h] = (gk, gv, gr)
+            both = pl.ds(base, 16)
+            for n, ref in enumerate((gk_ref, gv_ref, gr_ref)):
+                ref[both, lanes(j)] = jnp.concatenate([made[0][n], made[1][n]], axis=0).astype(BF16)
+        return tuple(carry)
+
+    carry = lax.fori_loop(0, pairs, pair, (zero,) * (4 * tiles))
+    for j in range(tiles):
+        rate_d = rows_ref[4:5, lanes(j)]
+        sums_ref[0:1, lanes(j)] = jnp.sum(carry[4 * j + 2], axis=0, keepdims=True)
+        sums_ref[1:2, lanes(j)] = -rate_d * jnp.sum(carry[4 * j + 3], axis=0, keepdims=True)
 
 
 def shifted(value, axis, steps):
@@ -56,14 +570,14 @@
     return lax.fori_loop(0, count, turn, start)
 
 
-def layer_norm(values, scale_vec, shift_vec):
+def wide_layer_norm(values, scale_vec, shift_vec):
     center = values - jnp.mean(values, axis=-1, keepdims=True)
     inverse = lax.rsqrt(jnp.mean(center * center, axis=-1, keepdims=True) + 1e-05)
     normed = center * inverse
     return (normed * scale_vec + shift_vec, normed, inverse)
 
 
-def norm_back(upstream, normed, inverse, scale_vec):
+def wide_norm_back(upstream, normed, inverse, scale_vec):
     scaled = upstream * scale_vec
     inner = (
         scaled
@@ -215,7 +729,7 @@
     return (g_inputs, grad_key, grad_value)
 
 
-def shards(
+def wide_shards(
     incoming_embeddings,
     text_boundary_indicators,
     upstream_sensitivity,
@@ -278,7 +792,7 @@
     )
     persist_indicator = (1 - text_boundary_indicators).astype(jnp.float32)
     inputs = incoming_embeddings.astype(jnp.float32)
-    normed_one, unit_one, inverse_one = layer_norm(
+    normed_one, unit_one, inverse_one = wide_layer_norm(
         inputs, initial_scaling_coords, initial_offset_coords
     )
     prev_one = shift_prev(normed_one, persist_indicator)
@@ -305,7 +819,7 @@
     sig_one = jax.nn.sigmoid(recept_one)
     mixed_att = (sig_one * blended_mean_state).astype(jnp.bfloat16)
     resid_one = inputs + project(mixed_att, emit_coefficients_initial)
-    normed_two, unit_two, inverse_two = layer_norm(
+    normed_two, unit_two, inverse_two = wide_layer_norm(
         resid_one, later_scaling_coords, later_offset_coords
     )
     prev_two = shift_prev(normed_two, persist_indicator)
@@ -350,7 +864,7 @@
     g_normed_two, shares_two = mix_back(
         (g_mix_k2, g_mix_r2), (share_k2, share_r2), differ_two, persist_indicator
     )
-    g_resid_part, grad_gain_two, grad_bias_two = norm_back(
+    g_resid_part, grad_gain_two, grad_bias_two = wide_norm_back(
         g_normed_two, unit_two, inverse_two, later_scaling_coords
     )
     g_resid = upstream + g_resid_part
@@ -394,7 +908,7 @@
         differ_one,
         persist_indicator,
     )
-    g_input_part, grad_gain_one, grad_bias_one = norm_back(
+    g_input_part, grad_gain_one, grad_bias_one = wide_norm_back(
         g_normed_one, unit_one, inverse_one, initial_scaling_coords
     )
     grad_tokens = g_resid + g_input_part
@@ -440,50 +954,214 @@
     )
 
 
+def local_call(body, outs, name, *args):
+    vmem = pl.BlockSpec(memory_space=pltpu.VMEM)
+    return pl.pallas_call(
+        body,
+        out_shape=outs,
+        in_specs=[vmem] * len(args),
+        out_specs=tuple([vmem] * len(outs)),
+        compiler_params=pltpu.CompilerParams(vmem_limit_bytes=48 * MIB),
+        name=name,
+    )(*args)
+
+
+def split_columns(w, parts):
+    rows, width = w.shape
+    return w.reshape(rows, parts, 2, width // (2 * parts)).transpose(2, 0, 1, 3).reshape(2, rows, width // 2)
+
+
+def join_columns(own, other, c, parts):
+    rows, half = own.shape[-2:]
+    a = jnp.where(c == 0, own, other).reshape(own.shape[:-1] + (parts, half // parts))
+    b = jnp.where(c == 0, other, own).reshape(own.shape[:-1] + (parts, half // parts))
+    return jnp.stack([a, b], axis=-2).reshape(own.shape[:-1] + (2 * half,))
+
+
+def pair_row(a, axis):
+    return lax.all_gather(a, "tensor", axis=axis, tiled=True)
+
+
+def pair_sum(a):
+    return lax.psum(a.astype(BF16), "tensor").astype(F32)
+
+
+def dot(a, b, dims, out=F32):
+    return lax.dot_general(a, b, (dims, ((), ())), preferred_element_type=out)
+
+
+NN, NT, TN = ((1,), (0,)), ((1,), (1,)), ((0,), (0,))
+
+
+def layer_norm(values, gain, bias):
+    center = values - jnp.mean(values, axis=-1, keepdims=True)
+    inverse = lax.rsqrt(jnp.mean(center * center, axis=-1, keepdims=True) + 1e-05)
+    normed = center * inverse
+    return normed * gain + bias, normed, inverse
+
+
+def norm_back(g, normed, inverse, gain):
+    q = g * gain
+    return inverse * (
+        q - jnp.mean(q, axis=-1, keepdims=True) - normed * jnp.mean(q * normed, axis=-1, keepdims=True)
+    )
+
+
+def shift_down(v, keep):
+    return jnp.concatenate([jnp.zeros_like(v[:1]), v[:-1]]) * keep[:, None]
+
+
+def shift_up(v, keep):
+    v = v * keep[:, None]
+    return jnp.concatenate([v[1:], jnp.zeros_like(v[:1])])
+
+
+VECTORS = 11
+
+
+def shards(
+    tokens, starts, upstream, gain1, bias1, gain2, bias2, fading, reward,
+    mk1, mv1, mr1, wk, wv, wr, wo, mk2, mr2, wg, fk, fv,
+):
+    c = lax.axis_index("tensor")
+    i = lax.axis_index("dp")
+    count = lax.axis_size("dp")
+    own_rows, width = wk.shape
+    half = width // 2
+    hidden = fk.shape[1]
+    block = width // (2 * count)
+
+    by_core = jnp.stack([split_columns(wk, count), split_columns(wv, count), split_columns(wr, count), split_columns(wg, 1)])
+    own4 = lax.dynamic_index_in_dim(by_core, c, 1, False)
+    other4 = lax.dynamic_index_in_dim(by_core, 1 - c, 1, False)
+    emit = wo.reshape(own_rows, 2, half).transpose(1, 0, 2).reshape(1, 2 * own_rows, half)
+    key4 = fk.reshape(2 * own_rows, 4, hidden // 4).transpose(1, 0, 2)
+    value4 = fv.reshape(4, hidden // 4, 2 * own_rows).transpose(0, 2, 1)
+    rest = jnp.concatenate([emit, key4, value4])
+    vectors = jnp.stack([gain1, bias1, gain2, bias2, fading, reward, mk1, mv1, mr1, mk2, mr2])
+    vectors = jnp.pad(vectors, ((0, 16 - VECTORS), (0, 0)))
+    slot = (2 * i + c) % (128 // own_rows)
+    lane = jnp.arange(128) // own_rows
+    vec = jnp.where(lane[None, :] == slot, jnp.tile(vectors, (1, 128 // own_rows)), 0).astype(BF16)
+
+    g, gv = gather_weights(own4, other4, rest, vec)
+
+    full = gv.reshape(count * 2 * own_rows // 128, 128 // own_rows, 16, 128).astype(F32).sum(1)
+    full = full.transpose(1, 0, 2).reshape(16, width)
+    gain1, bias1, gain2, bias2, fading, reward, mk1, mv1, mr1, mk2, mr2 = (full[n] for n in range(VECTORS))
+    g = g.reshape((PIECES, count, 2 * own_rows, half))
+    wk, wv, wr, wg = (g[n].reshape(width, half) for n in range(4))
+    wo = g[4].reshape(count, 2, own_rows, half).transpose(0, 2, 1, 3).reshape(half, width)
+    fk = jnp.concatenate([g[5 + n].reshape(width, hidden // 4) for n in range(4)], axis=1)
+    fv = jnp.concatenate([g[9 + n].reshape(width, hidden // 4) for n in range(4)], axis=1)
+
+    def own_channels(v):
+        return lax.dynamic_index_in_dim(split_columns(v[None], count)[:, 0], c, 0, False)
+
+    keep = pair_row((1 - starts[0]).astype(F32), 0)
+    x = pair_row(tokens[0], 0).astype(F32)
+    up_half = lax.dynamic_slice_in_dim(pair_row(upstream[0], 0), c * half, half, 1).astype(F32)
+    n1, u1, i1 = layer_norm(x, gain1, bias1)
+    p1 = shift_down(n1, keep)
+    d1 = n1 - p1
+    in_k, in_v, in_r = ((p1 + d1 * m).astype(BF16) for m in (mk1, mv1, mr1))
+    k, v, r = dot(in_k, wk, NN), dot(in_v, wv, NN), dot(in_r, wr, NN)
+    fmask, bmask = resets(keep)
+    rows = decay_rows(own_channels(fading), own_channels(reward))
+    shape = jax.ShapeDtypeStruct(k.shape, F32)
+    low = jax.ShapeDtypeStruct(k.shape, BF16)
+    mixed, sn, sd = local_call(wkv_forward, (low, shape, shape), "wkv_forward", k, v, r, fmask, rows)
+    resid = x + pair_sum(dot(mixed, wo, NN))
+    n2, u2, i2 = layer_norm(resid, gain2, bias2)
+    p2 = shift_down(n2, keep)
+    d2 = n2 - p2
+    in_k2, in_r2 = ((p2 + d2 * m).astype(BF16) for m in (mk2, mr2))
+    s2 = jax.nn.sigmoid(dot(in_r2, wg, NN))
+    pre = jax.nn.relu(dot(in_k2, fk, NN))
+    act = (pre * pre).astype(BF16)
+    value = lax.psum_scatter(dot(act, fv, NT).astype(BF16), "tensor", scatter_dimension=1, tiled=True).astype(F32)
+    resid_half = lax.dynamic_slice_in_dim(resid, c * half, half, 1)
+    out_half = (resid_half + s2 * value).astype(BF16)
+    layer_out = lax.all_to_all(out_half, "tensor", 0, 1, tiled=True)
+    g_value = (up_half * s2).astype(BF16)
+    g_recept2 = (up_half * value * s2 * (1.0 - s2)).astype(BF16)
+    g_value = pair_row(g_value, 1)
+    grad_fv = dot(g_value, act, TN)
+    g_pre = (2.0 * pre * dot(g_value, fv, NN)).astype(BF16)
+    grad_fk = dot(in_k2, g_pre, TN)
+    grad_wg = dot(in_r2, g_recept2, TN)
+    gk2 = dot(g_pre, fk, NT)
+    gr2 = dot(g_recept2, wg, NT)
+    grad_mk2, grad_mr2 = jnp.sum(gk2 * d2, 0), jnp.sum(gr2 * d2, 0)
+    gn2 = gk2 * mk2 + gr2 * mr2 + shift_up(gk2 * (1 - mk2) + gr2 * (1 - mr2), keep)
+    grad_gain2, grad_bias2 = jnp.sum(gn2 * u2, 0), jnp.sum(gn2, 0)
+    upstream_row = pair_row(upstream[0], 0).astype(F32)
+    g_resid = upstream_row + norm_back(pair_sum(gn2), u2, i2, gain2)
+    g_branch = g_resid.astype(BF16)
+    grad_wo = dot(mixed, g_branch, TN)
+    g_mixed = dot(g_branch, wo, NT)
+    gk1, gv1, gr1, wsums = local_call(
+        wkv_backward, (low, low, low, jax.ShapeDtypeStruct((8, half), F32)), "wkv_backward",
+        g_mixed, k, v, r, sn, sd, bmask, rows,
+    )
+    grad_wk, grad_wv, grad_wr = dot(in_k, gk1, TN), dot(in_v, gv1, TN), dot(in_r, gr1, TN)
+    toward, behind, grad_mix = 0.0, 0.0, []
+    for grad, w, m in ((gk1, wk, mk1), (gv1, wv, mv1), (gr1, wr, mr1)):
+        back = dot(grad, w, NT)
+        toward = toward + back * m
+        behind = behind + back * (1 - m)
+        grad_mix.append(jnp.sum(back * d1, 0))
+    gn1 = toward + shift_up(behind, keep)
+    grad_gain1, grad_bias1 = jnp.sum(gn1 * u1, 0), jnp.sum(gn1, 0)
+    gn1 = lax.psum_scatter(gn1.astype(BF16), "tensor", scatter_dimension=0, tiled=True).astype(F32)
+    span = tokens.shape[1]
+
+    def mine(v):
+        return lax.dynamic_slice_in_dim(v, c * span, span, 0)
+
+    grad_tokens = mine(g_resid) + norm_back(gn1, mine(u1), mine(i1), gain1)
+
+    blocks = (4, 4) if count == 16 else (count,)
+
+    def pieces(m):
+        return m.reshape((1,) + blocks + (2 * own_rows, half))
+
+    grad_wo = grad_wo.reshape(count, own_rows, 2, half).transpose(0, 2, 1, 3)
+    grad_fk, grad_fv = (
+        m.reshape(width, 4, hidden // 4).transpose(1, 0, 2).reshape((4,) + blocks + (2 * own_rows, half))
+        for m in (grad_fk, grad_fv)
+    )
+    partial = jnp.concatenate(
+        [pieces(grad_wk), pieces(grad_wv), pieces(grad_wr), pieces(grad_wg), pieces(grad_wo), grad_fk, grad_fv]
+    ).astype(BF16)
+
+    def all_channels(v):
+        z = jnp.zeros_like(v)
+        return join_columns(jnp.where(c == 0, v, z)[None], jnp.where(c == 1, v, z)[None], 0, count)[0]
+
+    vsums = jnp.stack([
+        grad_gain1, grad_bias1, grad_gain2, grad_bias2, all_channels(wsums[1]), all_channels(wsums[0]),
+        *grad_mix, grad_mk2, grad_mr2,
+    ])
+    vsums = jnp.pad(vsums, ((0, 16 - VECTORS), (0, 0)))
+    total, recv4, vtotal = reduce_weights(partial, vsums)
+    vtotal = lax.dynamic_slice_in_dim(vtotal, (2 * i + c) * own_rows, own_rows, 1)
+    own = lax.dynamic_slice_in_dim(total[:4], c * own_rows, own_rows, 1)
+    out_k, out_v, out_r = (join_columns(own[n], recv4[n], c, count) for n in range(3))
+    out_g = join_columns(own[3], recv4[3], c, 1)
+    out_o = total[4].reshape(2, own_rows, half).transpose(1, 0, 2).reshape(own_rows, width)
+    out_fk = total[5:9].transpose(1, 0, 2).reshape(2 * own_rows, hidden)
+    out_fv = total[9:13].transpose(0, 2, 1).reshape(hidden, 2 * own_rows)
+    return (
+        layer_out[None], grad_tokens[None], *(vtotal[n] for n in range(9)),
+        out_k, out_v, out_r, out_o, vtotal[9], vtotal[10], out_g, out_fk, out_fv,
+    )
+
+
 def solution(mesh):
-    in_specs = (
-        P("dp", "tensor", None),
-        P("dp", "tensor"),
-        P("dp", "tensor", None),
-        P(("dp", "tensor")),
-        P(("dp", "tensor")),
-        P(("dp", "tensor")),
-        P(("dp", "tensor")),
-        P(("dp", "tensor")),
-        P(("dp", "tensor")),
-        P(("dp", "tensor")),
-        P(("dp", "tensor")),
-        P(("dp", "tensor")),
-        P(("dp", "tensor"), None),
-        P(("dp", "tensor"), None),
-        P(("dp", "tensor"), None),
-        P(("dp", "tensor"), None),
-        P(("dp", "tensor")),
-        P(("dp", "tensor")),
-        P(("dp", "tensor"), None),
-        P("dp", "tensor"),
-        P("tensor", "dp"),
-    )
-    out_specs = (
-        P("dp", "tensor", None),
-        P("dp", "tensor", None),
-        P(("dp", "tensor")),
-        P(("dp", "tensor")),
-        P(("dp", "tensor")),
-        P(("dp", "tensor")),
-        P(("dp", "tensor")),
-        P(("dp", "tensor")),
-        P(("dp", "tensor")),
-        P(("dp", "tensor")),
-        P(("dp", "tensor")),
-        P(("dp", "tensor"), None),
-        P(("dp", "tensor"), None),
-        P(("dp", "tensor"), None),
-        P(("dp", "tensor"), None),
-        P(("dp", "tensor")),
-        P(("dp", "tensor")),
-        P(("dp", "tensor"), None),
-        P("dp", "tensor"),
-        P("tensor", "dp"),
-    )
-    return jax.shard_map(shards, mesh=mesh, in_specs=in_specs, out_specs=out_specs, check_vma=False)
+    row, vector, matrix = P("dp", "tensor", None), P(("dp", "tensor")), P(("dp", "tensor"), None)
+    key, value = P("dp", "tensor"), P("tensor", "dp")
+    in_specs = (row, P("dp", "tensor"), row) + (vector,) * 9 + (matrix,) * 4 + (vector,) * 2 + (matrix, key, value)
+    out_specs = (row, row) + (vector,) * 9 + (matrix,) * 4 + (vector,) * 2 + (matrix, key, value)
+    body = shards if (mesh.shape["dp"], mesh.shape["tensor"]) == (16, 2) else wide_shards
+    return jax.shard_map(body, mesh=mesh, in_specs=in_specs, out_specs=out_specs, check_vma=False)

time: 1490 us -> 593 us (0.40)
  waiting for transfers between devices: 615 us -> 37.4 us
  Pallas kernels: 0 us -> 296 us
  other arithmetic: 291 us -> 63.6 us
  matrix products: 282 us -> 81.1 us
  blocking collectives: 94.6 us -> 6.62 us
  local copies, waits for them, and re-layouts: 143 us -> 80.8 us
  loops' own time: 22.8 us -> 0 us
    reduce_scatter x9 -> x2, waiting for transfers between devices: 353 us -> 10.8 us  [the longest x1 10.8 us: shards(): lax.psum_scatter(dot(act, fv, NT).astype(BF16), 'tensor', scatter_dimensi...]
    pallas_call x0 -> x4, Pallas kernels: none -> 296 us  [the longest x1 150 us: gather_weights(): pl.pallas_call(gather_kernel, out_shape=(jax.ShapeDtypeStruct((PIECES, 4,...]
    all_gather x9 -> x3, waiting for transfers between devices: 258 us -> 0.6 us  [pair_row(): return lax.all_gather(a, 'tensor', axis=axis, tiled=True)]
    dot_general x117 -> x21, matrix products: 282 us -> 81.1 us  [dot(): return lax.dot_general(a, b, (dims, ((), ())), preferred_element_type=out)]
    dynamic_update_slice x96 -> x0, other arithmetic: 94.2 us -> none  [scan_fragments(): lax.scan(advance, (initial, initial), (split_blocks(lookup_wide), split_b...]
    unnamed x2 -> x0, blocking collectives: 84.9 us -> none
    reduce_sum x69 -> x5, other arithmetic: 82.4 us -> 18.9 us  [the longest x1 10.7 us: shards(): grad_gain1, grad_bias1 = (jnp.sum(gn1 * u1, 0), jnp.sum(gn1, 0))]
    add_any x48 -> x0, other arithmetic: 62.4 us -> none  [the longest x16 22.2 us: advance(): accrued_divisor_sum[:, None, :]]
  transfers between devices with their start and end apart: 22 -> 7, of which waited for: 11 -> 4; matrix products, arithmetic and copies ran while one was open for 46% -> 20% of each run, Pallas kernels for 0% -> 48%
where the time goes in v1:
time: 593 us; the launch traced here: 582 us
  Pallas kernels  296 us (50%)
  matrix products  81.1 us (14%)
  local copies, waits for them, and re-layouts  80.8 us (14%)
  other arithmetic  63.6 us (11%)
  waiting for transfers between devices  37.4 us (6%)
  between operations  15.7 us (3%)
  blocking collectives  6.62 us (1%)
    pallas_call x1, Pallas kernels, gather_weights(): pl.pallas_call(gather_kernel, out_shape=(jax.ShapeDtypeStruct((PIECES, 4,...  150 us
    pallas_call x1, Pallas kernels, reduce_weights(): pl.pallas_call(reduce_kernel, out_shape=(jax.ShapeDtypeStruct((PIECES, ro...  127 us
    dot_general x21, matrix products, dot(): return lax.dot_general(a, b, (dims, ((), ())), preferred_element_type=out)  81.1 us
    unnamed x139, local copies, waits for them, and re-layouts  34.1 us
    psum x2, waiting for transfers between devices, pair_sum(): return lax.psum(a.astype(BF16), 'tensor').astype(F32)  24.5 us
    pallas_call x2, Pallas kernels, local_call(): pl.pallas_call(body, out_shape=outs, in_specs=[vmem] * len(args), out_spe...  19.1 us
  transfers between devices with their start and end apart: 7, of which 4 were waited for; matrix products, arithmetic and copies ran while one was open for 20% of the time, Pallas kernels for 48%

profile of v1, /device:TPU:0, one launch (start us, length us, event | category | flops | bytes accessed | tf_op | source)
XLA Modules:
  0.0 582.4 jit_solution(12657198318593452440)
XLA Ops:
  8.7 1.9 all-gather.1
  20.7 150.3 %gather_weights.1 = (bf16[13,4,4,64,512]{4,3,2,1,0:T(8,128)(2,1)}, bf16[4,4,2,16,128]{4,3,2,1,0:T(8,128)(2,1)}) custom-call(bf16[4,32,512]{2,1,0:T(8,128)(2,1)} %get-tuple-element.113.own4, bf16[4,32,512]{2,1,0:T(8,128)(2,1)} %get-tuple-element.112.other4, bf16[9,64,512]{2,1,0:T(8,128)(2,1)} %pad_maximum_fusion.6.rest, ...), custom_call_target="tpu_custom_call" | custom-call | tf_op jit(solution)/shard_map/gather_weights/pallas_call | solution.py:149
  172.4 9.8 %fusion.59 = (bf16[1,4,4,64,512]{4,3,2,1,0:T(8,128)(2,1)}, bf16[1,4,4,64,512]{4,3,2,1,0:T(8,128)(2,1)}, bf16[1,4,4,64,512]{4,3,2,1,0:T(8,128)(2,1)}, bf16[1,4,4,...) fusion(bf16[13,4,4,64,512]{4,3,2,1,0:T(8,128)(2,1)} %get-tuple-, ...), kind=kLoop, calls=%fused_computation.203 | loop fusion | bytes 27262976 | tf_op jit(solution)/shard_map/slice | solution.py:1056
  189.0 2.1 convert_reduce_fusion
  191.1 2.3 fusion.4
  193.4 2.8 fusion.2
  196.2 6.3 %add_convert_fusion.2 = (bf16[1024,1024]{1,0:T(8,128)(2,1)S(1)}, bf16[1024,1024]{1,0:T(8,128)(2,1)S(1)}, bf16[1024,1024]{1,0:T(8,128)(2,1)S(1)}) fusion(f32[1023,1024]{1,0:T(8,128)S(1)} %bitcast.257, f32[1024]{0:T(1024)S(1)} %bitcast.327, f32[1024]{0:T(1024)S(1)} %bitcast.308, f32[1024]{0:T(1024)S(1)} %bitcast.325, f32[1024]{0:T(1024)S(1)} %bitcast.318, ...), kind=kLoop, calls=%fused_computation.41 | loop fusion | flops 16777216 | bytes 12611584 | tf_op jit(solution)/shard_map/convert_element_type | solution.py:1067
  202.6 3.0 fusion.64.r_ref
  205.6 2.6 fusion.63.v_ref
  208.3 2.6 fusion.62.k_ref
  210.8 8.1 %wkv_forward.1 = (bf16[1024,512]{1,0:T(8,128)(2,1)S(1)}, f32[1024,512]{1,0:T(8,128)S(1)}, f32[1024,512]{1,0:T(8,128)S(1)}) custom-call(f32[1024,512]{1,0:T(8,128)} %fusion.62.k_ref, f32[1024,512]{1,0:T(8,128)} %fusion.63.v_ref, f32[1024,512]{1,0:T(8,128)} %fusion.64.r_ref, f32[5,1024,128]{2,1,0:T(8,128)} %copy-done.26, f32[24,512]{1,0:T(8,128)S(1)} %concatenate.51.rows_ref), custom_call_target="tpu_custom_call" | custom-call | tf_op jit(solution)/shard_map/wkv_forward/pallas_call | solution.py:959
  221.6 2.6 convolution_convert_fusion.3
  225.2 21.4 %all-reduce.11.cloned.1.call-done = bf16[1024,1024]{1,0:T(8,128)(2,1)} async-done(((bf16[1024,1024]{1,0:T(8,128)(2,1)}), bf16[1024,1024]{1,0:T(8,128)(2,1)}) %all-reduce.11.cloned.1.call-update) | async-done | bytes 2097168 | tf_op jit(solution)/shard_map/psum | solution.py:986
  246.6 2.4 fusion.54
  250.9 2.9 add_convert_fusion
  256.1 4.5 fusion.24
  260.6 3.2 copy-done.58
  263.8 5.8 convolution_convert_fusion.2
  269.7 10.8 %reduce-scatter.3.cloned.1.call-done = bf16[1024,512]{1,0:T(8,128)(2,1)} async-done(((bf16[1024,1024]{1,0:T(8,128)(2,1)}), bf16[1024,512]{1,0:T(8,128)(2,1)}) %reduce-scatter.3.cloned.1.call-update) | async-done | bytes 1048592 | tf_op jit(solution)/shard_map/reduce_scatter | solution.py:1082
  280.5 6.5 %fusion.15 = (bf16[1024,512]{1,0:T(8,128)(2,1)}, bf16[1024,512]{1,0:T(8,128)(2,1)}, f32[1024,512]{1,0:T(8,128)}) fusion(bf16[1,1024,1024]{2,1,0:T(8,128)(2,1)} %all-gather.11.cloned.1.call-done, s32[]{:T(128)S(6)} %select_n.275, bf16[1024,512]{1,0:T(8,128)(2,1)} %reduce-scatter.3.cloned.1.call-done, bf16[1024,1024]{1,0:T(8,128)(2,1)} %get-tuple-element.91, ...), kind=kOutput, calls=%fused_computation.56 | convolution fusion | flops 1080033280 | bytes 9437188 | tf_op jit(solution)/shard_map/dot_general | solution.py:990
  293.3 5.1 fusion.65
  299.0 11.9 %multiply_convert_fusion = bf16[1024,2048]{1,0:T(8,128)(2,1)} fusion(f32[1024,2048]{1,0:T(8,128)} %copy-done.58, bf16[1024,1024]{1,0:T(8,128)(2,1)} %all-gather.7.cloned.1.call-done, bf16[1024,512]{1,0:T(8,128)(2,1)} %bitcast.293, bf16[1024,512]{1,0:T(8,128)(2,1)} %bitcast.295, bf16[1024,512]{1,0:T(8,128)(2,1)} %bitcast.297, bf16[1024,512]{1,0:T(8,128)(2,1)} %bitcast.291), kind=kOutput, calls=%fused_computation | convolution fusion | flops 4320133120 | bytes 18874368 | tf_op jit(solution)/shard_map/dot_general | solution.py:990
  311.0 6.9 %fusion.23 = f32[1024,1024]{1,0:T(8,128)S(1)} fusion(bf16[1024,2048]{1,0:T(8,128)(2,1)} %multiply_convert_fusion, bf16[1024,512]{1,0:T(8,128)(2,1)S(1)} %bitcast.284, bf16[1024,512]{1,0:T(8,128)(2,1)S(1)} %bitcast.286, bf16[1024,512]{1,0:T(8,128)(2,1)S(1)} %bitcast.288, bf16[1024,512]{1,0:T(8,128)(2,1)S(1)} %bitcast.290), kind=kOutput, calls=%fused_computation.75 | convolution fusion | flops 4311744512 | bytes 12582912 | tf_op jit(solution)/shard_map/dot_general | solution.py:990
  319.8 4.2 fusion.57
  324.1 4.3 convolution_convert_fusion.5
  328.5 5.1 convolution_convert_fusion.1
  333.7 2.4 copy.125
  336.1 5.0 convolution_convert_fusion
  341.1 2.4 copy.124
  343.5 3.1 all-reduce.13.cloned.1.call-done
  346.6 4.8 multiply_reduce_fusion.5
  352.0 3.2 convert_add_fusion
  357.1 11.0 %wkv_backward.1 = (bf16[1024,512]{1,0:T(8,128)(2,1)S(1)}, bf16[1024,512]{1,0:T(8,128)(2,1)S(1)}, bf16[1024,512]{1,0:T(8,128)(2,1)S(1)}, f32[8,512]{1,0:T(8,128)S(1)}) custom-call(f32[1024,512]{1,0:T(8,128)S(1)} %fusion.21.g_ref, f32[1024,512]{1,0:T(8,128)} %fusion.62.k_ref, f32[1024,512]{1,0:T(8,128)} %fusion.63.v_ref, f32[1024,512]{1,0:T(8,128)} %fusion.64.r_ref, ...), custom_call_target="tpu_custom_call" | custom-call | tf_op jit(solution)/shard_map/wkv_backward/pallas_call | solution.py:959
  373.1 2.1 copy-done.19
  375.2 3.8 fusion.6
  382.3 10.7 %fusion.55 = (f32[1024]{0:T(1024)S(1)}, f32[1024]{0:T(1024)S(1)}, f32[1024]{0:T(1024)S(1)}, f32[1024]{0:T(1024)S(1)}, f32[1024]{0:T(1024)S(1)}, /*index=5*/f32[1...) fusion(f32[1024]{0:T(1024)S(1)} %add_rsqrt_fusion.1, f32[1024]{0:T(1024)S(1)} %broadcast_multiply_fusion.3, ...), kind=kLoop, calls=%fused_computation.201 | loop fusion | flops 30401536 | bytes 41992192 | tf_op jit(solution)/shard_map/reduce_sum | solution.py:1115
  393.0 4.4 convolution_convert_fusion.4
  397.4 1.8 reshape.545
  400.5 3.3 fusion.14
  403.8 4.7 all_to_all.16
  408.5 2.1 copy.93
  410.6 2.6 broadcast_in_dim.28
  413.9 3.0 convolution_convert_fusion.8
  424.9 2.6 constant_dynamic-update-slice_fusion.1
  428.6 2.6 constant_dynamic-update-slice_fusion.partial
  431.2 127.0 %reduce_weights.1 = (f32[13,64,512]{2,1,0:T(8,128)S(1)}, f32[4,32,512]{2,1,0:T(8,128)S(1)}, f32[16,1024]{1,0:T(8,128)S(1)}) custom-call(bf16[13,4,4,64,512]{4,3,2,1,0:T(8,128)(2,1)} %constant_dynamic-update-slice_fusion.partial, f32[16,1024]{1,0:T(8,128)S(1)} %pad.15.vec), custom_call_target="tpu_custom_call" | custom-call | tf_op jit(solution)/shard_map/reduce_weights/pallas_call | solution.py:325
  568.3 2.4 fusion.19
  570.7 4.4 add_bitcast_fusion
  (274 shorter events, 67.8 us)
Async XLA Ops:
  7.2 11.8 %copy-start.54 = (bf16[2048,64]{0,1:T(8,128)(2,1)S(1)}, bf16[2048,64]{0,1:T(8,128)(2,1)}, u32[]{:S(2)}) copy-start(bf16[2048,64]{0,1:T(8,128)(2,1)} %param.41) | copy-start | bytes 786436
  7.2 11.7 %copy-start.55 = (bf16[64,2048]{1,0:T(8,128)(2,1)S(1)}, bf16[64,2048]{1,0:T(8,128)(2,1)}, u32[]{:S(2)}) copy-start(bf16[64,2048]{1,0:T(8,128)(2,1)} %param.40) | copy-start | bytes 786436
  7.2 181.8 %all-gather.9.cloned.1.call-start = ((), (), s32[]{:S(2)}) async-start(), calls=%async_computation.8 | async-start | bytes 3145728 | tf_op jit(solution)/shard_map/all_gather | solution.py:982
  7.9 238.6 %all-reduce.11.cloned.1.call-start = ((), (), s32[]{:S(2)}) async-start(), calls=%async_computation.3 | async-start | bytes 4194304 | tf_op jit(solution)/shard_map/psum | solution.py:986
  189.0 4.4 copy-start.4
  196.2 6.3 %copy-start.10 = (f32[1024,1024]{1,0:T(8,128)}, f32[1024,1024]{1,0:T(8,128)S(1)}, u32[]{:S(2)}) copy-start(f32[1024,1024]{1,0:T(8,128)S(1)} %get-tuple-element.100) | copy-start | bytes 12582916
  196.2 6.3 %copy-start.36 = (bf16[1,4,4,64,512]{4,3,2,1,0:T(8,128)(2,1)S(1)}, bf16[1,4,4,64,512]{4,3,2,1,0:T(8,128)(2,1)}, u32[]{:S(2)}) copy-start(bf16[1,4,4,64,512]{4,3,2,1,0:T(8,128)(2,1)} %get-tuple-element.87) | copy-start | bytes 3145732
  202.6 5.7 copy-start.33
  210.8 10.8 %copy-start.23 = (bf16[64,8,2,512]{3,1,2,0:T(8,128)(2,1)S(1)}, bf16[64,8,2,512]{3,1,2,0:T(8,128)(2,1)}, u32[]{:S(2)}) copy-start(bf16[64,8,2,512]{3,1,2,0:T(8,128)(2,1)} %copy.116) | copy-start | bytes 3145732
  224.2 45.5 %all-gather.11.cloned.1.call-start = ((), (), s32[]{:S(2)}) async-start(), calls=%async_computation.9 | async-start | bytes 3145728 | tf_op jit(solution)/shard_map/all_gather | solution.py:982
  224.9 55.6 %reduce-scatter.3.cloned.1.call-start = ((), (), s32[]{:S(2)}) async-start(), calls=%async_computation.4 | async-start | bytes 3145728 | tf_op jit(solution)/shard_map/reduce_scatter | solution.py:1082
  250.9 3.1 copy-start.6
  250.9 4.1 copy-start.46
  250.9 5.1 copy-start.48
  254.0 6.6 %copy-start.27 = (bf16[1024,1024]{1,0:T(8,128)(2,1)}, bf16[1024,1024]{1,0:T(8,128)(2,1)S(1)}, u32[]{:S(2)}) copy-start(bf16[1024,1024]{1,0:T(8,128)(2,1)S(1)} %get-tuple-element.90) | copy-start | bytes 6291460
  256.0 7.7 %copy-start.50 = (bf16[1,4,4,64,512]{4,3,2,1,0:T(8,128)(2,1)S(1)}, bf16[1,4,4,64,512]{4,3,2,1,0:T(8,128)(2,1)}, u32[]{:S(2)}) copy-start(bf16[1,4,4,64,512]{4,3,2,1,0:T(8,128)(2,1)} %get-tuple-element.77) | copy-start | bytes 3145732
  256.0 7.7 %copy-start.51 = (bf16[1,4,4,64,512]{4,3,2,1,0:T(8,128)(2,1)S(1)}, bf16[1,4,4,64,512]{4,3,2,1,0:T(8,128)(2,1)}, u32[]{:S(2)}) copy-start(bf16[1,4,4,64,512]{4,3,2,1,0:T(8,128)(2,1)} %get-tuple-element.78) | copy-start | bytes 3145732
  256.1 7.7 %copy-start.52 = (bf16[1,4,4,64,512]{4,3,2,1,0:T(8,128)(2,1)S(1)}, bf16[1,4,4,64,512]{4,3,2,1,0:T(8,128)(2,1)}, u32[]{:S(2)}) copy-start(bf16[1,4,4,64,512]{4,3,2,1,0:T(8,128)(2,1)} %get-tuple-element.79) | copy-start | bytes 3145732
  256.1 7.7 %copy-start.53 = (bf16[1,4,4,64,512]{4,3,2,1,0:T(8,128)(2,1)S(1)}, bf16[1,4,4,64,512]{4,3,2,1,0:T(8,128)(2,1)}, u32[]{:S(2)}) copy-start(bf16[1,4,4,64,512]{4,3,2,1,0:T(8,128)(2,1)} %get-tuple-element.80) | copy-start | bytes 3145732
  260.6 3.2 copy-start.58
  269.6 29.4 %all-gather.7.cloned.1.call-start = ((), (), s32[]{:S(2)}) async-start(), calls=%async_computation.5 | async-start | bytes 3145728 | tf_op jit(solution)/shard_map/all_gather | solution.py:982
  287.1 59.6 %all-reduce.13.cloned.1.call-start = ((), (), s32[]{:S(2)}) async-start(), calls=%async_computation.6 | async-start | bytes 4194304 | tf_op jit(solution)/shard_map/psum | solution.py:986
  299.0 11.9 %copy-start.43 = (bf16[1,4,4,64,512]{4,3,2,1,0:T(8,128)(2,1)S(1)}, bf16[1,4,4,64,512]{4,3,2,1,0:T(8,128)(2,1)}, u32[]{:S(2)}) copy-start(bf16[1,4,4,64,512]{4,3,2,1,0:T(8,128)(2,1)} %get-tuple-element.81) | copy-start | bytes 3145732
  299.0 11.9 %copy-start.45 = (bf16[1,4,4,64,512]{4,3,2,1,0:T(8,128)(2,1)S(1)}, bf16[1,4,4,64,512]{4,3,2,1,0:T(8,128)(2,1)}, u32[]{:S(2)}) copy-start(bf16[1,4,4,64,512]{4,3,2,1,0:T(8,128)(2,1)} %get-tuple-element.82) | copy-start | bytes 3145732
  299.0 11.9 %copy-start.47 = (bf16[1,4,4,64,512]{4,3,2,1,0:T(8,128)(2,1)S(1)}, bf16[1,4,4,64,512]{4,3,2,1,0:T(8,128)(2,1)}, u32[]{:S(2)}) copy-start(bf16[1,4,4,64,512]{4,3,2,1,0:T(8,128)(2,1)} %get-tuple-element.83) | copy-start | bytes 3145732
  299.0 11.9 %copy-start.49 = (bf16[1,4,4,64,512]{4,3,2,1,0:T(8,128)(2,1)S(1)}, bf16[1,4,4,64,512]{4,3,2,1,0:T(8,128)(2,1)}, u32[]{:S(2)}) copy-start(bf16[1,4,4,64,512]{4,3,2,1,0:T(8,128)(2,1)} %get-tuple-element.84) | copy-start | bytes 3145732
  310.9 6.9 %copy-start.12 = (f32[1024,1024]{1,0:T(8,128)S(1)}, f32[1024,1024]{1,0:T(8,128)}, u32[]{:S(2)}) copy-start(f32[1024,1024]{1,0:T(8,128)} %fusion.65) | copy-start | bytes 12582916
  324.1 244.2 %reduce-scatter.5.cloned.1.call-start = ((), (), s32[]{:S(2)}) async-start(), calls=%async_computation.7 | async-start | bytes 3145728 | tf_op jit(solution)/shard_map/reduce_scatter | solution.py:1116
  324.1 4.4 copy-start.28
  324.1 4.4 copy-start.57
  324.1 11.9 %slice-start = ((s8[8388608]{0:T(1024)(128)(4,1)}), s8[4194304]{0:T(1024)(128)(4,1)S(1)}, s32[]{:S(2)}) async-start(s8[8388608]{0:T(1024)(128)(4,1)} %bitcast.378), calls=%async_computation.10 | async-start | bytes 8388608
  328.5 7.6 %slice-start.1 = ((s8[8388608]{0:T(1024)(128)(4,1)}), s8[4194304]{0:T(1024)(128)(4,1)S(1)}, s32[]{:S(2)}) async-start(s8[8388608]{0:T(1024)(128)(4,1)} %bitcast.378), calls=%async_computation.11 | async-start | bytes 8388608
  346.6 4.9 copy-start.9
  346.6 4.9 copy-start.22
  346.6 5.3 copy-start.34
  351.9 3.2 copy-start.24
  357.1 11.0 %copy-start.41 = (bf16[1,4,4,64,512]{4,3,2,1,0:T(8,128)(2,1)S(1)}, bf16[1,4,4,64,512]{4,3,2,1,0:T(8,128)(2,1)}, u32[]{:S(2)}) copy-start(bf16[1,4,4,64,512]{4,3,2,1,0:T(8,128)(2,1)} %get-tuple-element.89) | copy-start | bytes 3145732
  369.4 3.6 copy-start.17
  371.7 7.3 %copy-start.15 = (f32[1024,1024]{1,0:T(8,128)S(1)}, f32[1024,1024]{1,0:T(8,128)}, u32[]{:S(2)}) copy-start(f32[1024,1024]{1,0:T(8,128)} %copy-done.14) | copy-start | bytes 12582916
  375.2 3.8 copy-start.5
  375.2 4.5 copy-start.7
  375.2 5.9 %copy-start.11 = (f32[1024,1024]{1,0:T(8,128)S(1)}, f32[1024,1024]{1,0:T(8,128)}, u32[]{:S(2)}) copy-start(f32[1024,1024]{1,0:T(8,128)} %copy-done.10) | copy-start | bytes 12582916
  375.2 7.0 %copy-start.13 = (f32[1024,1024]{1,0:T(8,128)S(1)}, f32[1024,1024]{1,0:T(8,128)}, u32[]{:S(2)}) copy-start(f32[1024,1024]{1,0:T(8,128)} %fusion.65) | copy-start | bytes 12582916
  403.8 10.1 %copy-start.3 = (bf16[1024,512]{1,0:T(8,128)(2,1)S(1)}, bf16[1024,512]{1,0:T(8,128)(2,1)}, u32[]{:S(2)}) copy-start(bf16[1024,512]{1,0:T(8,128)(2,1)} %copy-done.2) | copy-start | bytes 3145732
  413.8 4.1 copy-start.32
  420.3 3.5 copy-start.25
  421.7 3.3 copy-start.20
  424.9 3.7 copy-start.21
  (20 other events, 44.9 us)
Sparse Core Ops, SparseCore 0:
  9.6 13.2 all-gather.8
  224.3 22.1 all-reduce.10
  248.2 11.7 all-gather.10
  269.7 10.7 reduce-scatter.2
  287.2 11.7 all-gather.6
  324.2 22.3 all-reduce.12
  393.1 10.7 reduce-scatter.4

commit v2 on v1

--- a/solution.py
+++ b/solution.py
@@ -88,84 +88,6 @@
     def finish(self, p):
         for copy in self.along(p) + self.plane(p) + self.onward(p):
             copy.wait_send()
-
-
-def gather_kernel(own4, other4, rest, vec, g, gv, local_sem, ex_send, ex_recv, sends, recvs, vsends, vrecvs):
-    z, yx, c = place()
-    enter(z, yx, c)
-    half = own4.shape[1]
-    mine = pl.ds(pl.multiple_of(c * half, half), half)
-    partner = (z * 4 + yx, 1 - c)
-    swaps = [
-        remote(other4, g.at[0:4, z, yx, mine], ex_send.at[0], ex_recv.at[0], partner),
-        remote(vec, gv.at[z, yx, c], ex_send.at[1], ex_recv.at[1], partner),
-    ]
-    locals_ = [
-        pltpu.make_async_copy(own4, g.at[0:4, z, yx, mine], local_sem.at[0]),
-        pltpu.make_async_copy(rest, g.at[4:PIECES, z, yx], local_sem.at[1]),
-        pltpu.make_async_copy(vec, gv.at[z, yx, c], local_sem.at[2]),
-    ]
-    for copy in swaps + locals_:
-        copy.start()
-    for copy in swaps + locals_:
-        copy.wait()
-    weights = Gather(lambda p: g.at[p], sends, recvs)
-    vectors = Gather(lambda p: gv, vsends, vrecvs)
-    vectors.start(vectors.along(0))
-
-    def launch(p, carry):
-        weights.start(weights.along(p))
-        return carry
-
-    lax.fori_loop(0, PIECES, launch, 0)
-    vectors.step(0)
-
-    def turn(p, carry):
-        weights.step(p)
-
-        @pl.when(p > 0)
-        def _():
-            weights.forward(p - 1)
-
-        return carry
-
-    weights.step(0)
-    vectors.forward(0)
-    lax.fori_loop(1, PIECES, turn, 0)
-    weights.forward(PIECES - 1)
-
-    def close(p, carry):
-        weights.arrive(weights.onward(p))
-        weights.finish(p)
-        return carry
-
-    lax.fori_loop(0, PIECES, close, 0)
-    vectors.arrive(vectors.onward(0))
-    vectors.finish(0)
-
-
-def gather_weights(own4, other4, rest, vec):
-    any_ = pl.BlockSpec(memory_space=pl.ANY)
-    return pl.pallas_call(
-        gather_kernel,
-        out_shape=(
-            jax.ShapeDtypeStruct((PIECES, 4, 4) + rest.shape[1:], BF16),
-            jax.ShapeDtypeStruct((4, 4, 2) + vec.shape, BF16),
-        ),
-        in_specs=[any_] * 4,
-        out_specs=(any_, any_),
-        scratch_shapes=[
-            pltpu.SemaphoreType.DMA((3,)),
-            pltpu.SemaphoreType.DMA((2,)),
-            pltpu.SemaphoreType.DMA((2,)),
-            pltpu.SemaphoreType.DMA((PIECES, 7)),
-            pltpu.SemaphoreType.DMA((PIECES, 7)),
-            pltpu.SemaphoreType.DMA((1, 7)),
-            pltpu.SemaphoreType.DMA((1, 7)),
-        ],
-        compiler_params=pltpu.CompilerParams(collective_id=0, has_side_effects=True),
-        name="gather_weights",
-    )(own4, other4, rest, vec)
 
 
 class Reduce:
@@ -352,60 +274,6 @@
     )(partial, vec)
 
 
-def spread(column):
-    return jnp.broadcast_to(column[:, None], (column.shape[0], 128)).astype(F32)
-
-
-def resets(keep):
-    length = keep.shape[0]
-    place_in = jnp.arange(length) % 8
-
-    def masks(step, inside):
-        one = step
-        two = one * inside(one, 1)
-        four = two * inside(two, 2)
-        return one, two, four
-
-    def down(v, n):
-        return jnp.concatenate([jnp.zeros_like(v[:n]), v[:-n]])
-
-    def up(v, n):
-        return jnp.concatenate([v[n:], jnp.zeros_like(v[:n])])
-
-    f1, f2, f4 = masks(keep, down)
-    after = up(keep, 1)
-    b1, b2, b4 = masks(after, up)
-    grouped = keep.reshape(-1, 8)
-    fp = jnp.cumprod(grouped, axis=1).reshape(-1)
-    bp = jnp.cumprod(after.reshape(-1, 8)[:, ::-1], axis=1)[:, ::-1].reshape(-1)
-    forward = [
-        keep,
-        jnp.where(place_in >= 1, f1, 0.0),
-        jnp.where(place_in >= 2, f2, 0.0),
-        jnp.where(place_in >= 4, f4, 0.0),
-        fp,
-    ]
-    backward = [
-        after,
-        jnp.where(place_in <= 6, b1, 0.0),
-        jnp.where(place_in <= 5, b2, 0.0),
-        jnp.where(place_in <= 3, b4, 0.0),
-        bp,
-    ]
-    return jnp.stack([spread(m) for m in forward]), jnp.stack([spread(m) for m in backward])
-
-
-def decay_rows(fading, reward):
-    rate = jnp.exp(fading)
-    d = jnp.exp(-rate)
-    steps = jnp.arange(8, dtype=F32)[:, None]
-    rising = jnp.exp(-(steps + 1.0) * rate)
-    falling = jnp.exp(-(8.0 - steps) * rate)
-    zero = jnp.zeros_like(d)
-    head = jnp.stack([d, jnp.exp(-2.0 * rate), jnp.exp(-4.0 * rate), jnp.exp(reward), rate * d, zero, zero, zero])
-    return jnp.concatenate([head, rising, falling])
-
-
 def lanes(j):
     return slice(j * 128, (j + 1) * 128)
 
@@ -418,22 +286,43 @@
     return jnp.broadcast_to(v[0:1], v.shape)
 
 
-def wkv_forward(k_ref, v_ref, r_ref, masks_ref, rows_ref, mixed_ref, sn_ref, sd_ref):
+def masks_down(keep, place_in):
+    m1 = jnp.where(place_in >= 1, keep, 0.0)
+    m2 = m1 * pltpu.roll(m1, 1, 0)
+    m4 = m2 * pltpu.roll(m2, 2, 0)
+    for n in (1, 2, 4):
+        keep = keep * jnp.where(place_in >= n, pltpu.roll(keep, n, 0), 1.0)
+    return m1, m2, m4, keep
+
+
+def masks_up(after, place_in):
+    m1 = jnp.where(place_in <= 6, after, 0.0)
+    m2 = m1 * pltpu.roll(m1, 7, 0)
+    m4 = m2 * pltpu.roll(m2, 6, 0)
+    for n in (1, 2, 4):
+        after = after * jnp.where(place_in <= 7 - n, pltpu.roll(after, 8 - n, 0), 1.0)
+    return m1, m2, m4, after
+
+
+def wkv_forward(k_ref, v_ref, r_ref, keep_ref, rows_ref, mixed_ref, sn_ref, sd_ref):
     length, width = k_ref.shape
     tiles = width // 128
-    first = lax.broadcasted_iota(jnp.int32, (8, 128), 0) == 0
+    place_in = lax.broadcasted_iota(jnp.int32, (8, 128), 0)
+    first = place_in == 0
     zero = jnp.zeros((8, 128), F32)
 
     def pair(g, carry):
         carry = list(carry)
         base = pl.multiple_of(g * 16, 16)
+        keeps = [keep_ref[pl.ds(base + 8 * h, 8), :] for h in range(2)]
+        masks = [masks_down(keep, place_in) for keep in keeps]
         for j in range(tiles):
             d1, d2, d4, eu = (rows_ref[n : n + 1, lanes(j)] for n in range(4))
             dp = rows_ref[8:16, lanes(j)]
             made = []
             for h in range(2):
                 at = pl.ds(base + 8 * h, 8)
-                keep, m1, m2, m4, mp = (masks_ref[n, at, :] for n in range(5))
+                keep, (m1, m2, m4, mp) = keeps[h], masks[h]
                 ek = jnp.exp(k_ref[at, lanes(j)])
                 v = v_ref[at, lanes(j)]
                 num, den = ek * v, ek
@@ -459,24 +348,32 @@
 
 
 def wkv_backward(
-    g_ref, k_ref, v_ref, r_ref, sn_ref, sd_ref, masks_ref, rows_ref, gk_ref, gv_ref, gr_ref, sums_ref
+    g_ref, k_ref, v_ref, r_ref, sn_ref, sd_ref, keep_ref, rows_ref, gk_ref, gv_ref, gr_ref, sums_ref
 ):
     length, width = k_ref.shape
     tiles = width // 128
-    last = lax.broadcasted_iota(jnp.int32, (8, 128), 0) == 7
+    place_in = lax.broadcasted_iota(jnp.int32, (8, 128), 0)
+    last = place_in == 7
     zero = jnp.zeros((8, 128), F32)
     pairs = length // 16
 
     def pair(step, carry):
         carry = list(carry)
         base = pl.multiple_of((pairs - 1 - step) * 16, 16)
+        low, high = (keep_ref[pl.ds(base + 8 * h, 8), :] for h in range(2))
+        afters = [
+            jnp.where(last, top(high), pltpu.roll(low, 7, 0)),
+            jnp.where(last, carry[4 * tiles], pltpu.roll(high, 7, 0)),
+        ]
+        masks = [masks_up(after, place_in) for after in afters]
+        carry[4 * tiles] = top(low)
         for j in range(tiles):
             d1, d2, d4, eu = (rows_ref[n : n + 1, lanes(j)] for n in range(4))
             dp = rows_ref[16:24, lanes(j)]
             made = [None, None]
             for h in (1, 0):
                 at = pl.ds(base + 8 * h, 8)
-                after, m1, m2, m4, mp = (masks_ref[n, at, :] for n in range(5))
+                after, (m1, m2, m4, mp) = afters[h], masks[h]
                 ek = jnp.exp(k_ref[at, lanes(j)])
                 v = v_ref[at, lanes(j)]
                 sn, sd = sn_ref[at, lanes(j)], sd_ref[at, lanes(j)]
@@ -511,11 +408,364 @@
                 ref[both, lanes(j)] = jnp.concatenate([made[0][n], made[1][n]], axis=0).astype(BF16)
         return tuple(carry)
 
-    carry = lax.fori_loop(0, pairs, pair, (zero,) * (4 * tiles))
+    carry = lax.fori_loop(0, pairs, pair, (zero,) * (4 * tiles + 1))
     for j in range(tiles):
         rate_d = rows_ref[4:5, lanes(j)]
         sums_ref[0:1, lanes(j)] = jnp.sum(carry[4 * j + 2], axis=0, keepdims=True)
         sums_ref[1:2, lanes(j)] = -rate_d * jnp.sum(carry[4 * j + 3], axis=0, keepdims=True)
+
+
+NN, NT, TN = ((1,), (0,)), ((1,), (1,)), ((0,), (0,))
+KEY, VALUE, GATE, EMIT, GATE2, FFN = 0, 1, 2, 3, 4, 5
+VECTORS = 11
+GAIN1, BIAS1, GAIN2, BIAS2, FADE, REWARD, MK1, MV1, MR1, MK2, MR2, OWN_FADE, OWN_REWARD = range(13)
+
+
+def dot(a, b, dims):
+    return lax.dot_general(a, b, (dims, ((), ())), preferred_element_type=F32)
+
+
+def strip(i, size):
+    return pl.ds(pl.multiple_of(i * size, size), size)
+
+
+def over_rows(length, size, body):
+    def step(i, carry):
+        body(strip(i, size))
+        return carry
+
+    lax.fori_loop(0, length // size, step, 0)
+
+
+def matrix(ref):
+    return ref[...].reshape(16 * ref.shape[2], ref.shape[3])
+
+
+def emit_half(ref, h):
+    rows = ref.shape[2] // 2
+    return ref[:, :, h * rows : (h + 1) * rows, :].reshape(16 * rows, ref.shape[3])
+
+
+def wide(column, width):
+    return jnp.concatenate([column] * (width // 128), axis=1)
+
+
+def norm(x):
+    center = x - jnp.mean(x, axis=-1, keepdims=True)
+    inverse = lax.rsqrt(jnp.mean(center * center, axis=-1, keepdims=True) + 1e-05)
+    return center * inverse, inverse
+
+
+def norm_and_mix(length, width, load, gain, bias, keep_ref, mixes, outs):
+    first = lax.broadcasted_iota(jnp.int32, (16, width), 0) == 0
+
+    def step(i, before):
+        at = strip(i, 16)
+        unit, _ = norm(load(at))
+        normed = unit * gain + bias
+        prev = jnp.where(first, before, pltpu.roll(normed, 1, 0)) * wide(keep_ref[at, :], width)
+        differ = normed - prev
+        for share, out in zip(mixes, outs):
+            out[at, :] = (prev + differ * share).astype(BF16)
+        return normed[15:16]
+
+    lax.fori_loop(0, length // 16, step, jnp.zeros((1, width), F32))
+
+
+def forward_kernel(
+    own4, other4, rest, vec, x_own, up_own, keep_own,
+    g, out, x_out, up_out, ins_out, kvr_out, sn_out, sd_out, mixed_out, resid_out, ins2_out, pre_out, act_out,
+    gv_out, gr_out, vec_out, rows_out, keep_out,
+    gv, w, x, up, ins, kvr, sn, sd, mixed, sum_own, sum_other, resid, ins2, pre, act, v_send, v_other, gval, grec, low_half,
+    local_sem, ex_send, ex_recv, sends, recvs, vsends, vrecvs, stage_sem, out_sem, sum_send, sum_recv, val_send, val_recv,
+):
+    z, yx, c = place()
+    length, width = x.shape
+    half = width // 2
+    span = length // 2
+    partner = (z * 4 + yx, 1 - c)
+    enter(z, yx, c)
+
+    block = own4.shape[1]
+    mine = strip(c, block)
+    rows_mine = strip(c, span)
+    swaps = [
+        (vec, gv.at[z, yx, c]),
+        (other4.at[0:3], g.at[0:3, z, yx, mine]),
+        (other4.at[3], g.at[GATE2, z, yx, mine]),
+        (x_own, x.at[rows_mine]),
+        (keep_own, keep_out.at[rows_mine]),
+        (up_own, up.at[rows_mine]),
+    ]
+    swaps = [remote(a, b, ex_send.at[n], ex_recv.at[n], partner) for n, (a, b) in enumerate(swaps)]
+    keeps = [
+        (vec, gv.at[z, yx, c]),
+        (own4.at[0:3], g.at[0:3, z, yx, mine]),
+        (own4.at[3], g.at[GATE2, z, yx, mine]),
+        (x_own, x.at[rows_mine]),
+        (keep_own, keep_out.at[rows_mine]),
+        (up_own, up.at[rows_mine]),
+        (rest.at[0], g.at[EMIT, z, yx]),
+        (rest.at[1:9], g.at[FFN : FFN + 8, z, yx]),
+    ]
+    keeps = [pltpu.make_async_copy(a, b, local_sem.at[n]) for n, (a, b) in enumerate(keeps)]
+    for copy in swaps + keeps:
+        copy.start()
+    weights = Gather(lambda p: g.at[p], sends, recvs)
+    vectors = Gather(lambda p: gv, vsends, vrecvs)
+
+    outs = []
+
+    def put(src, dst):
+        copy = pltpu.make_async_copy(src, dst, out_sem.at[len(outs)])
+        copy.start()
+        outs.append(copy)
+        return copy
+
+    def stage(p):
+        return pltpu.make_async_copy(g.at[p], w.at[p % 3], stage_sem.at[p])
+
+    def turn(n):
+        if n < PIECES:
+            weights.step(n)
+            if n + 2 < PIECES:
+                weights.start(weights.along(n + 2))
+        if 1 <= n <= PIECES:
+            weights.forward(n - 1)
+        if n >= 2:
+            weights.arrive(weights.onward(n - 2))
+            stage(n - 2).start()
+
+    def staged(p):
+        stage(p).wait()
+        return w.at[p % 3]
+
+    for n in (0, 1, 2):
+        swaps[n].wait()
+        keeps[n].wait()
+    vectors.start(vectors.along(0))
+    weights.start(weights.along(0))
+    for copy in keeps[6:]:
+        copy.wait()
+    weights.start(weights.along(1))
+    vectors.step(0)
+    turn(0)
+    vectors.forward(0)
+    for n in (3, 4, 5):
+        swaps[n].wait()
+        keeps[n].wait()
+    x_copy, up_copy = put(x, x_out), put(up, up_out)
+    turn(1)
+    vectors.arrive(vectors.onward(0))
+
+    for t in range(width // 128):
+        parts = [gv[(2 * t + k) // 4, (2 * t + k) % 4, core].astype(F32) for k in range(2) for core in range(2)]
+        vec_out[:, lanes(t)] = functools.reduce(lambda a, b: a + b, parts)
+    ramp = lax.broadcasted_iota(jnp.int32, (8, 128), 0).astype(F32)
+    for t in range(half // 128):
+        own = functools.reduce(lambda a, b: a + b, [gv[t, k, c].astype(F32) for k in range(4)])
+        rate = jnp.exp(own[OWN_FADE : OWN_FADE + 1])
+        head = [
+            jnp.exp(-rate), jnp.exp(-2.0 * rate), jnp.exp(-4.0 * rate), jnp.exp(own[OWN_REWARD : OWN_REWARD + 1]),
+            rate * jnp.exp(-rate),
+        ]
+        for n, row in enumerate(head):
+            rows_out[n : n + 1, lanes(t)] = row
+        rows_out[8:16, lanes(t)] = jnp.exp(-(ramp + 1.0) * rate)
+        rows_out[16:24, lanes(t)] = jnp.exp(-(8.0 - ramp) * rate)
+
+    def row(n):
+        return vec_out[n : n + 1, :]
+
+    norm_and_mix(
+        length, width, lambda at: x[at, :].astype(F32), row(GAIN1), row(BIAS1), keep_out,
+        [row(MK1), row(MV1), row(MR1)], [ins.at[n] for n in range(3)],
+    )
+    put(ins, ins_out)
+    kvr_copies = []
+    for n in range(3):
+        turn(n + 2)
+        weight = staged(n)
+
+        def project(at):
+            kvr[n, at, :] = dot(ins[n, at, :], matrix(weight), NN)
+
+        over_rows(length, 256, project)
+        kvr_copies.append(put(kvr.at[n], kvr_out.at[n]))
+    wkv_forward(kvr.at[0], kvr.at[1], kvr.at[2], keep_out, rows_out, mixed, sn, sd)
+    put(mixed, mixed_out)
+    put(sn, sn_out)
+    put(sd, sd_out)
+    turn(5)
+    weight = staged(EMIT)
+    quarters = length // 4
+    sums = []
+    for n in range(4):
+        at = pl.ds(n * quarters, quarters)
+        for h in range(2):
+            sum_own[at, h * half : (h + 1) * half] = dot(mixed[at, :], emit_half(weight, h), NN).astype(BF16)
+        sums.append(remote(sum_own.at[at], sum_other.at[at], sum_send.at[n], sum_recv.at[n], partner))
+        sums[-1].start()
+    turn(6)
+    for copy in sums:
+        copy.wait()
+
+    def add_up(at):
+        total = x[at, :].astype(F32) + (sum_own[at, :].astype(F32) + sum_other[at, :].astype(F32))
+        resid[0, at, :] = total[:, :half]
+        resid[1, at, :] = total[:, half:]
+        return total
+
+    norm_and_mix(
+        length, width, add_up, row(GAIN2), row(BIAS2), keep_out, [row(MK2), row(MR2)], [ins2.at[n] for n in range(2)]
+    )
+    put(resid, resid_out)
+    put(ins2, ins2_out)
+    for copy in kvr_copies:
+        copy.wait()
+    weight = staged(GATE2)
+
+    def gate(at):
+        kvr[2, at, :] = jax.nn.sigmoid(dot(ins2[1, at, :], matrix(weight), NN))
+
+    over_rows(length, 256, gate)
+    pre_copies = []
+    for j in range(4):
+        turn(FFN + 2 * j + 2)
+        weight = staged(FFN + 2 * j)
+        if j >= 2:
+            pre_copies[j - 2].wait()
+
+        def expand(at):
+            positive = jnp.maximum(dot(ins2[0, at, :], matrix(weight), NN), 0.0)
+            pre[j % 2, at, :] = positive.astype(BF16)
+            act[j, at, :] = (positive * positive).astype(BF16)
+
+        over_rows(length, 256, expand)
+        pre_copies.append(put(pre.at[j % 2], pre_out.at[j]))
+        put(act.at[j], act_out.at[j])
+        turn(FFN + 2 * j + 3)
+        weight = staged(FFN + 2 * j + 1)
+
+        def contract(at):
+            for h in range(2):
+                part = dot(act[j, at, :], weight[2 * h : 2 * h + 2].reshape(half, -1), NT)
+                kvr[h, at, :] = part if j == 0 else kvr[h, at, :] + part
+
+        over_rows(length, 256, contract)
+
+    vals = []
+    for n in range(4):
+        at = pl.ds(n * quarters, quarters)
+        v_send[at, :] = kvr[1 - c, at, :].astype(BF16)
+        vals.append(remote(v_send.at[at], v_other.at[at], val_send.at[n], val_recv.at[n], partner))
+        vals[-1].start()
+    columns = strip(c, half)
+    backs = []
+    for n in range(4):
+        vals[n].wait()
+
+        def finish(i, carry):
+            at = strip(n * (quarters // 16) + i, 16)
+            value = kvr[c, at, :] + v_other[at, :].astype(F32)
+            s = kvr[2, at, :]
+            low_half[at, :] = (resid[c, at, :] + s * value).astype(BF16)
+            upstream = up[at, columns].astype(F32)
+            gval[c, at, :] = (upstream * s).astype(BF16)
+            grec[at, :] = (upstream * value * s * (1.0 - s)).astype(BF16)
+            return carry
+
+        lax.fori_loop(0, quarters // 16, finish, 0)
+        at = pl.ds(n * quarters, quarters)
+        backs.append(remote(gval.at[c, at], gval.at[c, at], val_send.at[4 + n], val_recv.at[4 + n], partner))
+        backs[-1].start()
+    give = remote(low_half.at[strip(1 - c, span)], out.at[:, columns], val_send.at[8], val_recv.at[8], partner)
+    give.start()
+    put(low_half.at[rows_mine], out.at[:, columns])
+    put(grec, gr_out)
+    for copy in backs:
+        copy.wait()
+    put(gval, gv_out)
+    give.wait()
+
+    def close(p, carry):
+        weights.finish(p)
+        return carry
+
+    lax.fori_loop(0, PIECES, close, 0)
+    vectors.finish(0)
+    waited = kvr_copies + pre_copies[:2]
+    for copy in outs:
+        if not any(copy is other for other in waited):
+            copy.wait()
+
+
+def forward_call(own4, other4, rest, vec, x_own, up_own, keep_own):
+    span, width = x_own.shape
+    length, half = 2 * span, width // 2
+    block = rest.shape[1:]
+    any_, vmem = pl.BlockSpec(memory_space=pl.ANY), pl.BlockSpec(memory_space=pltpu.VMEM)
+    full, col = (length, width), (length, half)
+
+    def shape(dims, kind):
+        return jax.ShapeDtypeStruct(dims, kind)
+
+    outs = (
+        (shape((PIECES, 4, 4) + block, BF16), any_),
+        (shape((span, width), BF16), any_),
+        (shape(full, BF16), any_),
+        (shape(full, BF16), any_),
+        (shape((3,) + full, BF16), any_),
+        (shape((3,) + col, F32), any_),
+        (shape(col, F32), any_),
+        (shape(col, F32), any_),
+        (shape(col, BF16), any_),
+        (shape((2,) + col, F32), any_),
+        (shape((2,) + full, BF16), any_),
+        (shape((4,) + col, BF16), any_),
+        (shape((4,) + col, BF16), any_),
+        (shape((2,) + col, BF16), any_),
+        (shape(col, BF16), any_),
+        (shape((16, width), F32), vmem),
+        (shape((24, half), F32), vmem),
+        (shape((length, 128), F32), vmem),
+    )
+    dma = pltpu.SemaphoreType.DMA
+    return pl.pallas_call(
+        forward_kernel,
+        out_shape=tuple(o[0] for o in outs),
+        in_specs=[any_] * 7,
+        out_specs=tuple(o[1] for o in outs),
+        scratch_shapes=[
+            pltpu.VMEM((4, 4, 2) + vec.shape, BF16),
+            pltpu.VMEM((3, 4, 4) + block, BF16),
+            pltpu.VMEM(full, BF16),
+            pltpu.VMEM(full, BF16),
+            pltpu.VMEM((3,) + full, BF16),
+            pltpu.VMEM((3,) + col, F32),
+            pltpu.VMEM(col, F32),
+            pltpu.VMEM(col, F32),
+            pltpu.VMEM(col, BF16),
+            pltpu.VMEM(full, BF16),
+            pltpu.VMEM(full, BF16),
+            pltpu.VMEM((2,) + col, F32),
+            pltpu.VMEM((2,) + full, BF16),
+            pltpu.VMEM((2,) + col, BF16),
+            pltpu.VMEM((4,) + col, BF16),
+            pltpu.VMEM(col, BF16),
+            pltpu.VMEM(col, BF16),
+            pltpu.VMEM((2,) + col, BF16),
+            pltpu.VMEM(col, BF16),
+            pltpu.VMEM(col, BF16),
+            dma((8,)), dma((6,)), dma((6,)),
+            dma((PIECES, 7)), dma((PIECES, 7)), dma((1, 7)), dma((1, 7)),
+            dma((PIECES,)), dma((24,)), dma((4,)), dma((4,)), dma((9,)), dma((9,)),
+        ],
+        compiler_params=pltpu.CompilerParams(
+            collective_id=0, has_side_effects=True, vmem_limit_bytes=60 * MIB
+        ),
+        name="forward",
+    )(own4, other4, rest, vec, x_own, up_own, keep_own)
 
 
 def shifted(value, axis, steps):
@@ -978,25 +1228,12 @@
     return jnp.stack([a, b], axis=-2).reshape(own.shape[:-1] + (2 * half,))
 
 
-def pair_row(a, axis):
-    return lax.all_gather(a, "tensor", axis=axis, tiled=True)
-
-
 def pair_sum(a):
     return lax.psum(a.astype(BF16), "tensor").astype(F32)
 
 
-def dot(a, b, dims, out=F32):
-    return lax.dot_general(a, b, (dims, ((), ())), preferred_element_type=out)
-
-
-NN, NT, TN = ((1,), (0,)), ((1,), (1,)), ((0,), (0,))
-
-
 def layer_norm(values, gain, bias):
-    center = values - jnp.mean(values, axis=-1, keepdims=True)
-    inverse = lax.rsqrt(jnp.mean(center * center, axis=-1, keepdims=True) + 1e-05)
-    normed = center * inverse
+    normed, inverse = norm(values)
     return normed * gain + bias, normed, inverse
 
 
@@ -1016,76 +1253,62 @@
     return jnp.concatenate([v[1:], jnp.zeros_like(v[:1])])
 
 
-VECTORS = 11
-
-
-def shards(
-    tokens, starts, upstream, gain1, bias1, gain2, bias2, fading, reward,
-    mk1, mv1, mr1, wk, wv, wr, wo, mk2, mr2, wg, fk, fv,
-):
-    c = lax.axis_index("tensor")
-    i = lax.axis_index("dp")
-    count = lax.axis_size("dp")
+def pack(tokens, starts, upstream, gain1, bias1, gain2, bias2, fading, reward, mk1, mv1, mr1, wk, wv, wr, wo, mk2, mr2, wg, fk, fv):
+    i, c, count = lax.axis_index("dp"), lax.axis_index("tensor"), lax.axis_size("dp")
     own_rows, width = wk.shape
-    half = width // 2
-    hidden = fk.shape[1]
-    block = width // (2 * count)
-
+    half, hidden = width // 2, fk.shape[1]
     by_core = jnp.stack([split_columns(wk, count), split_columns(wv, count), split_columns(wr, count), split_columns(wg, 1)])
     own4 = lax.dynamic_index_in_dim(by_core, c, 1, False)
     other4 = lax.dynamic_index_in_dim(by_core, 1 - c, 1, False)
     emit = wo.reshape(own_rows, 2, half).transpose(1, 0, 2).reshape(1, 2 * own_rows, half)
     key4 = fk.reshape(2 * own_rows, 4, hidden // 4).transpose(1, 0, 2)
     value4 = fv.reshape(4, hidden // 4, 2 * own_rows).transpose(0, 2, 1)
-    rest = jnp.concatenate([emit, key4, value4])
-    vectors = jnp.stack([gain1, bias1, gain2, bias2, fading, reward, mk1, mv1, mr1, mk2, mr2])
-    vectors = jnp.pad(vectors, ((0, 16 - VECTORS), (0, 0)))
-    slot = (2 * i + c) % (128 // own_rows)
-    lane = jnp.arange(128) // own_rows
-    vec = jnp.where(lane[None, :] == slot, jnp.tile(vectors, (1, 128 // own_rows)), 0).astype(BF16)
-
-    g, gv = gather_weights(own4, other4, rest, vec)
-
-    full = gv.reshape(count * 2 * own_rows // 128, 128 // own_rows, 16, 128).astype(F32).sum(1)
-    full = full.transpose(1, 0, 2).reshape(16, width)
-    gain1, bias1, gain2, bias2, fading, reward, mk1, mv1, mr1, mk2, mr2 = (full[n] for n in range(VECTORS))
-    g = g.reshape((PIECES, count, 2 * own_rows, half))
-    wk, wv, wr, wg = (g[n].reshape(width, half) for n in range(4))
-    wo = g[4].reshape(count, 2, own_rows, half).transpose(0, 2, 1, 3).reshape(half, width)
-    fk = jnp.concatenate([g[5 + n].reshape(width, hidden // 4) for n in range(4)], axis=1)
-    fv = jnp.concatenate([g[9 + n].reshape(width, hidden // 4) for n in range(4)], axis=1)
-
-    def own_channels(v):
-        return lax.dynamic_index_in_dim(split_columns(v[None], count)[:, 0], c, 0, False)
-
-    keep = pair_row((1 - starts[0]).astype(F32), 0)
-    x = pair_row(tokens[0], 0).astype(F32)
-    up_half = lax.dynamic_slice_in_dim(pair_row(upstream[0], 0), c * half, half, 1).astype(F32)
+    ffn = jnp.stack([key4, value4], axis=1).reshape(8, 2 * own_rows, hidden // 4)
+    rest = jnp.concatenate([emit, ffn])
+    slots = 128 // own_rows
+    everywhere = jnp.stack([gain1, bias1, gain2, bias2, fading, reward, mk1, mv1, mr1, mk2, mr2])
+    own = jnp.stack([fading, reward, jnp.zeros_like(fading), jnp.zeros_like(fading), jnp.zeros_like(fading)])
+    lane = jnp.arange(128)[None, :] // own_rows
+    vec = jnp.concatenate([
+        jnp.where(lane == (2 * i + c) % slots, jnp.tile(everywhere, (1, slots)), 0),
+        jnp.where(lane == i % slots, jnp.tile(own, (1, slots)), 0),
+    ]).astype(BF16)
+    keep = jnp.broadcast_to((1 - starts[0]).astype(F32)[:, None], (starts.shape[1], 128))
+    return own4, other4, rest, vec, tokens[0], upstream[0], keep
+
+
+def shards(*args):
+    tokens = args[0]
+    c = lax.axis_index("tensor")
+    i = lax.axis_index("dp")
+    count = lax.axis_size("dp")
+    own_rows, width = args[12].shape
+    hidden = args[19].shape[1]
+    half = width // 2
+    (
+        g, layer_out, x, up, ins, kvr, sn, sd, mixed, resid, ins2, pre, act, g_value, g_recept2, vec, rows, keep,
+    ) = forward_call(*pack(*args))
+
+    gain1, bias1, gain2, bias2, fading, reward, mk1, mv1, mr1, mk2, mr2 = (vec[n] for n in range(VECTORS))
+    keep_rows, keep = keep, keep[:, 0]
+    g = g.reshape((PIECES, width, half))
+    wk, wv, wr, wg = g[KEY], g[VALUE], g[GATE], g[GATE2]
+    wo = g[EMIT].reshape(count, 2, own_rows, half).transpose(0, 2, 1, 3).reshape(half, width)
+    fk = jnp.concatenate([g[FFN + 2 * n] for n in range(4)], axis=1)
+    fv = jnp.concatenate([g[FFN + 1 + 2 * n] for n in range(4)], axis=1)
+    x, up = x.astype(F32), up.astype(F32)
     n1, u1, i1 = layer_norm(x, gain1, bias1)
-    p1 = shift_down(n1, keep)
-    d1 = n1 - p1
-    in_k, in_v, in_r = ((p1 + d1 * m).astype(BF16) for m in (mk1, mv1, mr1))
-    k, v, r = dot(in_k, wk, NN), dot(in_v, wv, NN), dot(in_r, wr, NN)
-    fmask, bmask = resets(keep)
-    rows = decay_rows(own_channels(fading), own_channels(reward))
-    shape = jax.ShapeDtypeStruct(k.shape, F32)
+    d1 = n1 - shift_down(n1, keep)
+    in_k, in_v, in_r = (ins[n] for n in range(3))
+    k, v, r = (kvr[n] for n in range(3))
+    resid = jnp.concatenate([resid[0], resid[1]], axis=1)
+    n2, u2, i2 = layer_norm(resid, gain2, bias2)
+    d2 = n2 - shift_down(n2, keep)
+    in_k2, in_r2 = ins2[0], ins2[1]
+    pre = jnp.concatenate([pre[n] for n in range(4)], axis=1).astype(F32)
+    act = jnp.concatenate([act[n] for n in range(4)], axis=1)
+    g_value = jnp.concatenate([g_value[0], g_value[1]], axis=1)
     low = jax.ShapeDtypeStruct(k.shape, BF16)
-    mixed, sn, sd = local_call(wkv_forward, (low, shape, shape), "wkv_forward", k, v, r, fmask, rows)
-    resid = x + pair_sum(dot(mixed, wo, NN))
-    n2, u2, i2 = layer_norm(resid, gain2, bias2)
-    p2 = shift_down(n2, keep)
-    d2 = n2 - p2
-    in_k2, in_r2 = ((p2 + d2 * m).astype(BF16) for m in (mk2, mr2))
-    s2 = jax.nn.sigmoid(dot(in_r2, wg, NN))
-    pre = jax.nn.relu(dot(in_k2, fk, NN))
-    act = (pre * pre).astype(BF16)
-    value = lax.psum_scatter(dot(act, fv, NT).astype(BF16), "tensor", scatter_dimension=1, tiled=True).astype(F32)
-    resid_half = lax.dynamic_slice_in_dim(resid, c * half, half, 1)
-    out_half = (resid_half + s2 * value).astype(BF16)
-    layer_out = lax.all_to_all(out_half, "tensor", 0, 1, tiled=True)
-    g_value = (up_half * s2).astype(BF16)
-    g_recept2 = (up_half * value * s2 * (1.0 - s2)).astype(BF16)
-    g_value = pair_row(g_value, 1)
     grad_fv = dot(g_value, act, TN)
     g_pre = (2.0 * pre * dot(g_value, fv, NN)).astype(BF16)
     grad_fk = dot(in_k2, g_pre, TN)
@@ -1095,14 +1318,13 @@
     grad_mk2, grad_mr2 = jnp.sum(gk2 * d2, 0), jnp.sum(gr2 * d2, 0)
     gn2 = gk2 * mk2 + gr2 * mr2 + shift_up(gk2 * (1 - mk2) + gr2 * (1 - mr2), keep)
     grad_gain2, grad_bias2 = jnp.sum(gn2 * u2, 0), jnp.sum(gn2, 0)
-    upstream_row = pair_row(upstream[0], 0).astype(F32)
-    g_resid = upstream_row + norm_back(pair_sum(gn2), u2, i2, gain2)
+    g_resid = up + norm_back(pair_sum(gn2), u2, i2, gain2)
     g_branch = g_resid.astype(BF16)
     grad_wo = dot(mixed, g_branch, TN)
     g_mixed = dot(g_branch, wo, NT)
     gk1, gv1, gr1, wsums = local_call(
         wkv_backward, (low, low, low, jax.ShapeDtypeStruct((8, half), F32)), "wkv_backward",
-        g_mixed, k, v, r, sn, sd, bmask, rows,
+        g_mixed, k, v, r, sn, sd, keep_rows, rows,
     )
     grad_wk, grad_wv, grad_wr = dot(in_k, gk1, TN), dot(in_v, gv1, TN), dot(in_r, gr1, TN)
     toward, behind, grad_mix = 0.0, 0.0, []
@@ -1121,14 +1343,12 @@
 
     grad_tokens = mine(g_resid) + norm_back(gn1, mine(u1), mine(i1), gain1)
 
-    blocks = (4, 4) if count == 16 else (count,)
-
     def pieces(m):
-        return m.reshape((1,) + blocks + (2 * own_rows, half))
+        return m.reshape(1, 4, 4, 2 * own_rows, half)
 
     grad_wo = grad_wo.reshape(count, own_rows, 2, half).transpose(0, 2, 1, 3)
     grad_fk, grad_fv = (
-        m.reshape(width, 4, hidden // 4).transpose(1, 0, 2).reshape((4,) + blocks + (2 * own_rows, half))
+        m.reshape(width, 4, hidden // 4).transpose(1, 0, 2).reshape((4, 4, 4) + (2 * own_rows, half))
         for m in (grad_fk, grad_fv)
     )
     partial = jnp.concatenate(
@@ -1137,7 +1357,7 @@
 
     def all_channels(v):
         z = jnp.zeros_like(v)
-        return join_columns(jnp.where(c == 0, v, z)[None], jnp.where(c == 1, v, z)[None], 0, count)[0]
+        return jnp.where(c == 0, jnp.concatenate([v, z]), jnp.concatenate([z, v]))
 
     vsums = jnp.stack([
         grad_gain1, grad_bias1, grad_gain2, grad_bias2, all_channels(wsums[1]), all_channels(wsums[0]),
@@ -1145,6 +1365,7 @@
     ])
     vsums = jnp.pad(vsums, ((0, 16 - VECTORS), (0, 0)))
     total, recv4, vtotal = reduce_weights(partial, vsums)
+    own_scan = lax.dynamic_slice_in_dim(vtotal, c * half + i * own_rows, own_rows, 1)
     vtotal = lax.dynamic_slice_in_dim(vtotal, (2 * i + c) * own_rows, own_rows, 1)
     own = lax.dynamic_slice_in_dim(total[:4], c * own_rows, own_rows, 1)
     out_k, out_v, out_r = (join_columns(own[n], recv4[n], c, count) for n in range(3))
@@ -1153,15 +1374,15 @@
     out_fk = total[5:9].transpose(1, 0, 2).reshape(2 * own_rows, hidden)
     out_fv = total[9:13].transpose(0, 2, 1).reshape(hidden, 2 * own_rows)
     return (
-        layer_out[None], grad_tokens[None], *(vtotal[n] for n in range(9)),
-        out_k, out_v, out_r, out_o, vtotal[9], vtotal[10], out_g, out_fk, out_fv,
+        layer_out[None], grad_tokens[None], *(vtotal[n] for n in range(4)), own_scan[4], own_scan[5],
+        *(vtotal[n] for n in range(6, 9)), out_k, out_v, out_r, out_o, vtotal[9], vtotal[10], out_g, out_fk, out_fv,
     )
 
 
 def solution(mesh):
-    row, vector, matrix = P("dp", "tensor", None), P(("dp", "tensor")), P(("dp", "tensor"), None)
+    row, vector, matrix_ = P("dp", "tensor", None), P(("dp", "tensor")), P(("dp", "tensor"), None)
     key, value = P("dp", "tensor"), P("tensor", "dp")
-    in_specs = (row, P("dp", "tensor"), row) + (vector,) * 9 + (matrix,) * 4 + (vector,) * 2 + (matrix, key, value)
-    out_specs = (row, row) + (vector,) * 9 + (matrix,) * 4 + (vector,) * 2 + (matrix, key, value)
+    in_specs = (row, P("dp", "tensor"), row) + (vector,) * 9 + (matrix_,) * 4 + (vector,) * 2 + (matrix_, key, value)
+    out_specs = (row, row) + (vector,) * 9 + (matrix_,) * 4 + (vector,) * 2 + (matrix_, key, value)
     body = shards if (mesh.shape["dp"], mesh.shape["tensor"]) == (16, 2) else wide_shards
     return jax.shard_map(body, mesh=mesh, in_specs=in_specs, out_specs=out_specs, check_vma=False)

time: 593 us -> 525 us (0.89); the launches traced: 582 us -> 521 us
  waiting for transfers between devices: 37.4 us -> 0.04 us
  matrix products: 81.1 us -> 55.1 us
  other arithmetic: 63.6 us -> 46.6 us
  local copies, waits for them, and re-layouts: 80.8 us -> 96 us
  Pallas kernels: 296 us -> 308 us
  blocking collectives: 6.62 us -> 0 us
    dot_general x0 -> x7, local copies, waits for them, and re-layouts: none -> 28.2 us  [dot(): return lax.dot_general(a, b, (dims, ((), ())), preferred_element_type=F32)]
    dot_general x21 -> x14, matrix products: 81.1 us -> 55.1 us  [dot(): return lax.dot_general(a, b, (dims, ((), ())), preferred_element_type=F32)]
    psum x2 -> x1, waiting for transfers between devices: 24.5 us -> 0.01 us  [pair_sum(): return lax.psum(a.astype(BF16), 'tensor').astype(F32)]
    pallas_call x1, Pallas kernels: 150 us -> 171 us  [forward_call(): pl.pallas_call(forward_kernel, out_shape=tuple((o[0] for o in outs)), in_...]
    unnamed x139 -> x94, local copies, waits for them, and re-layouts: 34.1 us -> 19.5 us
    convert_element_type x4 -> x1, other arithmetic: 13.2 us -> 0.68 us  [pack(): (1 - starts[0]).astype(F32)[:, None]]
    reduce_scatter x1 -> x0, waiting for transfers between devices: 10.8 us -> none  [shards(): lax.psum_scatter(dot(act, fv, NT).astype(BF16), 'tensor', scatter_dimensi...]
    pallas_call x2 -> x1, Pallas kernels: 19.1 us -> 9.98 us  [local_call(): pl.pallas_call(body, out_shape=outs, in_specs=[vmem] * len(args), out_spe...]
  transfers between devices with their start and end apart: 7 -> 2, of which waited for: 4 -> 0; matrix products, arithmetic and copies ran while one was open for 20% -> 19% of each run, Pallas kernels for 48% -> 24%
where the time goes in v2:
time: 525 us; the launch traced here: 521 us
  Pallas kernels  308 us (59%)
  local copies, waits for them, and re-layouts  96 us (18%)
  matrix products  55.1 us (10%)
  other arithmetic  46.6 us (9%)
  between operations  15.2 us (3%)
    pallas_call x1, Pallas kernels, forward_call(): pl.pallas_call(forward_kernel, out_shape=tuple((o[0] for o in outs)), in_...  171 us
    pallas_call x1, Pallas kernels, reduce_weights(): pl.pallas_call(reduce_kernel, out_shape=(jax.ShapeDtypeStruct((PIECES, ro...  126 us
    dot_general x14, matrix products, dot(): return lax.dot_general(a, b, (dims, ((), ())), preferred_element_type=F32)  55.1 us
    dot_general x7, local copies, waits for them, and re-layouts, dot(): return lax.dot_general(a, b, (dims, ((), ())), preferred_element_type=F32)  28.2 us
    unnamed x94, local copies, waits for them, and re-layouts  19.5 us
    reduce_sum x1, other arithmetic, shards(): grad_gain1, grad_bias1 = (jnp.sum(gn1 * u1, 0), jnp.sum(gn1, 0))  12.1 us
  transfers between devices with their start and end apart: 2, of which 0 were waited for; matrix products, arithmetic and copies ran while one was open for 19% of the time, Pallas kernels for 24%

profile of v2, /device:TPU:0, one launch (start us, length us, event | category | flops | bytes accessed | tf_op | source)
XLA Modules:
  0.0 520.5 jit_solution(11745856299356684080)
XLA Ops:
  7.3 1.6 stack.119
  19.6 171.1 %forward.1 = (bf16[13,4,4,64,512]{4,3,2,1,0:T(8,128)(2,1)}, bf16[512,1024]{1,0:T(8,128)(2,1)}, bf16[1024,1024]{1,0:T(8,128)(2,1)}, bf16[1024,1024]{1,0:T(8,128)(...) custom-call(bf16[4,32,512]{2,1,0:T(8,128)(2,1)} %get-tuple-element.1, ...), custom_call_target="tpu_custom_call" | custom-call | tf_op jit(solution)/shard_map/forward/pallas_call | solution.py:734
  190.7 9.9 %fusion.59 = (bf16[1,4,4,64,512]{4,3,2,1,0:T(8,128)(2,1)}, bf16[1,4,4,64,512]{4,3,2,1,0:T(8,128)(2,1)}, bf16[1,4,4,64,512]{4,3,2,1,0:T(8,128)(2,1)}, bf16[1,4,4,...) fusion(bf16[13,4,4,64,512]{4,3,2,1,0:T(8,128)(2,1)} %get-tuple-, ...), kind=kLoop, calls=%fused_computation.179 | loop fusion | bytes 27262976 | tf_op jit(solution)/shard_map/slice | solution.py:1295
  201.0 1.3 copy-done.27
  202.8 1.3 fusion.62
  204.1 10.2 %multiply_convert_fusion = bf16[1024,2048]{1,0:T(8,128)(2,1)S(1)} fusion(bf16[1024,512]{1,0:T(8,128)(2,1)S(1)} %get-tuple-element.120, bf16[1024,512]{1,0:T(8,128)(2,1)S(1)} %get-tuple-element.121, bf16[1024,512]{1,0:T(8,128)(2,1)S(1)} %get-tuple-element.122, bf16[1024,512]{1,0:T(8,128)(2,1)S(1)} %get-tuple-element.119, bf16[1024,512]{1,0:T(8,128)(2,1)} %bitcast.300, ...), kind=kOutput, calls=%fused_computation | convolution fusion | flops 4339007488 | bytes 14680064 | tf_op jit(solution)/shard_map/dot_general | solution.py:425
  214.3 7.8 %fusion.15 = f32[1024,1024]{1,0:T(8,128)S(1)} fusion(bf16[1024,2048]{1,0:T(8,128)(2,1)S(1)} %multiply_convert_fusion, bf16[1024,512]{1,0:T(8,128)(2,1)} %bitcast.296, bf16[1024,512]{1,0:T(8,128)(2,1)} %bitcast.297, bf16[1024,512]{1,0:T(8,128)(2,1)} %bitcast.298, bf16[1024,512]{1,0:T(8,128)(2,1)} %bitcast.299), kind=kOutput, calls=%fused_computation.25 | convolution fusion | flops 4311744512 | bytes 12582912 | tf_op jit(solution)/shard_map/dot_general | solution.py:425
  224.1 4.3 fusion.58
  228.5 2.8 slice_reduce_fusion
  232.4 2.8 copy-done.18
  236.0 2.9 slice_bitcast_fusion.1
  240.4 6.9 %fusion.32 = bf16[1024,2048]{1,0:T(8,128)(2,1)} fusion(bf16[1024,512]{1,0:T(8,128)(2,1)S(1)} %get-tuple-element.114, bf16[1024,512]{1,0:T(8,128)(2,1)S(1)} %get-tuple-element.115, bf16[1024,512]{1,0:T(8,128)(2,1)S(1)} %get-tuple-element.116, bf16[1024,512]{1,0:T(8,128)(2,1)S(1)} %get-tuple-element.113, bf16[1024,512]{1,0:T(8,128)(2,1)S(1)} %copy-done.34, ...), kind=kOutput, calls=%fused_computation.59 | convolution fusion | flops 4318035968 | bytes 10485760 | tf_op jit(solution)/shard_map/dot_general | solution.py:425
  247.3 2.5 copy.67
  251.1 2.3 copy.104
  253.4 3.9 copy.68
  257.4 3.9 copy.69
  261.3 4.0 copy.70
  265.3 6.4 %copy.89 = bf16[2048,1024]{1,0:T(8,128)(2,1)} copy(bf16[2048,1024]{0,1:T(8,128)(2,1)} %bitcast.276) | data formatting | bytes 8388608 | tf_op jit(solution)/shard_map/dot_general | solution.py:425
  271.7 4.3 multiply_add_fusion.1
  276.0 6.3 %slice_bitcast_fusion.4 = (f32[1024,512]{1,0:T(8,128)}, f32[1024,512]{1,0:T(8,128)}, f32[1024,512]{1,0:T(8,128)}) fusion(f32[3,1024,512]{2,1,0:T(8,128)} %get-tuple-element.55), kind=kLoop, calls=%fused_computation.72 | loop fusion | bytes 12582912 | tf_op jit(solution)/shard_map/squeeze | solution.py:1303
  283.5 6.2 %convolution_convert_fusion = bf16[1024,4,512]{2,0,1:T(8,128)(2,1)} fusion(bf16[4,512,1024]{2,1,0:T(8,128)(2,1)S(1)} %bitcast.278, bf16[2,1024,1024]{2,1,0:T(8,128)(2,1)S(1)} %copy-done.29), kind=kOutput, calls=%fused_computation.60 | convolution fusion | flops 4297064448 | bytes 10485760 | tf_op jit(solution)/shard_map/dot_general | solution.py:425
  289.7 4.8 multiply_reduce_fusion.5
  295.0 2.0 multiply_add_fusion.2
  297.1 1.3 fusion.51.g_ref
  298.4 10.0 %wkv_backward.1 = (bf16[1024,512]{1,0:T(8,128)(2,1)S(1)}, bf16[1024,512]{1,0:T(8,128)(2,1)S(1)}, bf16[1024,512]{1,0:T(8,128)(2,1)S(1)}, f32[8,512]{1,0:T(8,128)S(1)}) custom-call(f32[1024,512]{1,0:T(8,128)S(1)} %fusion.51.g_ref, f32[1024,512]{1,0:T(8,128)} %get-tuple-element.111.k_ref, f32[1024,512]{1,0:T(8,128)} %get-tuple-element.110.v_ref, ...), custom_call_target="tpu_custom_call" | custom-call | tf_op jit(solution)/shard_map/wkv_backward/pallas_call | solution.py:1209
  308.4 2.9 fusion.65
  311.3 1.3 fusion.64
  312.6 1.3 fusion.63
  314.6 3.5 fusion.4
  318.9 1.3 copy-done.6
  320.8 12.1 %fusion.57 = (f32[1024]{0:T(1024)S(1)}, f32[1024]{0:T(1024)S(1)}, f32[1024]{0:T(1024)S(1)}, f32[1024]{0:T(1024)S(1)}, f32[1024]{0:T(1024)S(1)}, /*index=5*/f32[1...) fusion(f32[1024]{0:T(1024)S(1)} %add_rsqrt_fusion, ...), kind=kLoop, calls=%fused_computation.177 | loop fusion | flops 30401536 | bytes 46186496 | tf_op jit(solution)/shard_map/reduce_sum | solution.py:1337
  332.9 3.1 slice_bitcast_fusion
  336.0 4.0 copy.71
  340.1 5.0 convolution_convert_fusion.1
  345.1 2.9 reshape.455
  348.0 2.4 copy.72
  350.5 4.3 fusion.39
  354.8 2.2 fusion.41
  357.1 2.2 fusion.43
  359.3 2.2 fusion.45
  362.7 2.6 constant_dynamic-update-slice_fusion.1
  366.4 2.5 constant_dynamic-update-slice_fusion.partial
  368.9 126.5 %reduce_weights.1 = (f32[13,64,512]{2,1,0:T(8,128)S(1)}, f32[4,32,512]{2,1,0:T(8,128)S(1)}, f32[16,1024]{1,0:T(8,128)S(1)}) custom-call(bf16[13,4,4,64,512]{4,3,2,1,0:T(8,128)(2,1)} %constant_dynamic-update-slice_fusion.partial, f32[16,1024]{1,0:T(8,128)S(1)} %pad.12.vec), custom_call_target="tpu_custom_call" | custom-call | tf_op jit(solution)/shard_map/reduce_weights/pallas_call | solution.py:247
  497.2 1.3 reshape.462
  499.2 1.3 reshape.461
  501.2 1.3 reshape.460
  505.5 2.4 fusion.37
  507.9 4.5 add_bitcast_fusion
  (172 shorter events, 31.4 us)
Async XLA Ops:
  7.2 9.9 %copy-start.38 = (bf16[64,2048]{1,0:T(8,128)(2,1)S(1)}, bf16[64,2048]{1,0:T(8,128)(2,1)}, u32[]{:S(2)}) copy-start(bf16[64,2048]{1,0:T(8,128)(2,1)} %param.40) | copy-start | bytes 786436
  7.2 9.9 %copy-start.37 = (bf16[2048,64]{0,1:T(8,128)(2,1)S(1)}, bf16[2048,64]{0,1:T(8,128)(2,1)}, u32[]{:S(2)}) copy-start(bf16[2048,64]{0,1:T(8,128)(2,1)} %param.41) | copy-start | bytes 786436
  7.2 282.5 %all-reduce.11.cloned.1.call-start = ((), (), s32[]{:S(2)}) async-start(), calls=%async_computation.1 | async-start | bytes 4194304 | tf_op jit(solution)/shard_map/psum | solution.py:1232
  190.7 10.0 %copy-start.20 = (bf16[4,1024,512]{2,1,0:T(8,128)(2,1)S(1)}, bf16[4,1024,512]{2,1,0:T(8,128)(2,1)}, u32[]{:S(2)}) copy-start(bf16[4,1024,512]{2,1,0:T(8,128)(2,1)} %get-tuple-element.48) | copy-start | bytes 12582916
  200.7 1.6 copy-start.27
  201.0 1.5 copy-start.39
  201.0 1.5 copy-start
  201.0 1.8 copy-start.40
  202.4 1.7 copy-start.31
  202.4 1.7 copy-start.33
  204.1 19.2 %copy-start.3 = (f32[1024,1024]{1,0:T(8,128)}, f32[1024,1024]{1,0:T(8,128)S(1)}, u32[]{:S(2)}) copy-start(f32[1024,1024]{1,0:T(8,128)S(1)} %fusion.62) | copy-start | bytes 12582916
  214.3 7.8 %copy-start.19 = (bf16[1024,2048]{1,0:T(8,128)(2,1)}, bf16[1024,2048]{1,0:T(8,128)(2,1)S(1)}, u32[]{:S(2)}) copy-start(bf16[1024,2048]{1,0:T(8,128)(2,1)S(1)} %multiply_convert_fusion) | copy-start | bytes 12582916
  222.1 2.0 copy-start.5
  228.4 277.1 %reduce-scatter.2.cloned.1.call-start = ((), (), s32[]{:S(2)}) async-start(), calls=%async_computation.2 | async-start | bytes 3145728 | tf_op jit(solution)/shard_map/reduce_scatter | solution.py:1338
  228.4 2.9 copy-start.9
  228.4 7.0 %slice-start = ((s8[6291456]{0:T(1024)(128)(4,1)}), s8[4194304]{0:T(1024)(128)(4,1)S(1)}, s32[]{:S(2)}) async-start(s8[6291456]{0:T(1024)(128)(4,1)} %bitcast.272), calls=%async_computation.3 | async-start | bytes 8388608
  231.3 7.6 %copy-start.7 = (f32[1024,512]{1,0:T(8,128)}, f32[1024,512]{1,0:T(8,128)S(1)}, u32[]{:S(2)}) copy-start(f32[1024,512]{1,0:T(8,128)S(1)} %get-tuple-element.118) | copy-start | bytes 6291460
  231.3 3.9 copy-start.18
  231.7 4.4 slice-start.1
  238.9 1.2 copy-start.32
  238.9 1.5 copy-start.34
  247.3 3.8 copy-start.21
  276.0 6.3 %copy-start.22 = (bf16[2048,1024]{1,0:T(8,128)(2,1)S(1)}, bf16[2048,1024]{1,0:T(8,128)(2,1)}, u32[]{:S(2)}) copy-start(bf16[2048,1024]{1,0:T(8,128)(2,1)} %copy.89) | copy-start | bytes 12582916
  276.0 7.5 %copy-start.29 = (bf16[2,1024,1024]{2,1,0:T(8,128)(2,1)S(1)}, bf16[2,1024,1024]{2,1,0:T(8,128)(2,1)}, u32[]{:S(2)}) copy-start(bf16[2,1024,1024]{2,1,0:T(8,128)(2,1)} %get-tuple-element.63) | copy-start | bytes 12582916
  289.7 4.8 copy-start.8
  289.7 4.8 copy-start.15
  289.7 5.3 %copy-start.28 = (bf16[1024,1024]{1,0:T(8,128)(2,1)S(1)}, bf16[1024,1024]{1,0:T(8,128)(2,1)}, u32[]{:S(2)}) copy-start(bf16[1024,1024]{1,0:T(8,128)(2,1)} %get-tuple-element.46) | copy-start | bytes 6291460
  295.0 2.0 copy-start.16
  297.0 11.3 %copy-start.11 = (f32[1024,1024]{1,0:T(8,128)}, f32[1024,1024]{1,0:T(8,128)S(1)}, u32[]{:S(2)}) copy-start(f32[1024,1024]{1,0:T(8,128)S(1)} %multiply_add_fusion.2) | copy-start | bytes 12582916
  297.0 1.3 copy-start.1
  308.4 4.2 copy-start.2
  308.4 2.9 copy-start.36
  311.3 1.3 copy-start.35
  312.6 2.0 copy-start.13
  313.9 4.2 copy-start.14
  314.6 4.3 copy-start.4
  314.6 5.5 %copy-start.6 = (f32[1024,1024]{1,0:T(8,128)S(1)}, f32[1024,1024]{1,0:T(8,128)}, u32[]{:S(2)}) copy-start(f32[1024,1024]{1,0:T(8,128)} %copy-done.5) | copy-start | bytes 12582916
  314.6 6.1 %copy-start.10 = (bf16[1024,1024]{1,0:T(8,128)(2,1)S(1)}, bf16[1024,1024]{1,0:T(8,128)(2,1)}, u32[]{:S(2)}) copy-start(bf16[1024,1024]{1,0:T(8,128)(2,1)} %get-tuple-element.54) | copy-start | bytes 6291460
  350.5 4.3 copy-start.25
  354.8 2.3 copy-start.24
  357.1 2.2 copy-start.26
  357.1 2.2 copy-start.41
  359.3 2.3 copy-start.23
  359.3 3.3 copy-start.17
  362.7 3.7 copy-start.12
  507.9 4.5 copy-start.30
Sparse Core Ops, SparseCore 0:
  228.5 20.3 all-reduce.10
  333.0 8.7 reduce-scatter.1

commit v3 on v2

--- a/solution.py
+++ b/solution.py
@@ -10,6 +10,7 @@
 F32, BF16 = jnp.float32, jnp.bfloat16
 MESH_ID = pl.DeviceIdType.MESH
 MIB = 1 << 20
+PARTS = 10
 PIECES = 13
 
 
@@ -92,7 +93,7 @@
 
 class Reduce:
     def __init__(self, part, ring1, ring2, line, out, sends, recvs):
-        self.part, self.ring1, self.ring2, self.line, self.out = part, ring1, ring2, line, out
+        self.all_parts, self.ring1, self.ring2, self.line, self.out = part, ring1, ring2, line, out
         self.sends, self.recvs = sends, recvs
         self.z, self.yx, self.c = place()
         self.x, self.y, self.d, self.zs = neighbours(self.z, self.yx)
@@ -100,22 +101,25 @@
     def copy(self, p, k, src, dst, z, yx):
         return remote(src, dst, self.sends.at[p, k], self.recvs.at[p, k], (z * 4 + yx, self.c))
 
+    def part(self, p):
+        return self.all_parts.at[p % PARTS]
+
     def diagonal(self, p):
-        part, z = self.part.at[p], self.z
+        part, z = self.part(p), self.z
         return [
             self.copy(p, 0, part.at[0:2, self.d], self.ring1.at[p, 0], z, self.x),
             self.copy(p, 1, part.at[2:4, self.d], self.ring1.at[p, 1], z, self.y),
         ]
 
     def side(self, p):
-        part, z = self.part.at[p], self.z
+        part, z = self.part(p), self.z
         return [
             self.copy(p, 2, part.at[:, self.x], self.ring2.at[p, 0], z, self.x),
             self.copy(p, 3, part.at[:, self.y], self.ring2.at[p, 1], z, self.y),
         ]
 
     def down(self, p):
-        part = self.part.at[p]
+        part = self.part(p)
         return [
             self.copy(p, 4 + k, part.at[peer, self.yx], self.line.at[p, k], peer, self.yx)
             for k, peer in enumerate(self.zs)
@@ -130,7 +134,7 @@
             copy.wait_recv()
 
     def add(self, p, a, yx, pieces):
-        total = self.part[p, a, yx].astype(F32)
+        total = self.part(p)[a, yx].astype(F32)
         for piece in pieces:
             total = total + piece.astype(F32)
         return total
@@ -141,14 +145,14 @@
     def stage2(self, p):
         self.arrive(self.diagonal(p))
         for a in range(2):
-            self.part[p, a, self.y] = self.add(p, a, self.y, [self.ring1[p, 0, a]]).astype(BF16)
-            self.part[p, a + 2, self.x] = self.add(p, a + 2, self.x, [self.ring1[p, 1, a]]).astype(BF16)
+            self.part(p)[a, self.y] = self.add(p, a, self.y, [self.ring1[p, 0, a]]).astype(BF16)
+            self.part(p)[a + 2, self.x] = self.add(p, a + 2, self.x, [self.ring1[p, 1, a]]).astype(BF16)
         self.start(self.side(p))
 
     def stage3(self, p):
         self.arrive(self.side(p))
         for a in range(4):
-            self.part[p, a, self.yx] = self.add(
+            self.part(p)[a, self.yx] = self.add(
                 p, a, self.yx, [self.ring2[p, 0, a], self.ring2[p, 1, a]]
             ).astype(BF16)
         self.start(self.down(p))
@@ -160,118 +164,6 @@
     def finish(self, p):
         for copy in self.diagonal(p) + self.side(p) + self.down(p):
             copy.wait_send()
-
-
-def reduce_kernel(
-    partial, vec, out, recv4, vout, part, ring1, ring2, line, vbuf, local_sem, sends, recvs, vsends, vrecvs, ex_send, ex_recv
-):
-    z, yx, c = place()
-    x, y, d, zs = neighbours(z, yx)
-    enter(z, yx, c)
-    sums = Reduce(part, ring1, ring2, line, out, sends, recvs)
-
-    def local(p):
-        return pltpu.make_async_copy(partial.at[p], part.at[p], local_sem.at[p])
-
-    def vec_copy(k, target):
-        return remote(vout, vbuf.at[k], vsends.at[k], vrecvs.at[k], target)
-
-    vcopies = [
-        [vec_copy(0, (z * 4 + yx, 1 - c))],
-        [vec_copy(1, (z * 4 + x, c))],
-        [vec_copy(2, (z * 4 + y, c))],
-        [vec_copy(3 + k, (peer * 4 + yx, c)) for k, peer in enumerate(zs)],
-    ]
-
-    vout[...] = vec[...]
-
-    def fetch(p, carry):
-        local(p).start()
-        return carry
-
-    lax.fori_loop(0, PIECES, fetch, 0)
-    for copy in vcopies[0]:
-        copy.start()
-
-    def turn(p, carry):
-        @pl.when(p < PIECES)
-        def _():
-            local(p).wait()
-            sums.stage1(p)
-
-        @pl.when((p >= 1) & (p < PIECES + 1))
-        def _():
-            sums.stage2(p - 1)
-
-        @pl.when((p >= 2) & (p < PIECES + 2))
-        def _():
-            sums.stage3(p - 2)
-
-        @pl.when(p >= 3)
-        def _():
-            sums.stage4(p - 3)
-
-        return carry
-
-    lax.fori_loop(0, 4, turn, 0)
-    at = 4
-    for k, copies in enumerate(vcopies):
-        for copy in copies:
-            copy.wait()
-        vout[...] = functools.reduce(
-            lambda a, b: a + b, [vbuf[j] for j in ([k] if k < 3 else [3, 4, 5])], vout[...]
-        )
-        if k + 1 < len(vcopies):
-            for copy in vcopies[k + 1]:
-                copy.start()
-        upto = at + 3 if k + 1 < len(vcopies) else PIECES + 3
-        lax.fori_loop(at, upto, turn, 0)
-        at = upto
-    half = recv4.shape[1]
-    others = pl.ds(pl.multiple_of((1 - c) * half, half), half)
-    swap = remote(out.at[0:4, others], recv4, ex_send, ex_recv, (z * 4 + yx, 1 - c))
-    swap.start()
-
-    def close(p, carry):
-        sums.finish(p)
-        return carry
-
-    lax.fori_loop(0, PIECES, close, 0)
-    swap.wait()
-
-
-def reduce_weights(partial, vec):
-    rows, width = partial.shape[3:]
-    any_ = pl.BlockSpec(memory_space=pl.ANY)
-    vmem = pl.BlockSpec(memory_space=pltpu.VMEM)
-    return pl.pallas_call(
-        reduce_kernel,
-        out_shape=(
-            jax.ShapeDtypeStruct((PIECES, rows, width), F32),
-            jax.ShapeDtypeStruct((4, rows // 2, width), F32),
-            jax.ShapeDtypeStruct(vec.shape, F32),
-        ),
-        in_specs=[any_, vmem],
-        out_specs=(vmem, vmem, vmem),
-        scratch_shapes=[
-            pltpu.VMEM((PIECES, 4, 4, rows, width), BF16),
-            pltpu.VMEM((PIECES, 2, 2, rows, width), BF16),
-            pltpu.VMEM((PIECES, 2, 4, rows, width), BF16),
-            pltpu.VMEM((PIECES, 3, rows, width), BF16),
-            pltpu.VMEM((6,) + vec.shape, F32),
-            pltpu.SemaphoreType.DMA((PIECES,)),
-            pltpu.SemaphoreType.DMA((PIECES, 7)),
-            pltpu.SemaphoreType.DMA((PIECES, 7)),
-            pltpu.SemaphoreType.DMA((6,)),
-            pltpu.SemaphoreType.DMA((6,)),
-            pltpu.SemaphoreType.DMA,
-            pltpu.SemaphoreType.DMA,
-        ],
-        compiler_params=pltpu.CompilerParams(
-            collective_id=1, has_side_effects=True, vmem_limit_bytes=48 * MIB
-        ),
-        name="reduce_weights",
-    )(partial, vec)
 
 
 def lanes(j):
@@ -348,7 +240,7 @@
 
 
 def wkv_backward(
-    g_ref, k_ref, v_ref, r_ref, sn_ref, sd_ref, keep_ref, rows_ref, gk_ref, gv_ref, gr_ref, sums_ref
+    g_ref, k_ref, v_ref, r_ref, sn_ref, sd_ref, keep_ref, rows_ref, gk_ref, gv_ref, gr_ref, begin, end, carry
 ):
     length, width = k_ref.shape
     tiles = width // 128
@@ -408,11 +300,13 @@
                 ref[both, lanes(j)] = jnp.concatenate([made[0][n], made[1][n]], axis=0).astype(BF16)
         return tuple(carry)
 
-    carry = lax.fori_loop(0, pairs, pair, (zero,) * (4 * tiles + 1))
-    for j in range(tiles):
-        rate_d = rows_ref[4:5, lanes(j)]
-        sums_ref[0:1, lanes(j)] = jnp.sum(carry[4 * j + 2], axis=0, keepdims=True)
-        sums_ref[1:2, lanes(j)] = -rate_d * jnp.sum(carry[4 * j + 3], axis=0, keepdims=True)
+    return lax.fori_loop(begin, end, pair, (zero,) * (4 * tiles + 1) if carry is None else carry)
+
+
+def wkv_sums(carry, rows_ref, decay_ref, bonus_ref):
+    for j in range(decay_ref.shape[1] // 128):
+        bonus_ref[0:1, lanes(j)] = jnp.sum(carry[4 * j + 2], axis=0, keepdims=True)
+        decay_ref[0:1, lanes(j)] = -rows_ref[4:5, lanes(j)] * jnp.sum(carry[4 * j + 3], axis=0, keepdims=True)
 
 
 NN, NT, TN = ((1,), (0,)), ((1,), (1,)), ((0,), (0,))
@@ -766,6 +660,435 @@
         ),
         name="forward",
     )(own4, other4, rest, vec, x_own, up_own, keep_own)
+
+
+R_VALUE, R_KEY, R_GATE2, R_EMIT, R_TIME = 0, 4, 8, 9, 10
+WEIGHT_ORDER = [FFN + 1, FFN, FFN + 3, FFN + 2, FFN + 5, FFN + 4, FFN + 7, FFN + 6, GATE2, EMIT, KEY, VALUE, GATE]
+S_GAIN1, S_BIAS1, S_GAIN2, S_BIAS2, S_DECAY, S_BONUS, S_MK1, S_MV1, S_MR1, S_MK2, S_MR2 = range(11)
+SLOTS = 12
+
+
+def whole(ref, at):
+    return jnp.concatenate([ref[0, at, :], ref[1, at, :]], axis=1)
+
+
+def halves(ref, at, value):
+    half = value.shape[1] // 2
+    ref[0, at, :] = value[:, :half].astype(ref.dtype)
+    ref[1, at, :] = value[:, half:].astype(ref.dtype)
+
+
+def fold(value):
+    return value[:8] + value[8:16]
+
+
+def back_through_norm(g, unit, inverse, gain):
+    q = g * gain
+    return inverse * (
+        q - jnp.mean(q, axis=-1, keepdims=True) - unit * jnp.mean(q * unit, axis=-1, keepdims=True)
+    )
+
+
+def lifted(now, following, last):
+    return jnp.where(last, following[0:1], pltpu.roll(now, now.shape[0] - 1, 0))
+
+
+def backward_kernel(
+    plan,
+    g, x_in, up_in, ins_in, kvr_in, sn_in, sd_in, mixed_in, resid_in, ins2_in, pre_in, act_in, gv_in, gr_in,
+    vec, rows, keep,
+    out, recv4, vout, gtok,
+    part, ring1, ring2, line, vbuf, b, w, f, resid, sum_other, n1_other, acc,
+    load_sem, w_sem, sends, recvs, vsends, vrecvs, ex_send, ex_recv, sum_send, sum_recv,
+):
+    z, yx, c = place()
+    nx, ny, nd, zs = neighbours(z, yx)
+    length, half = b.shape[1:]
+    width = 2 * half
+    span = length // 2
+    quarter = length // 4
+    partner = (z * 4 + yx, 1 - c)
+    loads = {}
+
+    def load(name, src, dst):
+        copy = pltpu.make_async_copy(src, dst, load_sem.at[len(loads)])
+        copy.start()
+        loads[name] = copy
+
+    def loaded(*names):
+        for name in names:
+            loads[name].wait()
+
+    def pair(n):
+        return b.at[n : n + 2]
+
+    def load_pair(name, src, n):
+        for h in range(2):
+            load((name, h), src.at[:, h * half : (h + 1) * half], b.at[n + h])
+
+    def loaded_pair(name):
+        loaded((name, 0), (name, 1))
+
+    def weight_copy(n):
+        return pltpu.make_async_copy(g.at[WEIGHT_ORDER[n]], w.at[n % 3], w_sem.at[n])
+
+    def weight(n):
+        weight_copy(n).wait()
+        return w.at[n % 3]
+
+    GVAL, ACT, PRE, IN_K2, IN_R2, GREC, GPRE = 0, 2, 4, 6, 8, 10, 11
+    load("gv0", gv_in.at[0], b.at[GVAL])
+    load("gv1", gv_in.at[1], b.at[GVAL + 1])
+    for j in range(2):
+        load(("act", j), act_in.at[j], b.at[ACT + j])
+    load_pair("in_k2", ins2_in.at[0], IN_K2)
+    for j in range(2):
+        load(("pre", j), pre_in.at[j], b.at[PRE + j])
+    for n in range(3):
+        weight_copy(n).start()
+    load_pair("in_r2", ins2_in.at[1], IN_R2)
+    load("gr", gr_in, b.at[GREC])
+    load("resid", resid_in, resid)
+    enter(z, yx, c)
+
+    sums = Reduce(part, ring1, ring2, line, out, sends, recvs)
+    stages = (None, sums.stage1, sums.stage2, sums.stage3, sums.stage4)
+    calls = iter(plan)
+
+    def pump():
+        for stage, p in next(calls):
+            stages[stage](p)
+
+    def gradient(p, lhs, rhs):
+        for a in range(4):
+            block = lhs[a // 2, :, (a % 2) * (half // 2) : (a % 2 + 1) * (half // 2)]
+            part[p % PARTS, a] = dot(block, rhs[...], TN).astype(BF16).reshape(part.shape[2:])
+
+    def thirds(ref, h):
+        return ref[2 * h : 2 * h + 2].reshape(half, half)
+
+    loaded("gv0", "gv1")
+    for j in range(4):
+        loaded(("act", j))
+        gradient(R_VALUE + j, pair(GVAL), b.at[ACT + j % 2])
+        if j < 2:
+            load(("act", j + 2), act_in.at[j + 2], b.at[ACT + j])
+        pump()
+    loaded_pair("in_k2")
+    for j in range(4):
+        loaded(("pre", j))
+        value_w = weight(2 * j)
+
+        def through(at):
+            g_hidden = sum(dot(b[GVAL + h, at, :], thirds(value_w, h), NN) for h in range(2))
+            b[GPRE, at, :] = (2.0 * b[PRE + j % 2, at, :].astype(F32) * g_hidden).astype(BF16)
+
+        over_rows(length, 256, through)
+        if j < 2:
+            load(("pre", j + 2), pre_in.at[j + 2], b.at[PRE + j])
+        weight_copy(2 * j + 3).start()
+        gradient(R_KEY + j, pair(IN_K2), b.at[GPRE])
+        pump()
+        key_w = weight(2 * j + 1)
+
+        def collect(at):
+            for h in range(2):
+                piece = dot(b[GPRE, at, :], thirds(key_w, h), NT)
+                f[h, at, :] = piece if j == 0 else f[h, at, :] + piece
+
+        over_rows(length, 256, collect)
+        weight_copy(2 * j + 4).start()
+    loaded_pair("in_r2")
+    loaded("gr")
+    gradient(R_GATE2, pair(IN_R2), b.at[GREC])
+    pump()
+    gate_w = weight(8)
+
+    def gate_back(at):
+        for h in range(2):
+            f[2 + h, at, :] = dot(b[GREC, at, :], thirds(gate_w, h), NT)
+
+    over_rows(length, 256, gate_back)
+    weight_copy(11).start()
+    loaded("resid")
+
+    SUM_OWN, UP, BRANCH, MIXED, G3, X, IN_K, IN_V, IN_R, SEND = 0, 2, 4, 6, 7, 4, 10, 0, 2, 6
+    load_pair("up", up_in, UP)
+    load("mixed", mixed_in, b.at[MIXED])
+    acc[...] = jnp.zeros_like(acc)
+    last = lax.broadcasted_iota(jnp.int32, (16, width), 0) == 15
+
+    def row(n):
+        return vec[n : n + 1, :]
+
+    def kept(at, n):
+        return wide(keep[at, :], width) if n is None else wide(keep[n, :], width)
+
+    gain2, bias2, mk2, mr2 = (GAIN2, BIAS2, MK2, MR2)
+    sum_copies = []
+    for q in range(4):
+
+        def tile(i, carry):
+            base = q * quarter + i * 16
+            at = pl.ds(pl.multiple_of(base, 16), 16)
+            after = pl.ds(pl.multiple_of(jnp.minimum(base + 16, length - 8), 8), 8)
+            inside = jnp.where(base + 16 < length, 1.0, 0.0)
+            keep_at, keep_after = wide(keep[at, :], width), wide(keep[after, :], width) * inside
+            unit, _ = norm(whole(resid, at))
+            normed = unit * row(gain2) + row(bias2)
+            total = jnp.zeros_like(unit)
+            for n, share in enumerate((mk2, mr2)):
+                back = whole(f.at[2 * n : 2 * n + 2], at)
+                ahead = lifted(back * keep_at, whole(f.at[2 * n : 2 * n + 2], after) * keep_after, last)
+                total = total + ahead + (back - ahead) * row(share)
+                acc[S_MK2 + n] = acc[S_MK2 + n] + fold(normed * (back - ahead))
+            acc[S_GAIN2] = acc[S_GAIN2] + fold(total * unit)
+            acc[S_BIAS2] = acc[S_BIAS2] + fold(total)
+            halves(b.at[SUM_OWN : SUM_OWN + 2], at, total)
+            return carry
+
+        lax.fori_loop(0, quarter // 16, tile, 0)
+        at = pl.ds(q * quarter, quarter)
+        sum_copies.append(
+            remote(b.at[SUM_OWN : SUM_OWN + 2, at], sum_other.at[:, at], sum_send.at[q], sum_recv.at[q], partner)
+        )
+        sum_copies[-1].start()
+        pump()
+    for n in range(3):
+        load(("kvr", n), kvr_in.at[n], f.at[n])
+    load("sn", sn_in, f.at[3])
+    load("sd", sd_in, f.at[4])
+    load_pair("in_k", ins_in.at[0], IN_K)
+
+    loaded_pair("up")
+    for q in range(4):
+        sum_copies[q].wait_recv()
+
+        def tile(i, carry):
+            at = pl.ds(pl.multiple_of(q * quarter + i * 16, 16), 16)
+            unit, inverse = norm(whole(resid, at))
+            total = whole(b.at[SUM_OWN : SUM_OWN + 2], at).astype(F32) + whole(sum_other, at).astype(F32)
+            back = whole(pair(UP), at).astype(F32) + back_through_norm(total, unit, inverse, row(gain2))
+            halves(pair(BRANCH), at, back)
+
+            @pl.when(c == q // 2)
+            def _():
+                gtok[pl.ds(pl.multiple_of((q % 2) * quarter + i * 16, 16), 16), :] = back
+
+            return carry
+
+        lax.fori_loop(0, quarter // 16, tile, 0)
+        pump()
+    for copy in sum_copies:
+        copy.wait_send()
+    load_pair("in_v", ins_in.at[1], IN_V)
+    load_pair("in_r", ins_in.at[2], IN_R)
+
+    loaded("mixed")
+    for h in range(2):
+        for a in range(2):
+            block = dot(b[MIXED, :, a * (half // 2) : (a + 1) * (half // 2)], b[BRANCH + h], TN).astype(BF16)
+            rows_h = part.shape[3] // 2
+            part[R_EMIT, 2 * a : 2 * a + 2, :, h * rows_h : (h + 1) * rows_h, :] = block.reshape(2, 4, rows_h, half)
+    pump()
+    emit_w = weight(9)
+
+    def emit_back(at):
+        resid[0, at, :] = sum(dot(b[BRANCH + h, at, :], emit_half(emit_w, h), NT) for h in range(2))
+
+    over_rows(length, 256, emit_back)
+    weight_copy(12).start()
+    load_pair("x", x_in, X)
+
+    loaded(("kvr", 0), ("kvr", 1), ("kvr", 2), "sn", "sd")
+    carry = None
+    for q in range(4):
+        carry = wkv_backward(
+            resid.at[0], f.at[0], f.at[1], f.at[2], f.at[3], f.at[4], keep, rows, b.at[G3], b.at[G3 + 1], b.at[G3 + 2],
+            q * (length // 64), (q + 1) * (length // 64), carry,
+        )
+        pump()
+    vout[...] = jnp.zeros_like(vout)
+    columns = strip(c, half)
+    wkv_sums(carry, rows, acc.at[S_DECAY, :, 0:half], acc.at[S_BONUS, :, 0:half])
+    vout[S_DECAY : S_DECAY + 1, columns] = acc[S_DECAY, 0:1, 0:half]
+    vout[S_BONUS : S_BONUS + 1, columns] = acc[S_BONUS, 0:1, 0:half]
+
+    for n, (name, slot) in enumerate((("in_k", IN_K), ("in_v", IN_V), ("in_r", IN_R))):
+        loaded_pair(name)
+        sums.finish(R_TIME + n - PARTS)
+        gradient(R_TIME + n, pair(slot), b.at[G3 + n])
+        pump()
+    loaded_pair("x")
+    time_w = [weight(10 + n) for n in range(3)]
+    for n in range(3):
+        for h in range(2):
+            f[n, pl.ds(h * span + quarter, 8), :] = jnp.zeros((8, half), F32)
+    n1_copies = []
+    for q in (3, 2, 1, 0):
+        for n in range(3):
+            for h in range(2):
+                if q < 3:
+                    f[n, pl.ds(h * span + quarter, 8), :] = f[n, pl.ds(h * span, 8), :]
+                f[n, pl.ds(h * span, quarter), :] = dot(
+                    b[G3 + n, pl.ds(q * quarter, quarter), :], thirds(time_w[n], h), NT
+                )
+
+        def tile(i, carry):
+            base = q * quarter + i * 16
+            at = pl.ds(pl.multiple_of(base, 16), 16)
+            after = pl.ds(pl.multiple_of(jnp.minimum(base + 16, length - 8), 8), 8)
+            keep_at, keep_after = wide(keep[at, :], width), wide(keep[after, :], width)
+
+            def take(n, start, size):
+                return jnp.concatenate(
+                    [f[n, pl.ds(pl.multiple_of(h * span + start, 8), size), :] for h in range(2)], axis=1
+                )
+
+            unit, _ = norm(whole(pair(X), at).astype(F32))
+            normed = unit * row(GAIN1) + row(BIAS1)
+            total = jnp.zeros_like(unit)
+            for n, share in enumerate((MK1, MV1, MR1)):
+                back = take(n, i * 16, 16)
+                ahead = lifted(back * keep_at, take(n, i * 16 + 16, 8) * keep_after, last)
+                total = total + ahead + (back - ahead) * row(share)
+                acc[S_MK1 + n] = acc[S_MK1 + n] + fold(normed * (back - ahead))
+            acc[S_GAIN1] = acc[S_GAIN1] + fold(total * unit)
+            acc[S_BIAS1] = acc[S_BIAS1] + fold(total)
+            rows_q = [pl.ds(pl.multiple_of(h * span + (q % 2) * quarter + i * 16, 16), 16) for h in range(2)]
+
+            @pl.when(c == q // 2)
+            def _():
+                for h in range(2):
+                    f[3, rows_q[h], :] = total[:, h * half : (h + 1) * half]
+
+            @pl.when(c != q // 2)
+            def _():
+                for h in range(2):
+                    b[SEND, rows_q[h], :] = total[:, h * half : (h + 1) * half].astype(BF16)
+
+            return carry
+
+        lax.fori_loop(0, quarter // 16, tile, 0)
+        pump()
+    swap_n1 = remote(b.at[SEND], n1_other, sum_send.at[4], sum_recv.at[4], partner)
+    swap_n1.start()
+
+    for n in (S_GAIN1, S_BIAS1, S_GAIN2, S_BIAS2, S_MK1, S_MV1, S_MR1, S_MK2, S_MR2):
+        vout[n : n + 1, :] = jnp.sum(acc[n], axis=0, keepdims=True)
+
+    def vec_copy(k, target):
+        return remote(vout, vbuf.at[k], vsends.at[k], vrecvs.at[k], target)
+
+    vec_stages = [
+        [vec_copy(0, partner)],
+        [vec_copy(1, (z * 4 + nx, c))],
+        [vec_copy(2, (z * 4 + ny, c))],
+        [vec_copy(3 + k, (peer * 4 + yx, c)) for k, peer in enumerate(zs)],
+    ]
+
+    def vec_start(k):
+        for copy in vec_stages[k]:
+            copy.start()
+
+    def vec_add(k):
+        for copy in vec_stages[k]:
+            copy.wait()
+        for j in [k] if k < 3 else [3, 4, 5]:
+            vout[...] = vout[...] + vbuf[j]
+
+    vec_start(0)
+    pump()
+    swap_n1.wait()
+
+    def tokens(i, carry):
+        at = strip(i, 16)
+        spans = [pl.ds(pl.multiple_of(h * span + i * 16, 16), 16) for h in range(2)]
+        unit, inverse = norm(whole(pair(X), pl.ds(pl.multiple_of(c * span + i * 16, 16), 16)).astype(F32))
+        total = jnp.concatenate([f[3, s, :] + n1_other[s, :].astype(F32) for s in spans], axis=1)
+        gtok[at, :] = gtok[at, :] + back_through_norm(total, unit, inverse, row(GAIN1))
+        return carry
+
+    lax.fori_loop(0, span // 16, tokens, 0)
+    vec_add(0)
+    vec_start(1)
+    pump()
+    vec_add(1)
+    vec_start(2)
+    pump()
+    vec_add(2)
+    vec_start(3)
+    pump()
+    vec_add(3)
+    for actions in calls:
+        for stage, p in actions:
+            stages[stage](p)
+    rows4 = recv4.shape[1]
+    others = strip(1 - c, rows4)
+    swaps = [
+        remote(out.at[R_TIME : R_TIME + 3, others], recv4.at[0:3], ex_send.at[0], ex_recv.at[0], partner),
+        remote(out.at[R_GATE2, others], recv4.at[3], ex_send.at[1], ex_recv.at[1], partner),
+    ]
+    for copy in swaps:
+        copy.start()
+    for p in range(PIECES - PARTS, PIECES):
+        sums.finish(p)
+    for copy in swaps:
+        copy.wait()
+
+
+def make_plan():
+    plan = [
+        [(1, 0)], [(1, 1)], [(1, 2)], [(1, 3), (2, 0)],
+        [(1, 4)], [(1, 5), (2, 1)], [(1, 6)], [(1, 7), (2, 2)],
+        [(1, 8)],
+        [(2, 3)], [(3, 0)], [(2, 4)], [(3, 1)],
+        [(2, 5)], [(3, 2)], [(4, 0)], [(2, 6), (3, 3)],
+        [(1, 9), (4, 1)],
+        [(2, 7), (3, 4)], [(4, 2)], [(2, 8), (3, 5)], [(4, 3)],
+        [(1, 10), (2, 9), (4, 4)], [(1, 11), (3, 6)], [(1, 12), (3, 7)],
+        [(2, 10)], [(3, 8)], [(2, 11)], [(3, 9), (4, 5)],
+        [(2, 12), (4, 6)], [(3, 10)], [(3, 11)], [(3, 12)],
+        [(4, p) for p in range(7, 13)],
+    ]
+    return plan
+
+
+def backward_call(g, x, up, ins, kvr, sn, sd, mixed, resid, ins2, pre, act, g_value, g_recept, vec, rows, keep):
+    block = g.shape[3:]
+    length, half = sn.shape
+    any_, vmem = pl.BlockSpec(memory_space=pl.ANY), pl.BlockSpec(memory_space=pltpu.VMEM)
+    dma = pltpu.SemaphoreType.DMA
+
+    def shape(*dims):
+        return jax.ShapeDtypeStruct(dims, F32)
+
+    return pl.pallas_call(
+        functools.partial(backward_kernel, make_plan()),
+        out_shape=(
+            shape(PIECES, *block), shape(4, block[0] // 2, block[1]), shape(16, 2 * half), shape(length // 2, 2 * half),
+        ),
+        in_specs=[any_] * 14 + [vmem] * 3,
+        out_specs=(vmem,) * 4,
+        scratch_shapes=[
+            pltpu.VMEM((PARTS, 4, 4) + block, BF16),
+            pltpu.VMEM((PIECES, 2, 2) + block, BF16),
+            pltpu.VMEM((PIECES, 2, 4) + block, BF16),
+            pltpu.VMEM((PIECES, 3) + block, BF16),
+            pltpu.VMEM((6, 16, 2 * half), F32),
+            pltpu.VMEM((SLOTS, length, half), BF16),
+            pltpu.VMEM((3, 4, 4) + block, BF16),
+            pltpu.VMEM((5, length, half), F32),
+            pltpu.VMEM((2, length, half), F32),
+            pltpu.VMEM((2, length, half), BF16),
+            pltpu.VMEM((length, half), BF16),
+            pltpu.VMEM((11, 8, 2 * half), F32),
+            dma((40,)), dma((PIECES,)), dma((PIECES, 7)), dma((PIECES, 7)), dma((6,)), dma((6,)), dma((2,)), dma((2,)),
+            dma((5,)), dma((5,)),
+        ],
+        compiler_params=pltpu.CompilerParams(collective_id=1, has_side_effects=True, vmem_limit_bytes=63 * MIB),
+        name="backward",
+    )(g, x, up, ins, kvr, sn, sd, mixed, resid, ins2, pre, act, g_value, g_recept, vec, rows, keep)
 
 
 def shifted(value, axis, steps):
@@ -1204,18 +1527,6 @@
     )
 
 
-def local_call(body, outs, name, *args):
-    vmem = pl.BlockSpec(memory_space=pltpu.VMEM)
-    return pl.pallas_call(
-        body,
-        out_shape=outs,
-        in_specs=[vmem] * len(args),
-        out_specs=tuple([vmem] * len(outs)),
-        compiler_params=pltpu.CompilerParams(vmem_limit_bytes=48 * MIB),
-        name=name,
-    )(*args)
-
-
 def split_columns(w, parts):
     rows, width = w.shape
     return w.reshape(rows, parts, 2, width // (2 * parts)).transpose(2, 0, 1, 3).reshape(2, rows, width // 2)
@@ -1226,31 +1537,6 @@
     a = jnp.where(c == 0, own, other).reshape(own.shape[:-1] + (parts, half // parts))
     b = jnp.where(c == 0, other, own).reshape(own.shape[:-1] + (parts, half // parts))
     return jnp.stack([a, b], axis=-2).reshape(own.shape[:-1] + (2 * half,))
-
-
-def pair_sum(a):
-    return lax.psum(a.astype(BF16), "tensor").astype(F32)
-
-
-def layer_norm(values, gain, bias):
-    normed, inverse = norm(values)
-    return normed * gain + bias, normed, inverse
-
-
-def norm_back(g, normed, inverse, gain):
-    q = g * gain
-    return inverse * (
-        q - jnp.mean(q, axis=-1, keepdims=True) - normed * jnp.mean(q * normed, axis=-1, keepdims=True)
-    )
-
-
-def shift_down(v, keep):
-    return jnp.concatenate([jnp.zeros_like(v[:1]), v[:-1]]) * keep[:, None]
-
-
-def shift_up(v, keep):
-    v = v * keep[:, None]
-    return jnp.concatenate([v[1:], jnp.zeros_like(v[:1])])
 
 
 def pack(tokens, starts, upstream, gain1, bias1, gain2, bias2, fading, reward, mk1, mv1, mr1, wk, wv, wr, wo, mk2, mr2, wg, fk, fv):
@@ -1289,90 +1575,17 @@
         g, layer_out, x, up, ins, kvr, sn, sd, mixed, resid, ins2, pre, act, g_value, g_recept2, vec, rows, keep,
     ) = forward_call(*pack(*args))
 
-    gain1, bias1, gain2, bias2, fading, reward, mk1, mv1, mr1, mk2, mr2 = (vec[n] for n in range(VECTORS))
-    keep_rows, keep = keep, keep[:, 0]
-    g = g.reshape((PIECES, width, half))
-    wk, wv, wr, wg = g[KEY], g[VALUE], g[GATE], g[GATE2]
-    wo = g[EMIT].reshape(count, 2, own_rows, half).transpose(0, 2, 1, 3).reshape(half, width)
-    fk = jnp.concatenate([g[FFN + 2 * n] for n in range(4)], axis=1)
-    fv = jnp.concatenate([g[FFN + 1 + 2 * n] for n in range(4)], axis=1)
-    x, up = x.astype(F32), up.astype(F32)
-    n1, u1, i1 = layer_norm(x, gain1, bias1)
-    d1 = n1 - shift_down(n1, keep)
-    in_k, in_v, in_r = (ins[n] for n in range(3))
-    k, v, r = (kvr[n] for n in range(3))
-    resid = jnp.concatenate([resid[0], resid[1]], axis=1)
-    n2, u2, i2 = layer_norm(resid, gain2, bias2)
-    d2 = n2 - shift_down(n2, keep)
-    in_k2, in_r2 = ins2[0], ins2[1]
-    pre = jnp.concatenate([pre[n] for n in range(4)], axis=1).astype(F32)
-    act = jnp.concatenate([act[n] for n in range(4)], axis=1)
-    g_value = jnp.concatenate([g_value[0], g_value[1]], axis=1)
-    low = jax.ShapeDtypeStruct(k.shape, BF16)
-    grad_fv = dot(g_value, act, TN)
-    g_pre = (2.0 * pre * dot(g_value, fv, NN)).astype(BF16)
-    grad_fk = dot(in_k2, g_pre, TN)
-    grad_wg = dot(in_r2, g_recept2, TN)
-    gk2 = dot(g_pre, fk, NT)
-    gr2 = dot(g_recept2, wg, NT)
-    grad_mk2, grad_mr2 = jnp.sum(gk2 * d2, 0), jnp.sum(gr2 * d2, 0)
-    gn2 = gk2 * mk2 + gr2 * mr2 + shift_up(gk2 * (1 - mk2) + gr2 * (1 - mr2), keep)
-    grad_gain2, grad_bias2 = jnp.sum(gn2 * u2, 0), jnp.sum(gn2, 0)
-    g_resid = up + norm_back(pair_sum(gn2), u2, i2, gain2)
-    g_branch = g_resid.astype(BF16)
-    grad_wo = dot(mixed, g_branch, TN)
-    g_mixed = dot(g_branch, wo, NT)
-    gk1, gv1, gr1, wsums = local_call(
-        wkv_backward, (low, low, low, jax.ShapeDtypeStruct((8, half), F32)), "wkv_backward",
-        g_mixed, k, v, r, sn, sd, keep_rows, rows,
-    )
-    grad_wk, grad_wv, grad_wr = dot(in_k, gk1, TN), dot(in_v, gv1, TN), dot(in_r, gr1, TN)
-    toward, behind, grad_mix = 0.0, 0.0, []
-    for grad, w, m in ((gk1, wk, mk1), (gv1, wv, mv1), (gr1, wr, mr1)):
-        back = dot(grad, w, NT)
-        toward = toward + back * m
-        behind = behind + back * (1 - m)
-        grad_mix.append(jnp.sum(back * d1, 0))
-    gn1 = toward + shift_up(behind, keep)
-    grad_gain1, grad_bias1 = jnp.sum(gn1 * u1, 0), jnp.sum(gn1, 0)
-    gn1 = lax.psum_scatter(gn1.astype(BF16), "tensor", scatter_dimension=0, tiled=True).astype(F32)
-    span = tokens.shape[1]
-
-    def mine(v):
-        return lax.dynamic_slice_in_dim(v, c * span, span, 0)
-
-    grad_tokens = mine(g_resid) + norm_back(gn1, mine(u1), mine(i1), gain1)
-
-    def pieces(m):
-        return m.reshape(1, 4, 4, 2 * own_rows, half)
-
-    grad_wo = grad_wo.reshape(count, own_rows, 2, half).transpose(0, 2, 1, 3)
-    grad_fk, grad_fv = (
-        m.reshape(width, 4, hidden // 4).transpose(1, 0, 2).reshape((4, 4, 4) + (2 * own_rows, half))
-        for m in (grad_fk, grad_fv)
-    )
-    partial = jnp.concatenate(
-        [pieces(grad_wk), pieces(grad_wv), pieces(grad_wr), pieces(grad_wg), pieces(grad_wo), grad_fk, grad_fv]
-    ).astype(BF16)
-
-    def all_channels(v):
-        z = jnp.zeros_like(v)
-        return jnp.where(c == 0, jnp.concatenate([v, z]), jnp.concatenate([z, v]))
-
-    vsums = jnp.stack([
-        grad_gain1, grad_bias1, grad_gain2, grad_bias2, all_channels(wsums[1]), all_channels(wsums[0]),
-        *grad_mix, grad_mk2, grad_mr2,
-    ])
-    vsums = jnp.pad(vsums, ((0, 16 - VECTORS), (0, 0)))
-    total, recv4, vtotal = reduce_weights(partial, vsums)
+    total, recv4, vtotal, grad_tokens = backward_call(
+        g, x, up, ins, kvr, sn, sd, mixed, resid, ins2, pre, act, g_value, g_recept2, vec, rows, keep
+    )
     own_scan = lax.dynamic_slice_in_dim(vtotal, c * half + i * own_rows, own_rows, 1)
     vtotal = lax.dynamic_slice_in_dim(vtotal, (2 * i + c) * own_rows, own_rows, 1)
-    own = lax.dynamic_slice_in_dim(total[:4], c * own_rows, own_rows, 1)
-    out_k, out_v, out_r = (join_columns(own[n], recv4[n], c, count) for n in range(3))
-    out_g = join_columns(own[3], recv4[3], c, 1)
-    out_o = total[4].reshape(2, own_rows, half).transpose(1, 0, 2).reshape(own_rows, width)
-    out_fk = total[5:9].transpose(1, 0, 2).reshape(2 * own_rows, hidden)
-    out_fv = total[9:13].transpose(0, 2, 1).reshape(hidden, 2 * own_rows)
+    own = lax.dynamic_slice_in_dim(total[R_GATE2:], c * own_rows, own_rows, 1)
+    out_k, out_v, out_r = (join_columns(own[2 + n], recv4[n], c, count) for n in range(3))
+    out_g = join_columns(own[0], recv4[3], c, 1)
+    out_o = total[R_EMIT].reshape(2, own_rows, half).transpose(1, 0, 2).reshape(own_rows, width)
+    out_fk = total[R_KEY : R_KEY + 4].transpose(1, 0, 2).reshape(2 * own_rows, hidden)
+    out_fv = total[R_VALUE : R_VALUE + 4].transpose(0, 2, 1).reshape(hidden, 2 * own_rows)
     return (
         layer_out[None], grad_tokens[None], *(vtotal[n] for n in range(4)), own_scan[4], own_scan[5],
         *(vtotal[n] for n in range(6, 9)), out_k, out_v, out_r, out_o, vtotal[9], vtotal[10], out_g, out_fk, out_fv,

time: 525 us -> 342 us (0.65)
  local copies, waits for them, and re-layouts: 96 us -> 20.3 us
  matrix products: 55.1 us -> 0 us
  other arithmetic: 46.6 us -> 2.79 us
  between operations: 15.2 us -> 1.16 us
  Pallas kernels: 308 us -> 317 us
    dot_general x14 -> x0, matrix products: 55.1 us -> none  [dot(): return lax.dot_general(a, b, (dims, ((), ())), preferred_element_type=F32)]
    dot_general x7 -> x0, local copies, waits for them, and re-layouts: 28.2 us -> none  [dot(): return lax.dot_general(a, b, (dims, ((), ())), preferred_element_type=F32)]
    reduce_sum x7 -> x0, other arithmetic: 23.7 us -> none  [the longest x1 12.1 us: shards(): grad_gain1, grad_bias1 = (jnp.sum(gn1 * u1, 0), jnp.sum(gn1, 0))]
    unnamed x94 -> x42, local copies, waits for them, and re-layouts: 19.5 us -> 3.18 us
    pallas_call x2 -> x1, Pallas kernels: 136 us -> 146 us  [backward_call(): pl.pallas_call(functools.partial(backward_kernel, make_plan()), out_shape...]
    slice x5 -> x2, local copies, waits for them, and re-layouts: 10.2 us -> 1.14 us  [the longest x1 1.13 us: shards(): own = lax.dynamic_slice_in_dim(total[R_GATE2:], c * own_rows, own_rows, 1)]
    reshape x6 -> x3, local copies, waits for them, and re-layouts: 9.96 us -> 2.34 us  [the longest x1 0.84 us: shards(): total[R_KEY:R_KEY + 4].transpose(1, 0, 2).reshape(2 * own_rows, hidden)]
    squeeze x4 -> x0, local copies, waits for them, and re-layouts: 6.99 us -> none  [the longest x1 6.32 us: shards(): k, v, r = (kvr[n] for n in range(3))]
  transfers between devices with their start and end apart: 2 -> 0, of which waited for: 0 -> 0; matrix products, arithmetic and copies ran while one was open for 19% -> 0% of each run, Pallas kernels for 24% -> 0%
where the time goes in v3:
time: 342 us; the launch traced here: 341 us
  Pallas kernels  317 us (93%)
  local copies, waits for them, and re-layouts  20.3 us (6%)
    pallas_call x1, Pallas kernels, forward_call(): pl.pallas_call(forward_kernel, out_shape=tuple((o[0] for o in outs)), in_...  171 us
    pallas_call x1, Pallas kernels, backward_call(): pl.pallas_call(functools.partial(backward_kernel, make_plan()), out_shape...  146 us

profile of v3, /device:TPU:0, one launch (start us, length us, event | category | flops | bytes accessed | tf_op | source)
XLA Modules:
  0.0 341.4 jit_solution(5602521345615304862)
XLA Ops:
  0.7 0.9 reshape.302
  1.6 1.1 reshape.301
  2.7 0.0 copy-start.4
  2.7 0.2 stack_reshape.10
  3.0 1.1 reshape.300
  4.1 0.2 stack_reshape.9
  4.3 0.2 reshape.299
  4.6 0.2 stack_reshape.8
  4.9 0.0 copy-start.9
  4.9 0.0 copy-start.10
  4.9 0.0 copy-start.13
  4.9 0.0 copy-start.14
  5.0 0.7 dynamic-slice_bitcast_fusion
  5.8 0.1 pad_maximum_fusion.1
  5.9 0.9 pad_maximum_fusion.rest
  6.7 0.1 pad.13.clone
  6.8 0.1 pad.12.clone
  6.9 0.1 maximum_maximum_fusion
  7.0 0.1 tile.21
  7.2 0.1 stack.83
  7.2 0.1 tile.9
  7.3 0.6 pad_maximum_fusion.7.vec
  8.0 0.8 broadcast_in_dim.41.keep_own
  8.8 171.0 %forward.1 = (bf16[13,4,4,64,512]{4,3,2,1,0:T(8,128)(2,1)}, bf16[512,1024]{1,0:T(8,128)(2,1)}, bf16[1024,1024]{1,0:T(8,128)(2,1)}, bf16[1024,1024]{1,0:T(8,128)(...) custom-call(bf16[4,32,512]{2,1,0:T(8,128)(2,1)} %get-tuple-element.7, ...), custom_call_target="tpu_custom_call" | custom-call | tf_op jit(solution)/shard_map/forward/pallas_call | solution.py:628
  179.8 146.2 %backward.1 = (f32[13,64,512]{2,1,0:T(8,128)}, f32[4,32,512]{2,1,0:T(8,128)}, f32[16,1024]{1,0:T(8,128)}, f32[512,1024]{1,0:T(8,128)}) custom-call(bf16[13,4,4,64,512]{4,3,2,1,0:T(8,128)(2,1)} %get-tuple-element.43.g, bf16[1024,1024]{1,0:T(8,128)(2,1)} %get-tuple-element.44.x_in, bf16[1024,1024]{1,0:T(8,128)(2,1)} %get-tuple-element.45.up_in, ...), custom_call_target="tpu_custom_call" | custom-call | tf_op jit(solution)/shard_map/backward/pallas_call | solution.py:1066
  326.0 1.6 dynamic-slice_bitcast_fusion.2
  327.6 1.1 slice.78
  328.8 1.0 select_bitcast_fusion.1
  329.8 0.1 select_n.180
  329.9 0.1 select_n.178
  330.1 0.4 copy.59
  330.5 1.3 reshape.308
  331.8 0.1 select_n.184
  331.9 0.1 select_n.182
  332.1 0.4 copy.60
  332.5 1.3 reshape.309
  333.8 0.1 select_n.188
  334.0 0.1 select_n.186
  334.1 0.4 copy.61
  334.5 1.3 reshape.310
  335.9 0.7 copy.69
  336.6 0.1 copy.63
  336.7 0.7 copy.72
  337.4 0.1 slice_bitcast_fusion
  337.5 0.8 copy.70
  338.3 0.8 copy.71
  339.1 1.0 copy.81
  340.1 1.3 copy.82
  (52 shorter events, 0.5 us)
Async XLA Ops:
  0.7 3.7 %copy-start.5 = (bf16[32,1024]{1,0:T(8,128)(2,1)S(1)}, bf16[32,1024]{1,0:T(8,128)(2,1)}, u32[]{:S(2)}) copy-start(bf16[32,1024]{1,0:T(8,128)(2,1)} %param.33) | copy-start | bytes 196612
  2.7 3.1 copy-start.3
  2.7 3.1 copy-start.4
  4.5 1.3 copy-start.6
  4.8 2.0 copy-start.8
  4.9 2.0 copy-start.9
  4.9 2.2 copy-start.10
  4.9 2.2 copy-start.11
  4.9 2.2 copy-start.12
  4.9 2.2 copy-start.13
  4.9 2.2 copy-start.14
  4.9 2.2 copy-start.15
  4.9 2.2 copy-start.16
  5.0 2.2 copy-start.17
  5.0 2.2 copy-start.18
  5.0 3.0 copy-start.7
  332.5 3.4 copy-start.1
  337.4 1.8 copy-start.2
  337.5 2.7 copy-start
